TPU v7x, 256 devices: a whole 4x4x8 slice. The times are simulated.
256 devices in a mesh: ctx: 32 (over y_hi, z, core), exp: 8 (over x, y_lo).
Axes of the slice: x: 4, y: 4 (y_hi: 2, y_lo: 2; y = y_hi * 2 + y_lo), z: 8, core: 2. Of those that a mesh axis runs over, the one named last changes fastest.
Arguments:
- queries: bfloat16 [4096, 6144], P('ctx', 'exp'), may hold values from -12 to 12
- keys_values: bfloat16 [4096, 8, 256], P('ctx', 'exp'), may hold values from -12 to 12
- doc_ids: int32 [4096], P('ctx'), may hold values from 0 to 7, never falling along the last dimension, each value on 1 to 3072 neighbouring positions
- gate_up: bfloat16 [8, 1280, 16384], P('exp', None, 'ctx'), may hold values from -6 to 6
- down_weight: bfloat16 [8, 16384, 6144], P('exp', 'ctx'), may hold values from -0.046875 to 0.046875
- routes: int32 [4096, 2], P(('ctx', 'exp')), may hold values from 0 to 7, all different within a row; in each aligned block of 16 rows (0 to 15, 16 to 31, ...) at most 5 rows name the same one
- route_weights: float32 [4096, 2], P(('ctx', 'exp')), may hold values from 0.1 to 1
Outputs:
- context: bfloat16 [4096, 6144], P('ctx', 'exp')
- moe_out: bfloat16 [4096, 6144], P(('ctx', 'exp'))
Inputs may be any that keep to these rules, and one draw needn't show every extreme that they name: doc_ids never falls along the sequence; each document has 1 to 3072 tokens and one has exactly 3072. `routes`: the 2 experts of a token differ; among the 16 tokens of one device (aligned blocks) no expert is named more than 5 times, a bound that some block reaches.
All inputs are finite; a program needn't handle non-finite values.
Results may differ from a plain program's by a relative error of at most 0.025.
Values may be sent and summed in bfloat16 or wider, within the bound.
No kernel may reach another device: no remote copies, remote signals or barrier semaphores. Data moves between devices by JAX's collectives and lax.ppermute only.
A program may use at most 128 MiB of HBM per device.

v0:
```python
import math

import jax
import jax.numpy as jnp
from jax import lax
from jax.sharding import PartitionSpec as P


def shards(queries, keys_values, doc_ids, gate_up, down_weight, routes, route_weights):
    tok_rows = queries.shape[0]
    local_heads = keys_values.shape[1]
    head_size = keys_values.shape[2] // 2
    groups = queries.shape[1] // (local_heads * head_size)
    query_grid = queries.reshape(tok_rows, local_heads, groups, head_size)
    first_pos = lax.axis_index("ctx") * tok_rows
    query_pos = first_pos + jnp.arange(tok_rows, dtype=jnp.int32)
    scale = 1.0 / math.sqrt(head_size)
    doc_wire = doc_ids.astype(jnp.bfloat16)
    kv_piece = lax.all_gather(keys_values, "ctx", axis=0, tiled=True)
    doc_piece = lax.all_gather(doc_wire, "ctx", axis=0, tiled=True)
    count = kv_piece.shape[0]
    key_pos = jnp.arange(count, dtype=jnp.int32)
    scores = (
        jnp.einsum(
            "qhgd,khd->hgqk",
            query_grid,
            kv_piece[:, :, :head_size],
            preferred_element_type=jnp.float32,
        )
        * scale
    )
    allowed = (doc_ids[:, None] == doc_piece.astype(jnp.int32)[None, :]) & (
        key_pos[None, :] <= query_pos[:, None]
    )
    scores = jnp.where(allowed, scores, jnp.float32(-1e30))
    run_max = jnp.full((local_heads, groups, tok_rows), -1e30, jnp.float32)
    new_max = jnp.maximum(run_max, jnp.max(scores, axis=-1))
    weights = jnp.where(allowed, jnp.exp(scores - new_max[..., None]), jnp.float32(0.0))
    new_total = jnp.sum(weights, axis=-1)
    update = jnp.einsum(
        "hgqk,khd->qhgd",
        weights.astype(jnp.bfloat16),
        kv_piece[:, :, head_size:],
        preferred_element_type=jnp.float32,
    )
    context = (
        (update / jnp.transpose(new_total, (2, 0, 1))[..., None])
        .reshape(tok_rows, -1)
        .astype(jnp.bfloat16)
    )
    residual = lax.all_to_all(context, "exp", split_axis=0, concat_axis=1, tiled=True)
    acts = gate_up[0]
    weight = down_weight[0]
    slot_total = acts.shape[0]
    ctx_count = lax.axis_size("ctx")
    exp_count = lax.axis_size("exp")
    capacity = slot_total // (ctx_count * exp_count)
    width = weight.shape[1]
    mine = lax.psum_scatter(
        jnp.dot(acts, weight, preferred_element_type=jnp.float32).astype(jnp.bfloat16),
        "ctx",
        scatter_dimension=0,
        tiled=True,
    ).astype(jnp.float32)
    mine = mine.astype(jnp.bfloat16).reshape(exp_count, capacity, width)
    home_rows = lax.all_to_all(mine, "exp", split_axis=0, concat_axis=0, tiled=True)
    expert_count = home_rows.shape[0]
    flat_routes = routes.reshape(-1)
    onehot = (flat_routes[:, None] == jnp.arange(expert_count, dtype=jnp.int32)[None, :]).astype(
        jnp.int32
    )
    earlier = jnp.cumsum(onehot, axis=0) - onehot
    slot_index = jnp.sum(earlier * onehot, axis=1)
    row_index = flat_routes * capacity + slot_index
    picked = home_rows.reshape(expert_count * capacity, width)[row_index]
    picked = picked.reshape(routes.shape[0], routes.shape[1], width).astype(jnp.float32)
    mixed = jnp.sum(route_weights[:, :, None] * picked, axis=1)
    moe_out = (residual.astype(jnp.float32) + mixed).astype(jnp.bfloat16)
    return (context, moe_out)


def solution(mesh):
    in_specs = (
        P("ctx", "exp"),
        P("ctx", "exp", None),
        P("ctx"),
        P("exp", None, "ctx"),
        P("exp", "ctx", None),
        P(("ctx", "exp"), None),
        P(("ctx", "exp"), None),
    )
    out_specs = (P("ctx", "exp"), P(("ctx", "exp"), None))
    return jax.shard_map(shards, mesh=mesh, in_specs=in_specs, out_specs=out_specs, check_vma=False)
```

profile of v0, /device:TPU:16, one launch (start us, length us, event | category | flops | bytes accessed | tf_op | source)
XLA Modules:
  0.0 309.7 jit_solution(5982555002560854336)
XLA Ops:
  7.2 0.7 all-gather.3.cloned.1.call-update
  8.0 0.5 copy-done
  8.5 14.4 %convolution_convert_fusion = bf16[1280,6144]{1,0:T(8,128)(2,1)} fusion(bf16[1,512,6144]{2,1,0:T(8,128)(2,1)} %param.11, bf16[1,1280,512]{2,1,0:T(8,128)(2,1)S(1)} %copy-done), kind=kOutput, calls=%fused_computation.1 | convolution fusion | flops 8060928000 | bytes 23330816 | tf_op jit(solution)/shard_map/dot_general | solution.py:60
  23.0 0.6 copy-done.4
  23.6 41.8 %all-gather = bf16[32,1,128]{2,1,0:T(2,128)(2,1)S(1)} all-gather(bf16[1,1,128]{2,1,0:T(2,128)(2,1)S(1)} %convert_bitcast_fusion.1), channel_id=1, replica_groups=mesh['ctx'=32,'exp'=8] {'ctx'}, dimensions={0}, use_global_device_ids=true | all-gather | bytes 8448 | tf_op jit(solution)/shard_map/all_gather | solution.py:20
  65.4 0.2 copy.36
  65.6 0.1 copy.44
  65.7 0.1 eq.31
  65.8 0.1 fusion.20
  65.8 1.8 fusion.8
  67.7 23.4 %all-gather.3.cloned.1.call-done = bf16[4096,1,256]{2,0,1:T(8,128)(2,1)} async-done(((bf16[128,1,256]{2,0,1:T(8,128)(2,1)}), bf16[4096,1,256]{2,0,1:T(8,128)(2,1)}) %all-gather.3.cloned.1.call-update) | async-done | bytes 2097168 | tf_op jit(solution)/shard_map/all_gather | solution.py:19
  91.1 3.3 %fusion = (f32[6,128]{1,0:T(8,128)S(1)}, f32[4096,128,6]{1,0,2:T(8,128)S(1)}) fusion(pred[128,4096]{0,1:T(8,128)(4,1)S(1)} %fusion.8, bf16[128,6,128]{0,2,1:T(8,128)(2,1)S(1)} %bitcast.86, bf16[4096,1,256]{2,0,1:T(8,128)(2,1)} %all-gather.3.cloned.1.call-done), kind=kOutput, calls=%fused_computation.4 | convolution fusion | flops 814742784 | bytes 14355456 | tf_op jit(solution)/shard_map/qhgd,khd->hgqk/dot_general | solution.py:24
  94.4 3.1 %fusion.1 = f32[6,128]{1,0:T(8,128)S(1)} fusion(f32[4096,128,6]{1,0,2:T(8,128)S(1)} %get-tuple-element.11, f32[6,128]{1,0:T(8,128)S(1)} %broadcast_maximum_fusion, pred[128,4096]{0,1:T(8,128)(4,1)S(1)} %fusion.8), kind=kLoop, calls=%fused_computation.5 | loop fusion | flops 15727872 | bytes 13113344 | tf_op jit(solution)/shard_map/reduce_sum | solution.py:39
  97.6 3.4 %fusion.17 = bf16[128,1,6,128]{0,3,2,1:T(8,128)(2,1)S(1)} fusion(bf16[4096,1,256]{2,0,1:T(8,128)(2,1)S(1)} %copy-done.5, f32[4096,128,6]{1,0,2:T(8,128)S(1)} %get-tuple-element.11, f32[6,128]{1,0:T(8,128)S(1)} %broadcast_maximum_fusion, pred[128,4096]{0,1:T(8,128)(4,1)S(1)} %fusion.8, f32[128,6]{0,1:T(8,128)S(1)} %bitcast.88), kind=kOutput, calls=%fused_computation.19 | convolution fusion | flops 821231616 | bytes 14360576 | tf_op jit(solution)/shard_map/hgqk,khd->qhgd/dot_general | solution.py:40
  100.9 0.2 copy.40
  101.1 0.9 convert_element_type.50
  102.1 5.8 %all-to-all-start = ((bf16[8,16,768]{2,1,0:T(8,128)(2,1)}), bf16[8,16,768]{2,1,0:T(8,128)(2,1)S(1)}, u32[]{:S(2)}, u32[]{:S(2)}) async-start(bf16[8,16,768]{2,1,0:T(8,128)(2,1)} %convert_element_type.50), calls=%async_computation | async-start | bytes 393216 | tf_op jit(solution)/shard_map/all_to_all | solution.py:51
  107.9 0.1 copy.43
  107.9 0.1 mul.50
  108.0 0.1 reduce_window_sum.11
  108.1 0.2 select_reduce_fusion
  108.3 173.7 %reduce-scatter.2.cloned.1.call-done = bf16[40,6144]{1,0:T(8,128)(2,1)} async-done(((bf16[1280,6144]{1,0:T(8,128)(2,1)}), bf16[40,6144]{1,0:T(8,128)(2,1)}) %reduce-scatter.2.cloned.1.call-update) | async-done | bytes 491536 | tf_op jit(solution)/shard_map/reduce_scatter | solution.py:59
  281.9 2.1 reshape.94
  284.1 5.9 %all-to-all-start.1 = ((bf16[8,5,6144]{2,1,0:T(8,128)(2,1)}), bf16[8,5,6144]{2,1,0:T(8,128)(2,1)S(1)}, u32[]{:S(2)}, u32[]{:S(2)}) async-start(bf16[8,5,6144]{2,1,0:T(8,128)(2,1)} %reshape.94), calls=%async_computation.2 | async-start | bytes 1572864 | tf_op jit(solution)/shard_map/all_to_all | solution.py:66
  290.0 0.1 copy.42
  290.0 0.8 copy.45
  290.9 8.6 %all-to-all-done.1 = bf16[8,5,6144]{2,1,0:T(8,128)(2,1)S(1)} async-done(((bf16[8,5,6144]{2,1,0:T(8,128)(2,1)}), bf16[8,5,6144]{2,1,0:T(8,128)(2,1)S(1)}, u32[]{:S(2)}, u32[]{:S(2)}) %all-to-all-start.1) | async-done | bytes 491552 | tf_op jit(solution)/shard_map/all_to_all | solution.py:66
  299.5 0.2 reshape.95
  299.7 0.8 gather_fusion
  300.5 0.5 reshape.97
  301.0 1.1 multiply_reduce_fusion
  302.1 0.7 add_convert_fusion
  (23 shorter events, 0.2 us)
Async XLA Ops:
  7.2 1.3 copy-start
  7.2 83.9 %all-gather.3.cloned.1.call-start = ((), (), s32[]{:S(2)}) async-start(), calls=%async_computation.3 | async-start | bytes 2162688 | tf_op jit(solution)/shard_map/all_gather | solution.py:19
  7.9 274.0 %reduce-scatter.2.cloned.1.call-start = ((), (), s32[]{:S(2)}) async-start(), calls=%async_computation.4 | async-start | bytes 16220160 | tf_op jit(solution)/shard_map/reduce_scatter | solution.py:59
  22.9 0.7 copy-start.4
  22.9 42.5 %copy-start.1 = (bf16[128,768]{1,0:T(8,128)(2,1)S(1)}, bf16[128,768]{1,0:T(8,128)(2,1)}, u32[]{:S(2)}) copy-start(bf16[128,768]{1,0:T(8,128)(2,1)} %param.7) | copy-start | bytes 589828
  22.9 42.6 %copy-start.2 = (s32[16,2]{0,1:T(2,128)S(1)}, s32[16,2]{0,1:T(2,128)}, u32[]{:S(2)}) copy-start(s32[16,2]{0,1:T(2,128)} %param.12) | copy-start | bytes 388
  91.1 6.5 %copy-start.5 = (bf16[4096,1,256]{2,0,1:T(8,128)(2,1)S(1)}, bf16[4096,1,256]{2,0,1:T(8,128)(2,1)}, u32[]{:S(2)}) copy-start(bf16[4096,1,256]{2,0,1:T(8,128)(2,1)} %all-gather.3.cloned.1.call-done) | copy-start | bytes 6291460
  97.6 192.4 %copy-start.3 = (f32[16,2]{0,1:T(2,128)S(1)}, f32[16,2]{0,1:T(2,128)}, u32[]{:S(2)}) copy-start(f32[16,2]{0,1:T(2,128)} %param.13) | copy-start | bytes 388
  102.1 182.0 %all-to-all-start = ((bf16[8,16,768]{2,1,0:T(8,128)(2,1)}), bf16[8,16,768]{2,1,0:T(8,128)(2,1)S(1)}, u32[]{:S(2)}, u32[]{:S(2)}) async-start(bf16[8,16,768]{2,1,0:T(8,128)(2,1)} %convert_element_type.50), calls=%async_computation | async-start | bytes 393216 | tf_op jit(solution)/shard_map/all_to_all | solution.py:51
  284.1 15.4 %all-to-all-start.1 = ((bf16[8,5,6144]{2,1,0:T(8,128)(2,1)}), bf16[8,5,6144]{2,1,0:T(8,128)(2,1)S(1)}, u32[]{:S(2)}, u32[]{:S(2)}) async-start(bf16[8,5,6144]{2,1,0:T(8,128)(2,1)} %reshape.94), calls=%async_computation.2 | async-start | bytes 1572864 | tf_op jit(solution)/shard_map/all_to_all | solution.py:66
Sparse Core Ops, SparseCore 0:
  10.8 80.2 all-gather.2
  95.7 186.2 reduce-scatter.1
where the time goes:
time: 311 us; the launch traced here: 310 us
  waiting for transfers between devices  206 us (66%)
  blocking collectives  41.8 us (13%)
  matrix products  21.2 us (7%)
  between operations  14.2 us (5%)
  starting transfers between devices  11.7 us (4%)
  local copies, waits for them, and re-layouts  7.35 us (2%)
  other arithmetic  7.13 us (2%)
    reduce_scatter x1, waiting for transfers between devices, shards(): lax.psum_scatter(jnp.dot(acts, weight, preferred_element_type=jnp.float32...  174 us
    all_gather x1, blocking collectives, shards(): doc_piece = lax.all_gather(doc_wire, 'ctx', axis=0, tiled=True)  41.8 us
    all_gather x1, waiting for transfers between devices, shards(): kv_piece = lax.all_gather(keys_values, 'ctx', axis=0, tiled=True)  23.4 us
    dot_general x1, matrix products, shards(): jnp.dot(acts, weight, preferred_element_type=jnp.float32)  14.4 us
    all_to_all x1, waiting for transfers between devices, shards(): lax.all_to_all(mine, 'exp', split_axis=0, concat_axis=0, tiled=True)  8.58 us
  transfers between devices with their start and end apart: 4, of which 3 were waited for; matrix products, arithmetic and copies ran while one was open for 10% of the time, Pallas kernels for 0%

commit v1 on v0

v1 whole, which is shorter than its diff:
```python
import math

import jax
import jax.numpy as jnp
from jax import lax
from jax.experimental import pallas as pl
from jax.experimental.pallas import tpu as pltpu
from jax.sharding import Mesh
from jax.sharding import PartitionSpec as P

AXES = ("yh", "z", "c", "x", "yl")
SHAPE = (2, 8, 2, 4, 2)
CTX = ("yh", "z", "c")
EXP = ("x", "yl")
Z = 8
EXPERTS = 8
PAD = 16
GROUPS = 2
PIECES = 4
PRODUCT_VMEM = 16 * 1024 * 1024
ATTENTION_VMEM = 24 * 1024 * 1024


def shift(value, step):
    return lax.ppermute(value, "z", [(i, (i + step) % Z) for i in range(Z)])


def swap(value, axis):
    return lax.ppermute(value, axis, [(0, 1), (1, 0)])


def after(value, *earlier):
    return lax.optimization_barrier((value,) + earlier)[0]


def attention_kernel(head, place, q_ref, doc_ref, a_ref, b_ref, o_ref, q_all, scores, top, total, acc):
    tokens = q_ref.shape[0]
    groups = q_ref.shape[1] // head
    high, along, core = place[0], place[1], place[2]
    mine = (high * Z + along) * 2 + core
    for g in range(groups):
        q_all[g * tokens : (g + 1) * tokens, :] = q_ref[:, g * head : (g + 1) * head]
    row = doc_ref[...].astype(jnp.float32)
    query_docs = jnp.transpose(jnp.broadcast_to(row, (tokens, tokens)))
    query_pos = lax.broadcasted_iota(jnp.int32, (tokens, tokens), 0) + mine * tokens
    lane = lax.broadcasted_iota(jnp.int32, (tokens, tokens), 1)
    top[...] = jnp.full_like(top, -1e30)
    total[...] = jnp.zeros_like(total)
    acc[...] = jnp.zeros_like(acc)
    arrays = ((a_ref, 0), (b_ref, 1))

    def origin(k, other_core):
        other_high = lax.rem(k, 2)
        high_at = high + other_high - 2 * high * other_high
        core_at = core + other_core - 2 * core * other_core
        return (high_at * Z + lax.div(k, 2)) * 2 + core_at

    for n, (ref, other_core) in enumerate(arrays):

        def score(k, carry, ref=ref, n=n, other_core=other_core):
            where = origin(k, other_core)

            @pl.when(where <= mine)
            def _():
                docs = ref[k, tokens : tokens + PAD, :tokens].astype(jnp.float32)[:1]
                allowed = (docs == query_docs) & (where * tokens + lane <= query_pos)
                s = lax.dot_general(
                    q_all[...],
                    ref[k, :tokens, :head],
                    (((1,), (1,)), ((), ())),
                    preferred_element_type=jnp.float32,
                )
                s = s.reshape(groups, tokens, tokens)
                s = jnp.where(allowed[None], s, jnp.float32(-1e30)).reshape(groups * tokens, tokens)
                scores[n * 2 * Z + k] = s
                top[...] = jnp.maximum(top[...], s)

            return carry

        lax.fori_loop(0, 2 * Z, score, 0)
    top[...] = jnp.broadcast_to(jnp.max(top[...], axis=1, keepdims=True), top.shape)
    factor = math.log2(math.e) / math.sqrt(head)
    for n, (ref, other_core) in enumerate(arrays):

        def mix(k, carry, ref=ref, n=n, other_core=other_core):
            where = origin(k, other_core)

            @pl.when(where <= mine)
            def _():
                weights = jnp.exp2((scores[n * 2 * Z + k] - top[...]) * factor)
                total[...] += weights
                acc[...] += jnp.dot(
                    weights.astype(jnp.bfloat16),
                    ref[k, :tokens, head:],
                    preferred_element_type=jnp.float32,
                )

            return carry

        lax.fori_loop(0, 2 * Z, mix, 0)
    out = acc[...] / jnp.sum(total[...], axis=1, keepdims=True)
    out = out.astype(o_ref.dtype)
    for g in range(groups):
        o_ref[:, g * head : (g + 1) * head] = out[g * tokens : (g + 1) * tokens, :]


def key_block(keys_values, doc_ids):
    tokens, width = doc_ids.shape[0], keys_values.shape[2]
    docs = jnp.pad(doc_ids.astype(jnp.bfloat16)[None, :], ((0, PAD - 1), (0, width - tokens)))
    return jnp.concatenate([keys_values, docs[:, None, :]], axis=0)


def attend(place, queries, doc_ids, near, far):
    tokens, width = doc_ids.shape[0], near.shape[-1]
    head = width // 2
    rows = queries.shape[1] // head * tokens
    spec = pl.BlockSpec(memory_space=pltpu.VMEM)
    return pl.pallas_call(
        lambda *refs: attention_kernel(head, *refs),
        out_shape=jax.ShapeDtypeStruct(queries.shape, jnp.bfloat16),
        in_specs=[pl.BlockSpec(memory_space=pltpu.SMEM)] + [spec] * 4,
        out_specs=spec,
        scratch_shapes=[
            pltpu.VMEM((rows, head), jnp.bfloat16),
            pltpu.VMEM((4 * Z, rows, tokens), jnp.float32),
            pltpu.VMEM((rows, tokens), jnp.float32),
            pltpu.VMEM((rows, tokens), jnp.float32),
            pltpu.VMEM((rows, head), jnp.float32),
        ],
        compiler_params=pltpu.CompilerParams(vmem_limit_bytes=ATTENTION_VMEM),
        name="attention",
    )(place, queries, doc_ids[None, :], near, far)


def product_kernel(place, a_ref, b_ref, wa_ref, wb_ref, o_ref):
    depth = a_ref.shape[-1]
    out = jnp.dot(a_ref[...].reshape(-1, depth), wa_ref[...], preferred_element_type=jnp.float32)
    out += jnp.dot(b_ref[...].reshape(-1, depth), wb_ref[...], preferred_element_type=jnp.float32)
    o_ref[...] = out.astype(o_ref.dtype).reshape(o_ref.shape)


def product(place, acts, acts_other, weight, other, first, tile, tiles, block, steps, pick):
    depth, rows = acts.shape[-1], acts.shape[2]
    half, start = weight.shape[1] // (2 * tile), first % (other.shape[1] // tile)
    acts_spec = pl.BlockSpec(block + (rows, depth), lambda j, i, s: pick(i, s) + (0, 0))
    return pl.pallas_call(
        product_kernel,
        out_shape=jax.ShapeDtypeStruct((steps * block[0], block[1], rows, tiles * tile), jnp.bfloat16),
        grid_spec=pltpu.PrefetchScalarGridSpec(
            num_scalar_prefetch=1,
            grid=(tiles, steps),
            in_specs=[
                acts_spec,
                acts_spec,
                pl.BlockSpec((depth, tile), lambda j, i, s: (0, s[2] * half + first + j)),
                pl.BlockSpec((depth, tile), lambda j, i, s: (0, start + j)),
            ],
            out_specs=pl.BlockSpec(block + (rows, tile), lambda j, i, s: (i, 0, 0, j)),
        ),
        compiler_params=pltpu.CompilerParams(vmem_limit_bytes=PRODUCT_VMEM),
        name="product",
    )(place, acts, acts_other, weight, other)


def add(*terms):
    total = terms[0].astype(jnp.float32)
    for term in terms[1:]:
        total = total + term.astype(jnp.float32)
    return total.astype(jnp.bfloat16)


def join(*values):
    return lax.optimization_barrier(values)


def chunk(array, at, axis):
    return lax.dynamic_index_in_dim(array, at % Z, axis, keepdims=False)


def shards(queries, keys_values, doc_ids, gate_up, down_weight, routes, route_weights):
    high, along, core = (lax.axis_index(name).astype(jnp.int32) for name in CTX)
    place = jnp.stack([high, along, core])
    weight = down_weight[0]
    columns = weight.shape[1] // (2 * GROUPS)
    depth = weight.shape[0]
    acts = gate_up[0].reshape(2, Z, -1, depth)

    acts_other = swap(gate_up[0], "c")
    part = lax.dynamic_slice(weight, (0, (1 - core) * GROUPS * columns), (depth, columns))
    other = [swap(part, "c")]
    block = key_block(keys_values, doc_ids)
    block_other = swap(block, "yh")
    at = after(((1 - core) * GROUPS + 1) * columns, part, block)
    other.append(swap(lax.dynamic_slice(weight, (0, at), (depth, columns)), "c"))
    acts_other, other[0], block_other = join(acts_other, other[0], block_other)
    acts_other = acts_other.reshape(2, Z, -1, depth)
    near = lax.all_gather(jnp.concatenate([block, block_other], axis=0), "z", axis=0, tiled=True)

    def first_group(where, block, steps, pick):
        return product(where, acts, acts_other, weight, other[0], 0, columns // 2, 2, block, steps, pick)

    def second_group(where, piece, pieces, pick):
        tile = columns // PIECES
        return product(
            where, acts, acts_other, weight, other[1], PIECES + piece, tile, pieces, (1, Z), 1, pick
        )[0]

    def sent_piece(where, piece):
        return second_group(where, piece, 1, lambda i, s: (1 - s[0], 0))

    down = first_group(place, (2, 1), 1, lambda i, s: (0, (s[1] + 4) % Z))[:, 0]
    up = first_group(after(place, down), (2, 1), 1, lambda i, s: (0, (s[1] + 3) % Z))[:, 0]
    sent = sent_piece(after(place, up), 0)
    down, up, sent = join(down, up, sent)
    got = []

    down, up, piece = shift(down, -1), shift(up, 1), swap(sent, "yh")
    full = first_group(after(place, sent), (1, Z), 2, lambda i, s: (i, 0))
    sent = sent_piece(after(place, full), 1)
    down, up, piece, full, sent = join(down, up, piece, full, sent)
    got.append(piece)
    down = add(down, chunk(full, along + 5, 1))
    up = add(up, chunk(full, along + 2, 1))
    down, up, sent = join(down, up, sent)

    here = after(place, down)
    down, up, piece = shift(down, -1), shift(up, 1), swap(sent, "yh")
    sent = sent_piece(here, 2)
    kept = second_group(after(place, sent), 0, PIECES, lambda i, s: (s[0], 0))
    down, up, piece, kept, sent = join(down, up, piece, kept, sent)
    got.append(piece)
    down = add(down, chunk(full, along + 6, 1))
    up = add(up, chunk(full, along + 1, 1))
    down, up, sent = join(down, up, sent)

    here = after(place, down)
    down, up, piece = shift(down, -1), shift(up, 1), swap(sent, "yh")
    sent = sent_piece(here, 3)
    down, up, piece, sent = join(down, up, piece, sent)
    got.append(piece)
    down = add(down, chunk(full, along + 7, 1))
    down, sent = join(down, sent)

    down, piece = shift(down, -1), swap(sent, "yh")
    down, piece, near = join(down, piece, near)
    got.append(piece)
    first = add(down, up, chunk(full, along, 1))

    def second_term(offset):
        received = jnp.concatenate([chunk(piece, along + offset, 0) for piece in got], axis=1)
        return chunk(kept, along + offset, 0), received

    going = chunk_of(first, 1 - high)
    down, up = add(*second_term(4)), add(*second_term(3))
    down, up, going = join(down, up, going)
    down, up, moved = shift(down, -1), shift(up, 1), swap(going, "yh")
    near = near.reshape(2 * Z, -1, near.shape[-1])
    context = attend(place, queries, doc_ids, near, swap(near, "c"))
    down, up, context = join(down, up, context)
    residual = lax.all_to_all(context, EXP, split_axis=0, concat_axis=1, tiled=True)
    down, up = add(down, *second_term(5)), add(up, *second_term(2))
    down, up = shift(down, -1), shift(up, 1)
    down, up, moved = join(down, up, moved)
    first = add(chunk_of(first, high), moved)
    down, up = add(down, *second_term(6)), add(up, *second_term(1))
    down, up = shift(down, -1), shift(up, 1)
    down, up, residual = join(down, up, residual)
    down = add(down, *second_term(7))
    second = add(shift(down, -1), up, *second_term(0))

    tokens = routes.shape[0]
    capacity = first.shape[0] // (2 * EXPERTS)
    mix = mixing(routes, route_weights, capacity)
    mixed = []
    for rows in (first, second):
        home = lax.all_to_all(
            rows.reshape(2 * EXPERTS, capacity, -1), ("c",) + EXP, split_axis=0, concat_axis=0, tiled=True
        )
        home = home.reshape(2, EXPERTS * capacity, -1)
        both = jnp.einsum("tr,crn->tcn", mix, home, preferred_element_type=jnp.float32)
        mixed.append(both[:tokens] + both[tokens:])
    mixed = jnp.concatenate(mixed, axis=2).reshape(tokens, -1)
    moe_out = residual.astype(jnp.float32) + mixed
    return (context, moe_out.astype(jnp.bfloat16))


def chunk_of(array, at):
    return lax.dynamic_index_in_dim(array, at, 0, keepdims=False)


def mixing(routes, route_weights, capacity):
    flat = routes.reshape(-1)
    pairs = jnp.arange(flat.shape[0])
    same = (flat[:, None] == flat[None, :]) & (pairs[None, :] < pairs[:, None])
    slot = jnp.sum(same.astype(jnp.int32), axis=1).reshape(routes.shape)
    row = routes * capacity + slot
    hit = row[:, :, None] == jnp.arange(EXPERTS * capacity)[None, None, :]
    mix = jnp.sum(jnp.where(hit, route_weights[:, :, None], 0.0), axis=1)
    coarse = mix.astype(jnp.bfloat16)
    fine = (mix - coarse.astype(jnp.float32)).astype(jnp.bfloat16)
    return jnp.concatenate([coarse, fine], axis=0)


def solution(mesh):
    inner = Mesh(mesh.devices.reshape(SHAPE), AXES)
    in_specs = (
        P(CTX, EXP),
        P(CTX, EXP, None),
        P(CTX),
        P(EXP, None, CTX),
        P(EXP, CTX, None),
        P(CTX + EXP, None),
        P(CTX + EXP, None),
    )
    out_specs = (P(CTX, EXP), P(CTX + EXP, None))
    return jax.shard_map(shards, mesh=inner, in_specs=in_specs, out_specs=out_specs, check_vma=False)
```

time: 311 us -> 206 us (0.66)
  waiting for transfers between devices: 206 us -> 49.2 us
  blocking collectives: 41.8 us -> 0 us
  Pallas kernels: 0 us -> 41.1 us
  starting transfers between devices: 11.7 us -> 48.4 us
  local copies, waits for them, and re-layouts: 7.35 us -> 28.5 us
  matrix products: 21.2 us -> 0.38 us
  other arithmetic: 7.13 us -> 22.1 us
    reduce_scatter x1 -> x0, waiting for transfers between devices: 174 us -> none  [shards(): lax.psum_scatter(jnp.dot(acts, weight, preferred_element_type=jnp.float32...]
    all_gather x1 -> x0, blocking collectives: 41.8 us -> none  [shards(): doc_piece = lax.all_gather(doc_wire, 'ctx', axis=0, tiled=True)]
    pallas_call x0 -> x9, Pallas kernels: none -> 41.1 us  [the longest x8 30.5 us: product(): pl.pallas_call(product_kernel, out_shape=jax.ShapeDtypeStruct((steps * bl...]
    ppermute x0 -> x24, starting transfers between devices: none -> 34.6 us  [the longest x14 26.6 us: shift(): return lax.ppermute(value, 'z', [(i, (i + step) % Z) for i in range(Z)])]
    ppermute x0 -> x24, waiting for transfers between devices: none -> 28.9 us  [the longest x14 23.2 us: shift(): return lax.ppermute(value, 'z', [(i, (i + step) % Z) for i in range(Z)])]
    all_gather x1, waiting for transfers between devices: 23.4 us -> 0.01 us  [shards(): lax.all_gather(jnp.concatenate([block, block_other], axis=0), 'z', axis=0...]
    dot_general x3 -> x2, matrix products: 21.2 us -> 0.38 us  [shards(): jnp.einsum('tr,crn->tcn', mix, home, preferred_element_type=jnp.float32)]
    convert_element_type x3 -> x12, other arithmetic: 0.82 us -> 19.5 us  [the longest x10 18.8 us: add(): return total.astype(jnp.bfloat16)]
  transfers between devices with their start and end apart: 4 -> 28, of which waited for: 3 -> 12; matrix products, arithmetic and copies ran while one was open for 10% -> 14% of each run, Pallas kernels for 0% -> 19%
where the time goes in v1:
time: 206 us; the launch traced here: 204 us
  waiting for transfers between devices  49.2 us (24%)
  starting transfers between devices  48.4 us (23%)
  Pallas kernels  41.1 us (20%)
  local copies, waits for them, and re-layouts  28.5 us (14%)
  other arithmetic  22.1 us (11%)
  between operations  14.3 us (7%)
    pallas_call x8, Pallas kernels, product(): pl.pallas_call(product_kernel, out_shape=jax.ShapeDtypeStruct((steps * bl...  30.5 us
    ppermute x14, starting transfers between devices, shift(): return lax.ppermute(value, 'z', [(i, (i + step) % Z) for i in range(Z)])  26.6 us
    ppermute x14, waiting for transfers between devices, shift(): return lax.ppermute(value, 'z', [(i, (i + step) % Z) for i in range(Z)])  23.2 us
    convert_element_type x10, other arithmetic, add(): return total.astype(jnp.bfloat16)  18.8 us
    all_to_all x2, waiting for transfers between devices, shards(): lax.all_to_all(rows.reshape(2 * EXPERTS, capacity, -1), ('c',) + EXP, spl...  13.8 us
    unnamed x33, local copies, waits for them, and re-layouts  13.4 us
    pallas_call x1, Pallas kernels, attend(): pl.pallas_call(lambda *refs: attention_kernel(head, *refs), out_shape=jax...  10.7 us
    all_to_all x2, starting transfers between devices, shards(): lax.all_to_all(rows.reshape(2 * EXPERTS, capacity, -1), ('c',) + EXP, spl...  9 us
  transfers between devices with their start and end apart: 28, of which 12 were waited for; matrix products, arithmetic and copies ran while one was open for 14% of the time, Pallas kernels for 19%

profile of v1, /device:TPU:16, one launch (start us, length us, event | category | flops | bytes accessed | tf_op | source)
XLA Modules:
  0.0 204.1 jit_solution(15794386291180738204)
XLA Ops:
  7.2 2.8 %dynamic-slice_bitcast_fusion.1 = bf16[512,1536]{1,0:T(8,128)(2,1)} fusion(bf16[1,512,6144]{2,1,0:T(8,128)(2,1)} %param.11, s32[]{:T(128)S(6)} %select_n.193), kind=kLoop, calls=%fused_computation.1 | loop fusion | bytes 3145732 | tf_op jit(solution)/shard_map/dynamic_slice | solution.py:189
  11.5 3.5 %dynamic-slice_bitcast_fusion = bf16[512,1536]{1,0:T(8,128)(2,1)} fusion(bf16[1,512,6144]{2,1,0:T(8,128)(2,1)} %param.11, s32[]{:T(128)S(6)} %select_n.194), kind=kLoop, calls=%fused_computation | loop fusion | bytes 3145732 | tf_op jit(solution)/shard_map/dynamic_slice | solution.py:194
  17.7 4.0 %collective-permute-done.2 = bf16[144,1,256]{2,0,1:T(8,128)(2,1)S(1)} collective-permute-done((bf16[144,1,256]{2,0,1:T(8,128)(2,1)S(1)}, bf16[144,1,256]{2,0,1:T(8,128)(2,1)S(1)}, u32[]{:S(2)}, u32[]{:S(2)}) %collective-permute-start.2) | collective-permute-done | bytes 73760 | tf_op jit(solution)/shard_map/ppermute | solution.py:29
  21.7 2.8 %copy-done = bf16[1,512,6144]{2,1,0:T(8,128)(2,1)S(1)} copy-done((bf16[1,512,6144]{2,1,0:T(8,128)(2,1)S(1)}, bf16[1,512,6144]{2,1,0:T(8,128)(2,1)}, u32[]{:S(2)}) %copy-start) | copy-done | bytes 6291480
  24.5 3.3 %product.8 = bf16[2,1,80,1536]{3,2,1,0:T(8,128)(2,1)} custom-call(s32[3]{0:T(128)S(1)} %pad_add_fusion.place.refs_0_, bf16[2,8,80,512]{3,2,1,0:T(8,128)(2,1)S(1)} %bitcast.157, bf16[2,8,80,512]{3,2,1,0:T(8,128)(2,1)S(1)} %bitcast.165, bf16[512,6144]{1,0:T(8,128)(2,1)S(1)} %bitcast.148, bf16[512,1536]{1,0:T(8,128)(2,1)} %collective-permute-done.1.wb_ref), custom_call_target="tpu_custom_call" | custom-call | tf_op jit(solution)/shard_map/product/pallas_call | solution.py:146
  27.9 3.4 %product.9 = bf16[2,1,80,1536]{3,2,1,0:T(8,128)(2,1)} custom-call(s32[3]{0:T(128)S(1)} %pad_add_fusion.place.refs_0_, bf16[2,8,80,512]{3,2,1,0:T(8,128)(2,1)S(1)} %bitcast.158, bf16[2,8,80,512]{3,2,1,0:T(8,128)(2,1)S(1)} %bitcast.166, bf16[512,6144]{1,0:T(8,128)(2,1)S(1)} %bitcast.149, bf16[512,1536]{1,0:T(8,128)(2,1)} %collective-permute-done.1.wb_ref), custom_call_target="tpu_custom_call" | custom-call | tf_op jit(solution)/shard_map/product/pallas_call | solution.py:146
  31.3 3.2 %product.10 = bf16[1,8,80,384]{3,2,1,0:T(8,128)(2,1)} custom-call(s32[3]{0:T(128)S(1)} %pad_add_fusion.place.refs_0_, bf16[2,8,80,512]{3,2,1,0:T(8,128)(2,1)S(1)} %bitcast.159, bf16[2,8,80,512]{3,2,1,0:T(8,128)(2,1)S(1)} %bitcast.167, bf16[512,6144]{1,0:T(8,128)(2,1)S(1)} %bitcast.150, bf16[512,1536]{1,0:T(8,128)(2,1)} %collective-permute-done.3.wb_ref), custom_call_target="tpu_custom_call" | custom-call | tf_op jit(solution)/shard_map/product/pallas_call | solution.py:146
  34.5 5.9 %collective-permute-start.4 = (bf16[2,80,1536]{2,1,0:T(8,128)(2,1)}, bf16[2,80,1536]{2,1,0:T(8,128)(2,1)}, u32[]{:S(2)}, u32[]{:S(2)}) collective-permute-start(bf16[2,80,1536]{2,1,0:T(8,128)(2,1)} %bitcast.10), channel_id=1, source_target_pairs={{0,112},{16,0},{32,16},{48,32},{64,48},{80,64},{96,80},{112,96},{1... | collective-permute-start | bytes 1474568 | tf_op jit(solution)/shard_map/ppermute | solution.py:25
  40.7 2.8 %copy-done.1 = bf16[1,512,6144]{2,1,0:T(8,128)(2,1)S(1)} copy-done((bf16[1,512,6144]{2,1,0:T(8,128)(2,1)S(1)}, bf16[1,512,6144]{2,1,0:T(8,128)(2,1)}, u32[]{:S(2)}) %copy-start.1) | copy-done | bytes 6291480
  43.5 6.9 %product.11 = bf16[2,8,80,1536]{3,2,1,0:T(8,128)(2,1)S(1)} custom-call(s32[3]{0:T(128)S(1)} %pad_add_fusion.place.refs_0_, bf16[2,8,80,512]{3,2,1,0:T(8,128)(2,1)S(1)} %bitcast.160, bf16[2,8,80,512]{3,2,1,0:T(8,128)(2,1)S(1)} %bitcast.168, bf16[512,6144]{1,0:T(8,128)(2,1)S(1)} %bitcast.151, bf16[512,1536]{1,0:T(8,128)(2,1)} %collective-permute-done.1.wb_ref), custom_call_target="tpu_custom_call" | custom-call | tf_op jit(solution)/shard_map/product/pallas_call | solution.py:146
  50.4 2.7 %product.12 = bf16[1,8,80,384]{3,2,1,0:T(8,128)(2,1)S(1)} custom-call(s32[3]{0:T(128)S(1)} %pad_add_fusion.place.refs_0_, bf16[2,8,80,512]{3,2,1,0:T(8,128)(2,1)S(1)} %bitcast.161, bf16[2,8,80,512]{3,2,1,0:T(8,128)(2,1)S(1)} %bitcast.169, bf16[512,6144]{1,0:T(8,128)(2,1)S(1)} %bitcast.152, bf16[512,1536]{1,0:T(8,128)(2,1)} %collective-permute-done.3.wb_ref), custom_call_target="tpu_custom_call" | custom-call | tf_op jit(solution)/shard_map/product/pallas_call | solution.py:146
  54.8 2.4 %fusion.4 = (bf16[2,80,1536]{2,1,0:T(8,128)(2,1)}, bf16[2,80,1536]{2,1,0:T(8,128)(2,1)}) fusion(bf16[2,80,1536]{2,1,0:T(8,128)(2,1)} %collective-permute-done.5, s32[]{:T(128)S(6)} %select_n.198, s32[]{:T(128)S(6)} %select_n.196, bf16[2,80,1536]{2,1,0:T(8,128)(2,1)} %collective-permute-done.4, bf16[2,8,80,1536]{3,2,1,0:T(8,128)(2,1)S(1)} %product.11), kind=kLoop, calls=%fused_computation.11 | loop fusion | flops 1966080 | bytes 2949128 | tf_op jit(solution)/shard_map/convert_element_type | solution.py:169
  57.1 3.0 %collective-permute-start.7 = (bf16[2,80,1536]{2,1,0:T(8,128)(2,1)}, bf16[2,80,1536]{2,1,0:T(8,128)(2,1)}, u32[]{:S(2)}, u32[]{:S(2)}) collective-permute-start(bf16[2,80,1536]{2,1,0:T(8,128)(2,1)} %get-tuple-element.67), channel_id=1, source_target_pairs={{0,112},{16,0},{32,16},{48,32},{64,48},{80,64},{96,80},{112,96},{1... | collective-permute-start | bytes 1474568 | tf_op jit(solution)/shard_map/ppermute | solution.py:25
  62.6 2.8 %copy-done.2 = bf16[1,512,6144]{2,1,0:T(8,128)(2,1)S(1)} copy-done((bf16[1,512,6144]{2,1,0:T(8,128)(2,1)S(1)}, bf16[1,512,6144]{2,1,0:T(8,128)(2,1)}, u32[]{:S(2)}) %copy-start.2) | copy-done | bytes 6291480
  65.4 3.2 %product.13 = bf16[1,8,80,384]{3,2,1,0:T(8,128)(2,1)} custom-call(s32[3]{0:T(128)S(1)} %pad_add_fusion.place.refs_0_, bf16[2,8,80,512]{3,2,1,0:T(8,128)(2,1)S(1)} %bitcast.162, bf16[2,8,80,512]{3,2,1,0:T(8,128)(2,1)S(1)} %bitcast.170, bf16[512,6144]{1,0:T(8,128)(2,1)S(1)} %bitcast.153, bf16[512,1536]{1,0:T(8,128)(2,1)} %collective-permute-done.3.wb_ref), custom_call_target="tpu_custom_call" | custom-call | tf_op jit(solution)/shard_map/product/pallas_call | solution.py:146
  68.6 5.4 %product.14 = bf16[1,8,80,1536]{3,2,1,0:T(8,128)(2,1)S(1)} custom-call(s32[3]{0:T(128)S(1)} %pad_add_fusion.place.refs_0_, bf16[2,8,80,512]{3,2,1,0:T(8,128)(2,1)S(1)} %bitcast.163, bf16[2,8,80,512]{3,2,1,0:T(8,128)(2,1)S(1)} %bitcast.171, bf16[512,6144]{1,0:T(8,128)(2,1)S(1)} %bitcast.154, bf16[512,1536]{1,0:T(8,128)(2,1)} %collective-permute-done.3.wb_ref), custom_call_target="tpu_custom_call" | custom-call | tf_op jit(solution)/shard_map/product/pallas_call | solution.py:146
  75.3 2.7 %fusion.2 = (bf16[2,80,1536]{2,1,0:T(8,128)(2,1)}, bf16[2,80,1536]{2,1,0:T(8,128)(2,1)}) fusion(bf16[2,80,1536]{2,1,0:T(8,128)(2,1)} %collective-permute-done.8, s32[]{:T(128)S(6)} %select_n.204, s32[]{:T(128)S(6)} %select_n.202, bf16[2,80,1536]{2,1,0:T(8,128)(2,1)} %collective-permute-done.7, bf16[2,8,80,1536]{3,2,1,0:T(8,128)(2,1)} %copy-done.5), kind=kLoop, calls=%fused_computation.7 | loop fusion | flops 1966080 | bytes 2949128 | tf_op jit(solution)/shard_map/convert_element_type | solution.py:169
  78.0 3.2 %collective-permute-start.10 = (bf16[2,80,1536]{2,1,0:T(8,128)(2,1)}, bf16[2,80,1536]{2,1,0:T(8,128)(2,1)}, u32[]{:S(2)}, u32[]{:S(2)}) collective-permute-start(bf16[2,80,1536]{2,1,0:T(8,128)(2,1)} %get-tuple-element.78), channel_id=1, source_target_pairs={{0,112},{16,0},{32,16},{48,32},{64,48},{80,64},{96,80},{112,96},{1... | collective-permute-start | bytes 1474568 | tf_op jit(solution)/shard_map/ppermute | solution.py:25
  83.0 2.8 %copy-done.3 = bf16[1,512,6144]{2,1,0:T(8,128)(2,1)S(1)} copy-done((bf16[1,512,6144]{2,1,0:T(8,128)(2,1)S(1)}, bf16[1,512,6144]{2,1,0:T(8,128)(2,1)}, u32[]{:S(2)}) %copy-start.3) | copy-done | bytes 6291480
  85.8 2.4 %product.15 = bf16[1,8,80,384]{3,2,1,0:T(8,128)(2,1)S(1)} custom-call(s32[3]{0:T(128)S(1)} %pad_add_fusion.place.refs_0_, bf16[2,8,80,512]{3,2,1,0:T(8,128)(2,1)S(1)} %bitcast.164, bf16[2,8,80,512]{3,2,1,0:T(8,128)(2,1)S(1)} %bitcast.172, bf16[512,6144]{1,0:T(8,128)(2,1)S(1)} %bitcast.155, bf16[512,1536]{1,0:T(8,128)(2,1)} %collective-permute-done.3.wb_ref), custom_call_target="tpu_custom_call" | custom-call | tf_op jit(solution)/shard_map/product/pallas_call | solution.py:146
  88.2 9.5 %collective-permute-done.10 = bf16[2,80,1536]{2,1,0:T(8,128)(2,1)} collective-permute-done((bf16[2,80,1536]{2,1,0:T(8,128)(2,1)}, bf16[2,80,1536]{2,1,0:T(8,128)(2,1)}, u32[]{:S(2)}, u32[]{:S(2)}) %collective-permute-start.10) | collective-permute-done | bytes 491552 | tf_op jit(solution)/shard_map/ppermute | solution.py:25
  97.6 3.1 %collective-permute-done.11 = bf16[2,80,1536]{2,1,0:T(8,128)(2,1)} collective-permute-done((bf16[2,80,1536]{2,1,0:T(8,128)(2,1)}, bf16[2,80,1536]{2,1,0:T(8,128)(2,1)}, u32[]{:S(2)}, u32[]{:S(2)}) %collective-permute-start.11) | collective-permute-done | bytes 491552 | tf_op jit(solution)/shard_map/ppermute | solution.py:25
  108.4 5.8 %collective-permute-done.13 = bf16[2,80,1536]{2,1,0:T(8,128)(2,1)} collective-permute-done((bf16[2,80,1536]{2,1,0:T(8,128)(2,1)}, bf16[2,80,1536]{2,1,0:T(8,128)(2,1)}, u32[]{:S(2)}, u32[]{:S(2)}) %collective-permute-start.13) | collective-permute-done | bytes 491552 | tf_op jit(solution)/shard_map/ppermute | solution.py:25
  125.6 10.7 %attention.1 = bf16[128,768]{1,0:T(8,128)(2,1)} custom-call(s32[3]{0:T(128)S(1)} %pad_add_fusion.place.refs_0_, bf16[128,768]{1,0:T(8,128)(2,1)S(1)} %copy-done.9, s32[1,128]{1,0:T(1,128)S(1)} %bitcast.182, bf16[16,144,256]{2,1,0:T(8,128)(2,1)S(1)} %bitcast.179, bf16[16,144,256]{2,1,0:T(8,128)(2,1)} %collective-permute-done.17.refs_4_), custom_call_target="tpu_custom_call" | custom-call | tf_op jit(solution)/shard_map/attention/pallas_call | solution.py:118
  138.6 7.4 %collective-permute-start.18 = (bf16[80,1536]{1,0:T(8,128)(2,1)}, bf16[80,1536]{1,0:T(8,128)(2,1)S(1)}, u32[]{:S(2)}, u32[]{:S(2)}) collective-permute-start(bf16[80,1536]{1,0:T(8,128)(2,1)} %get-tuple-element.111), channel_id=1, source_target_pairs={{0,112},{16,0},{32,16},{48,32},{64,48},{80,64},{96,80},{112,96},{1... | collective-permute-start | bytes 737288 | tf_op jit(solution)/shard_map/ppermute | solution.py:25
  145.9 4.8 %all-to-all-start = ((bf16[8,16,768]{2,1,0:T(8,128)(2,1)}), bf16[8,16,768]{2,1,0:T(8,128)(2,1)S(1)}, u32[]{:S(2)}, u32[]{:S(2)}) async-start(bf16[8,16,768]{2,1,0:T(8,128)(2,1)} %bitcast.184), calls=%async_computation | async-start | bytes 393216 | tf_op jit(solution)/shard_map/all_to_all | solution.py:260
  150.8 6.6 %all-to-all-done = bf16[8,16,768]{2,1,0:T(8,128)(2,1)S(1)} async-done(((bf16[8,16,768]{2,1,0:T(8,128)(2,1)}), bf16[8,16,768]{2,1,0:T(8,128)(2,1)S(1)}, u32[]{:S(2)}, u32[]{:S(2)}) %all-to-all-start) | async-done | bytes 196640 | tf_op jit(solution)/shard_map/all_to_all | solution.py:260
  159.5 3.2 %collective-permute-start.21 = (bf16[80,1536]{1,0:T(8,128)(2,1)}, bf16[80,1536]{1,0:T(8,128)(2,1)}, u32[]{:S(2)}, u32[]{:S(2)}) collective-permute-start(bf16[80,1536]{1,0:T(8,128)(2,1)} %get-tuple-element.109), channel_id=1, source_target_pairs={{0,112},{16,0},{32,16},{48,32},{64,48},{80,64},{96,80},{112,96},{1... | collective-permute-start | bytes 737288 | tf_op jit(solution)/shard_map/ppermute | solution.py:25
  164.6 3.6 %all-to-all-start.1 = ((bf16[16,5,1536]{2,1,0:T(8,128)(2,1)}), bf16[16,5,1536]{2,1,0:T(8,128)(2,1)S(1)}, u32[]{:S(2)}, u32[]{:S(2)}) async-start(bf16[16,5,1536]{2,1,0:T(8,128)(2,1)} %reshape.70), calls=%async_computation.1 | async-start | bytes 786432 | tf_op jit(solution)/shard_map/all_to_all | solution.py:276
  173.3 4.3 %all-to-all-done.1 = bf16[16,5,1536]{2,1,0:T(8,128)(2,1)S(1)} async-done(((bf16[16,5,1536]{2,1,0:T(8,128)(2,1)}), bf16[16,5,1536]{2,1,0:T(8,128)(2,1)S(1)}, u32[]{:S(2)}, u32[]{:S(2)}) %all-to-all-start.1) | async-done | bytes 245792 | tf_op jit(solution)/shard_map/all_to_all | solution.py:276
  181.2 5.4 %all-to-all-start.2 = ((bf16[16,5,1536]{2,1,0:T(8,128)(2,1)}), bf16[16,5,1536]{2,1,0:T(8,128)(2,1)S(1)}, u32[]{:S(2)}, u32[]{:S(2)}) async-start(bf16[16,5,1536]{2,1,0:T(8,128)(2,1)} %reshape.72), calls=%async_computation.2 | async-start | bytes 786432 | tf_op jit(solution)/shard_map/all_to_all | solution.py:276
  186.7 9.5 %all-to-all-done.2 = bf16[16,5,1536]{2,1,0:T(8,128)(2,1)S(1)} async-done(((bf16[16,5,1536]{2,1,0:T(8,128)(2,1)}), bf16[16,5,1536]{2,1,0:T(8,128)(2,1)S(1)}, u32[]{:S(2)}, u32[]{:S(2)}) %all-to-all-start.2) | async-done | bytes 245792 | tf_op jit(solution)/shard_map/all_to_all | solution.py:276
  (107 shorter events, 46.8 us)
Async XLA Ops:
  7.2 108.4 %all-gather.2.cloned.1.call-start = ((), (), s32[]{:S(2)}) async-start(), calls=%async_computation.3 | async-start | bytes 1327104 | tf_op jit(solution)/shard_map/all_gather | solution.py:197
  10.0 11.8 %collective-permute-start.1 = (bf16[512,1536]{1,0:T(8,128)(2,1)}, bf16[512,1536]{1,0:T(8,128)(2,1)}, u32[]{:S(2)}, u32[]{:S(2)}) collective-permute-start(bf16[512,1536]{1,0:T(8,128)(2,1)} %dynamic-slice_bitcast_fusion.1), channel_id=1, source_target_pairs={{0,8},{8,0},{1,9},{9,1},{2,10},{10,2},{3,11},{11,3},{4,12},{12,4},... | collective-permute-start | bytes 4718600 | tf_op jit(solution)/shard_map/ppermute | solution.py:29
  15.0 16.3 %collective-permute-start.3 = (bf16[512,1536]{1,0:T(8,128)(2,1)}, bf16[512,1536]{1,0:T(8,128)(2,1)}, u32[]{:S(2)}, u32[]{:S(2)}) collective-permute-start(bf16[512,1536]{1,0:T(8,128)(2,1)} %dynamic-slice_bitcast_fusion), channel_id=1, source_target_pairs={{0,8},{8,0},{1,9},{9,1},{2,10},{10,2},{3,11},{11,3},{4,12},{12,4},... | collective-permute-start | bytes 4718600 | tf_op jit(solution)/shard_map/ppermute | solution.py:29
  15.5 6.2 %collective-permute-start = (bf16[1280,512]{1,0:T(8,128)(2,1)S(1)}, bf16[1280,512]{1,0:T(8,128)(2,1)S(1)}, u32[]{:S(2)}, u32[]{:S(2)}) collective-permute-start(bf16[1280,512]{1,0:T(8,128)(2,1)S(1)} %bitcast.156), channel_id=1, source_target_pairs={{0,8},{8,0},{1,9},{9,1},{2,10},{10,2},{3,11},{11,3},{4,12},{12,4},... | collective-permute-start | bytes 3932168 | tf_op jit(solution)/shard_map/ppermute | solution.py:29
  15.5 6.2 %collective-permute-start.2 = (bf16[144,1,256]{2,0,1:T(8,128)(2,1)S(1)}, bf16[144,1,256]{2,0,1:T(8,128)(2,1)S(1)}, u32[]{:S(2)}, u32[]{:S(2)}) collective-permute-start(bf16[144,1,256]{2,0,1:T(8,128)(2,1)S(1)} %pad_maximum_fusion.1), channel_id=1, source_target_pairs={{0,128},{128,0},{1,129},{129,1},{2,130},{130,2},{3,131},{131,3},{4... | collective-permute-start | bytes 221192 | tf_op jit(solution)/shard_map/ppermute | solution.py:29
  34.5 18.6 %collective-permute-start.4 = (bf16[2,80,1536]{2,1,0:T(8,128)(2,1)}, bf16[2,80,1536]{2,1,0:T(8,128)(2,1)}, u32[]{:S(2)}, u32[]{:S(2)}) collective-permute-start(bf16[2,80,1536]{2,1,0:T(8,128)(2,1)} %bitcast.10), channel_id=1, source_target_pairs={{0,112},{16,0},{32,16},{48,32},{64,48},{80,64},{96,80},{112,96},{1... | collective-permute-start | bytes 1474568 | tf_op jit(solution)/shard_map/ppermute | solution.py:25
  40.4 14.1 %collective-permute-start.5 = (bf16[2,80,1536]{2,1,0:T(8,128)(2,1)}, bf16[2,80,1536]{2,1,0:T(8,128)(2,1)}, u32[]{:S(2)}, u32[]{:S(2)}) collective-permute-start(bf16[2,80,1536]{2,1,0:T(8,128)(2,1)} %bitcast.11), channel_id=1, source_target_pairs={{0,16},{16,32},{32,48},{48,64},{64,80},{80,96},{96,112},{112,0},{1... | collective-permute-start | bytes 1474568 | tf_op jit(solution)/shard_map/ppermute | solution.py:25
  40.4 14.4 %collective-permute-start.6 = (bf16[8,80,384]{2,1,0:T(8,128)(2,1)}, bf16[8,80,384]{2,1,0:T(8,128)(2,1)}, u32[]{:S(2)}, u32[]{:S(2)}) collective-permute-start(bf16[8,80,384]{2,1,0:T(8,128)(2,1)} %bitcast.13), channel_id=1, source_target_pairs={{0,128},{128,0},{1,129},{129,1},{2,130},{130,2},{3,131},{131,3},{4... | collective-permute-start | bytes 1474568 | tf_op jit(solution)/shard_map/ppermute | solution.py:29
  57.1 18.2 %collective-permute-start.7 = (bf16[2,80,1536]{2,1,0:T(8,128)(2,1)}, bf16[2,80,1536]{2,1,0:T(8,128)(2,1)}, u32[]{:S(2)}, u32[]{:S(2)}) collective-permute-start(bf16[2,80,1536]{2,1,0:T(8,128)(2,1)} %get-tuple-element.67), channel_id=1, source_target_pairs={{0,112},{16,0},{32,16},{48,32},{64,48},{80,64},{96,80},{112,96},{1... | collective-permute-start | bytes 1474568 | tf_op jit(solution)/shard_map/ppermute | solution.py:25
  60.1 15.3 %collective-permute-start.8 = (bf16[2,80,1536]{2,1,0:T(8,128)(2,1)}, bf16[2,80,1536]{2,1,0:T(8,128)(2,1)}, u32[]{:S(2)}, u32[]{:S(2)}) collective-permute-start(bf16[2,80,1536]{2,1,0:T(8,128)(2,1)} %get-tuple-element.68), channel_id=1, source_target_pairs={{0,16},{16,32},{32,48},{48,64},{64,80},{80,96},{96,112},{112,0},{1... | collective-permute-start | bytes 1474568 | tf_op jit(solution)/shard_map/ppermute | solution.py:25
  60.1 15.3 %collective-permute-start.9 = (bf16[8,80,384]{2,1,0:T(8,128)(2,1)S(1)}, bf16[8,80,384]{2,1,0:T(8,128)(2,1)}, u32[]{:S(2)}, u32[]{:S(2)}) collective-permute-start(bf16[8,80,384]{2,1,0:T(8,128)(2,1)S(1)} %bitcast.181), channel_id=1, source_target_pairs={{0,128},{128,0},{1,129},{129,1},{2,130},{130,2},{3,131},{131,3},{4... | collective-permute-start | bytes 1474568 | tf_op jit(solution)/shard_map/ppermute | solution.py:29
  78.0 19.6 %collective-permute-start.10 = (bf16[2,80,1536]{2,1,0:T(8,128)(2,1)}, bf16[2,80,1536]{2,1,0:T(8,128)(2,1)}, u32[]{:S(2)}, u32[]{:S(2)}) collective-permute-start(bf16[2,80,1536]{2,1,0:T(8,128)(2,1)} %get-tuple-element.78), channel_id=1, source_target_pairs={{0,112},{16,0},{32,16},{48,32},{64,48},{80,64},{96,80},{112,96},{1... | collective-permute-start | bytes 1474568 | tf_op jit(solution)/shard_map/ppermute | solution.py:25
  81.3 19.5 %collective-permute-start.11 = (bf16[2,80,1536]{2,1,0:T(8,128)(2,1)}, bf16[2,80,1536]{2,1,0:T(8,128)(2,1)}, u32[]{:S(2)}, u32[]{:S(2)}) collective-permute-start(bf16[2,80,1536]{2,1,0:T(8,128)(2,1)} %get-tuple-element.79), channel_id=1, source_target_pairs={{0,16},{16,32},{32,48},{48,64},{64,80},{80,96},{96,112},{112,0},{1... | collective-permute-start | bytes 1474568 | tf_op jit(solution)/shard_map/ppermute | solution.py:25
  81.3 19.5 %collective-permute-start.12 = (bf16[8,80,384]{2,1,0:T(8,128)(2,1)}, bf16[8,80,384]{2,1,0:T(8,128)(2,1)}, u32[]{:S(2)}, u32[]{:S(2)}) collective-permute-start(bf16[8,80,384]{2,1,0:T(8,128)(2,1)} %bitcast.17), channel_id=1, source_target_pairs={{0,128},{128,0},{1,129},{129,1},{2,130},{130,2},{3,131},{131,3},{4... | collective-permute-start | bytes 1474568 | tf_op jit(solution)/shard_map/ppermute | solution.py:29
  103.0 11.3 %collective-permute-start.13 = (bf16[2,80,1536]{2,1,0:T(8,128)(2,1)}, bf16[2,80,1536]{2,1,0:T(8,128)(2,1)}, u32[]{:S(2)}, u32[]{:S(2)}) collective-permute-start(bf16[2,80,1536]{2,1,0:T(8,128)(2,1)} %fusion.1), channel_id=1, source_target_pairs={{0,112},{16,0},{32,16},{48,32},{64,48},{80,64},{96,80},{112,96},{1... | collective-permute-start | bytes 1474568 | tf_op jit(solution)/shard_map/ppermute | solution.py:25
  103.6 12.0 %collective-permute-start.14 = (bf16[8,80,384]{2,1,0:T(8,128)(2,1)S(1)}, bf16[8,80,384]{2,1,0:T(8,128)(2,1)}, u32[]{:S(2)}, u32[]{:S(2)}) collective-permute-start(bf16[8,80,384]{2,1,0:T(8,128)(2,1)S(1)} %bitcast.180), channel_id=1, source_target_pairs={{0,128},{128,0},{1,129},{129,1},{2,130},{130,2},{3,131},{131,3},{4... | collective-permute-start | bytes 1474568 | tf_op jit(solution)/shard_map/ppermute | solution.py:29
  104.4 21.2 %copy-start.9 = (bf16[128,768]{1,0:T(8,128)(2,1)S(1)}, bf16[128,768]{1,0:T(8,128)(2,1)}, u32[]{:S(2)}) copy-start(bf16[128,768]{1,0:T(8,128)(2,1)} %refs_1_.1) | copy-start | bytes 589828
  104.4 21.2 %copy-start.10 = (s32[128]{0:T(128)S(1)}, s32[128]{0:T(128)}, u32[]{:S(2)}) copy-start(s32[128]{0:T(128)} %param.9) | copy-start | bytes 1540
  115.6 10.0 %collective-permute-start.17 = (bf16[16,144,256]{2,1,0:T(8,128)(2,1)}, bf16[16,144,256]{2,1,0:T(8,128)(2,1)}, u32[]{:S(2)}, u32[]{:S(2)}) collective-permute-start(bf16[16,144,256]{2,1,0:T(8,128)(2,1)} %bitcast.178), channel_id=1, source_target_pairs={{0,8},{8,0},{1,9},{9,1},{2,10},{10,2},{3,11},{11,3},{4,12},{12,4},... | collective-permute-start | bytes 3538952 | tf_op jit(solution)/shard_map/ppermute | solution.py:29
  119.8 31.0 %copy-start.15 = (f32[16,2]{0,1:T(2,128)S(1)}, f32[16,2]{0,1:T(2,128)}, u32[]{:S(2)}) copy-start(f32[16,2]{0,1:T(2,128)} %param.13) | copy-start | bytes 388
  122.4 13.9 %collective-permute-start.15 = (bf16[80,1536]{1,0:T(8,128)(2,1)}, bf16[80,1536]{1,0:T(8,128)(2,1)}, u32[]{:S(2)}, u32[]{:S(2)}) collective-permute-start(bf16[80,1536]{1,0:T(8,128)(2,1)} %get-tuple-element.91), channel_id=1, source_target_pairs={{0,112},{16,0},{32,16},{48,32},{64,48},{80,64},{96,80},{112,96},{1... | collective-permute-start | bytes 737288 | tf_op jit(solution)/shard_map/ppermute | solution.py:25
  122.7 13.6 %collective-permute-start.16 = (bf16[80,1536]{1,0:T(8,128)(2,1)}, bf16[80,1536]{1,0:T(8,128)(2,1)}, u32[]{:S(2)}, u32[]{:S(2)}) collective-permute-start(bf16[80,1536]{1,0:T(8,128)(2,1)} %get-tuple-element.92), channel_id=1, source_target_pairs={{0,16},{16,32},{32,48},{48,64},{64,80},{80,96},{96,112},{112,0},{1... | collective-permute-start | bytes 737288 | tf_op jit(solution)/shard_map/ppermute | solution.py:25
  124.9 32.5 %collective-permute-start.20 = (bf16[80,1536]{1,0:T(8,128)(2,1)}, bf16[80,1536]{1,0:T(8,128)(2,1)}, u32[]{:S(2)}, u32[]{:S(2)}) collective-permute-start(bf16[80,1536]{1,0:T(8,128)(2,1)} %dynamic-slice_bitcast_fusion.2), channel_id=1, source_target_pairs={{0,128},{128,0},{1,129},{129,1},{2,130},{130,2},{3,131},{131,3},{4... | collective-permute-start | bytes 737288 | tf_op jit(solution)/shard_map/ppermute | solution.py:29
  136.3 26.5 %copy-start.12 = (bf16[2,80,1536]{2,1,0:T(8,128)(2,1)S(1)}, bf16[2,80,1536]{2,1,0:T(8,128)(2,1)}, u32[]{:S(2)}) copy-start(bf16[2,80,1536]{2,1,0:T(8,128)(2,1)} %copy-done.11) | copy-start | bytes 1474564
  138.6 18.9 %collective-permute-start.18 = (bf16[80,1536]{1,0:T(8,128)(2,1)}, bf16[80,1536]{1,0:T(8,128)(2,1)S(1)}, u32[]{:S(2)}, u32[]{:S(2)}) collective-permute-start(bf16[80,1536]{1,0:T(8,128)(2,1)} %get-tuple-element.111), channel_id=1, source_target_pairs={{0,112},{16,0},{32,16},{48,32},{64,48},{80,64},{96,80},{112,96},{1... | collective-permute-start | bytes 737288 | tf_op jit(solution)/shard_map/ppermute | solution.py:25
  145.9 11.5 %collective-permute-start.19 = (bf16[80,1536]{1,0:T(8,128)(2,1)S(1)}, bf16[80,1536]{1,0:T(8,128)(2,1)}, u32[]{:S(2)}, u32[]{:S(2)}) collective-permute-start(bf16[80,1536]{1,0:T(8,128)(2,1)S(1)} %get-tuple-element.110), channel_id=1, source_target_pairs={{0,16},{16,32},{32,48},{48,64},{64,80},{80,96},{96,112},{112,0},{1... | collective-permute-start | bytes 737288 | tf_op jit(solution)/shard_map/ppermute | solution.py:25
  145.9 11.5 %all-to-all-start = ((bf16[8,16,768]{2,1,0:T(8,128)(2,1)}), bf16[8,16,768]{2,1,0:T(8,128)(2,1)S(1)}, u32[]{:S(2)}, u32[]{:S(2)}) async-start(bf16[8,16,768]{2,1,0:T(8,128)(2,1)} %bitcast.184), calls=%async_computation | async-start | bytes 393216 | tf_op jit(solution)/shard_map/all_to_all | solution.py:260
  159.5 8.7 %collective-permute-start.21 = (bf16[80,1536]{1,0:T(8,128)(2,1)}, bf16[80,1536]{1,0:T(8,128)(2,1)}, u32[]{:S(2)}, u32[]{:S(2)}) collective-permute-start(bf16[80,1536]{1,0:T(8,128)(2,1)} %get-tuple-element.109), channel_id=1, source_target_pairs={{0,112},{16,0},{32,16},{48,32},{64,48},{80,64},{96,80},{112,96},{1... | collective-permute-start | bytes 737288 | tf_op jit(solution)/shard_map/ppermute | solution.py:25
  162.8 7.4 %collective-permute-start.22 = (bf16[80,1536]{1,0:T(8,128)(2,1)S(1)}, bf16[80,1536]{1,0:T(8,128)(2,1)S(1)}, u32[]{:S(2)}, u32[]{:S(2)}) collective-permute-start(bf16[80,1536]{1,0:T(8,128)(2,1)S(1)} %get-tuple-element.108), channel_id=1, source_target_pairs={{0,16},{16,32},{32,48},{48,64},{64,80},{80,96},{96,112},{112,0},{1... | collective-permute-start | bytes 737288 | tf_op jit(solution)/shard_map/ppermute | solution.py:25
  164.6 13.0 %all-to-all-start.1 = ((bf16[16,5,1536]{2,1,0:T(8,128)(2,1)}), bf16[16,5,1536]{2,1,0:T(8,128)(2,1)S(1)}, u32[]{:S(2)}, u32[]{:S(2)}) async-start(bf16[16,5,1536]{2,1,0:T(8,128)(2,1)} %reshape.70), calls=%async_computation.1 | async-start | bytes 786432 | tf_op jit(solution)/shard_map/all_to_all | solution.py:276
  172.0 7.3 %collective-permute-start.23 = (bf16[80,1536]{1,0:T(8,128)(2,1)}, bf16[80,1536]{1,0:T(8,128)(2,1)S(1)}, u32[]{:S(2)}, u32[]{:S(2)}) collective-permute-start(bf16[80,1536]{1,0:T(8,128)(2,1)} %fusion.9), channel_id=1, source_target_pairs={{0,112},{16,0},{32,16},{48,32},{64,48},{80,64},{96,80},{112,96},{1... | collective-permute-start | bytes 737288 | tf_op jit(solution)/shard_map/ppermute | solution.py:25
  181.2 14.9 %all-to-all-start.2 = ((bf16[16,5,1536]{2,1,0:T(8,128)(2,1)}), bf16[16,5,1536]{2,1,0:T(8,128)(2,1)S(1)}, u32[]{:S(2)}, u32[]{:S(2)}) async-start(bf16[16,5,1536]{2,1,0:T(8,128)(2,1)} %reshape.72), calls=%async_computation.2 | async-start | bytes 786432 | tf_op jit(solution)/shard_map/all_to_all | solution.py:276
  (12 other events, 87.3 us)
Sparse Core Ops, SparseCore 0:
  62.7 39.4 all-gather.1

commit v2 on v1

--- a/solution.py
+++ b/solution.py
@@ -16,7 +16,7 @@
 EXPERTS = 8
 PAD = 16
 GROUPS = 2
-PIECES = 4
+ORDER = (4, 3, 5, 2, 6, 1, 7, 0)
 PRODUCT_VMEM = 16 * 1024 * 1024
 ATTENTION_VMEM = 24 * 1024 * 1024
 
@@ -132,34 +132,95 @@
     )(place, queries, doc_ids[None, :], near, far)
 
 
-def product_kernel(place, a_ref, b_ref, wa_ref, wb_ref, o_ref):
-    depth = a_ref.shape[-1]
-    out = jnp.dot(a_ref[...].reshape(-1, depth), wa_ref[...], preferred_element_type=jnp.float32)
-    out += jnp.dot(b_ref[...].reshape(-1, depth), wb_ref[...], preferred_element_type=jnp.float32)
-    o_ref[...] = out.astype(o_ref.dtype).reshape(o_ref.shape)
-
-
-def product(place, acts, acts_other, weight, other, first, tile, tiles, block, steps, pick):
+def slice_kernel(place, weight_ref, *refs):
+    outs, sems = refs[:-1], refs[-1]
+    columns, strip = outs[0].shape[1], outs[0].shape[0] // 2
+    copies = []
+    for i, out in enumerate(outs):
+        at = pl.multiple_of(((1 - place[2]) * len(outs) + i) * columns, columns)
+        for k in range(2):
+            rows = pl.ds(k * strip, strip)
+            copies.append(
+                pltpu.make_async_copy(weight_ref.at[rows, pl.ds(at, columns)], out.at[rows, :], sems.at[2 * i + k])
+            )
+    for copy in copies:
+        copy.start()
+    for copy in copies:
+        copy.wait()
+
+
+def other_columns(place, weight, columns):
+    any_spec = pl.BlockSpec(memory_space=pl.ANY)
+    return pl.pallas_call(
+        slice_kernel,
+        out_shape=[jax.ShapeDtypeStruct((weight.shape[0], columns), weight.dtype)] * GROUPS,
+        in_specs=[pl.BlockSpec(memory_space=pltpu.SMEM), any_spec],
+        out_specs=[any_spec] * GROUPS,
+        scratch_shapes=[pltpu.SemaphoreType.DMA((2 * GROUPS,))],
+        name="columns",
+    )(place, weight)
+
+
+def product_kernel(count, offsets, place, *refs):
+    depth = refs[0].shape[-1]
+    wa_ref, wb_ref = refs[2 * count : 2 * count + 2]
+    a = jnp.concatenate([ref[...].reshape(-1, depth) for ref in refs[:count]], axis=0)
+    b = jnp.concatenate([ref[...].reshape(-1, depth) for ref in refs[count : 2 * count]], axis=0)
+    out = jnp.dot(a, wa_ref[...], preferred_element_type=jnp.float32)
+    out += jnp.dot(b, wb_ref[...], preferred_element_type=jnp.float32)
+    out = out.astype(jnp.bfloat16)
+    if offsets is None:
+        o_refs = refs[2 * count + 2 :]
+        rows = out.shape[0] // len(o_refs)
+        for i, o_ref in enumerate(o_refs):
+            o_ref[...] = out[i * rows : (i + 1) * rows].reshape(o_ref.shape)
+    else:
+        o_refs, chunks = refs[2 * count + 2 : -1], refs[-1]
+        chunks[...] = out.reshape(chunks.shape)
+        for o_ref, picks in zip(o_refs, offsets):
+            for k, offset in enumerate(picks):
+                o_ref[k] = chunks[lax.rem(place[1] + offset, Z)].reshape(o_ref.shape[1:])
+
+
+def product(place, acts, acts_other, weight, other, first, block, picks, steps, offsets, split):
     depth, rows = acts.shape[-1], acts.shape[2]
-    half, start = weight.shape[1] // (2 * tile), first % (other.shape[1] // tile)
-    acts_spec = pl.BlockSpec(block + (rows, depth), lambda j, i, s: pick(i, s) + (0, 0))
+    columns = other.shape[1]
+    tile = columns // 2
+    half, start = weight.shape[1] // (2 * tile), first * 2
+    specs = [pl.BlockSpec(block + (rows, depth), lambda j, i, s, pick=pick: pick(i, s) + (0, 0)) for pick in picks]
+    if offsets is None:
+        shapes, blocks = [block + (rows, columns)] * len(picks), [block + (rows, tile)] * len(picks)
+        scratch = []
+    else:
+        split = (steps,) if split else ()
+        shapes = [(len(o),) + split + (rows, columns) for o in offsets]
+        blocks = [(len(o),) + (1,) * len(split) + (rows, tile) for o in offsets]
+        scratch = [pltpu.VMEM(block[1:] + (rows, tile), jnp.bfloat16)]
+
+    def out_map(rank):
+        if rank == 3:
+            return lambda j, i, s: (0, 0, j)
+        return lambda j, i, s: (0, i, 0, j)
+
+    weight = pltpu.with_memory_space_constraint(weight, pltpu.HBM)
     return pl.pallas_call(
-        product_kernel,
-        out_shape=jax.ShapeDtypeStruct((steps * block[0], block[1], rows, tiles * tile), jnp.bfloat16),
+        lambda *refs: product_kernel(len(picks), offsets, *refs),
+        out_shape=[jax.ShapeDtypeStruct(shape, jnp.bfloat16) for shape in shapes],
         grid_spec=pltpu.PrefetchScalarGridSpec(
             num_scalar_prefetch=1,
-            grid=(tiles, steps),
-            in_specs=[
-                acts_spec,
-                acts_spec,
-                pl.BlockSpec((depth, tile), lambda j, i, s: (0, s[2] * half + first + j)),
-                pl.BlockSpec((depth, tile), lambda j, i, s: (0, start + j)),
+            grid=(2, steps),
+            in_specs=specs
+            + specs
+            + [
+                pl.BlockSpec((depth, tile), lambda j, i, s: (0, s[2] * half + start + j)),
+                pl.BlockSpec((depth, tile), lambda j, i, s: (0, j)),
             ],
-            out_specs=pl.BlockSpec(block + (rows, tile), lambda j, i, s: (i, 0, 0, j)),
+            out_specs=[pl.BlockSpec(b, out_map(len(b))) for b in blocks],
+            scratch_shapes=scratch,
         ),
         compiler_params=pltpu.CompilerParams(vmem_limit_bytes=PRODUCT_VMEM),
         name="product",
-    )(place, acts, acts_other, weight, other)
+    )(place, *([acts] * len(picks)), *([acts_other] * len(picks)), weight, other)
 
 
 def add(*terms):
@@ -171,10 +232,6 @@
 
 def join(*values):
     return lax.optimization_barrier(values)
-
-
-def chunk(array, at, axis):
-    return lax.dynamic_index_in_dim(array, at % Z, axis, keepdims=False)
 
 
 def shards(queries, keys_values, doc_ids, gate_up, down_weight, routes, route_weights):
@@ -186,87 +243,70 @@
     acts = gate_up[0].reshape(2, Z, -1, depth)
 
     acts_other = swap(gate_up[0], "c")
-    part = lax.dynamic_slice(weight, (0, (1 - core) * GROUPS * columns), (depth, columns))
-    other = [swap(part, "c")]
-    block = key_block(keys_values, doc_ids)
+    parts = other_columns(place, weight, columns)
+    other = [swap(part, "c") for part in parts]
+    block = key_block(keys_values, after(doc_ids, *parts))
     block_other = swap(block, "yh")
-    at = after(((1 - core) * GROUPS + 1) * columns, part, block)
-    other.append(swap(lax.dynamic_slice(weight, (0, at), (depth, columns)), "c"))
     acts_other, other[0], block_other = join(acts_other, other[0], block_other)
     acts_other = acts_other.reshape(2, Z, -1, depth)
     near = lax.all_gather(jnp.concatenate([block, block_other], axis=0), "z", axis=0, tiled=True)
 
-    def first_group(where, block, steps, pick):
-        return product(where, acts, acts_other, weight, other[0], 0, columns // 2, 2, block, steps, pick)
-
-    def second_group(where, piece, pieces, pick):
-        tile = columns // PIECES
-        return product(
-            where, acts, acts_other, weight, other[1], PIECES + piece, tile, pieces, (1, Z), 1, pick
-        )[0]
-
-    def sent_piece(where, piece):
-        return second_group(where, piece, 1, lambda i, s: (1 - s[0], 0))
-
-    down = first_group(place, (2, 1), 1, lambda i, s: (0, (s[1] + 4) % Z))[:, 0]
-    up = first_group(after(place, down), (2, 1), 1, lambda i, s: (0, (s[1] + 3) % Z))[:, 0]
-    sent = sent_piece(after(place, up), 0)
-    down, up, sent = join(down, up, sent)
+    def make(where, group, block, picks, steps=1, offsets=None, split=False):
+        return product(where, acts, acts_other, weight, other[group], group, block, picks, steps, offsets, split)
+
+    down, up = make(
+        place, 0, (2, 1), [lambda i, s: (0, lax.rem(s[1] + 4, Z)), lambda i, s: (0, lax.rem(s[1] + 3, Z))]
+    )
+    down, up = down[:, 0], up[:, 0]
+    sent = make(after(place, down), 1, (1, Z), [lambda i, s: (1 - s[0], 0)], 1, [ORDER[k : k + 2] for k in (0, 2, 4, 6)])
     got = []
 
-    down, up, piece = shift(down, -1), shift(up, 1), swap(sent, "yh")
-    full = first_group(after(place, sent), (1, Z), 2, lambda i, s: (i, 0))
-    sent = sent_piece(after(place, full), 1)
-    down, up, piece, full, sent = join(down, up, piece, full, sent)
+    down, up, piece = shift(down, -1), shift(up, 1), swap(sent[0], "yh")
+    (full,) = make(after(place, sent[0]), 0, (1, Z), [lambda i, s: (i, 0)], 2, [ORDER], True)
+    down, up, piece, full = join(down, up, piece, full)
     got.append(piece)
-    down = add(down, chunk(full, along + 5, 1))
-    up = add(up, chunk(full, along + 2, 1))
-    down, up, sent = join(down, up, sent)
-
-    here = after(place, down)
-    down, up, piece = shift(down, -1), shift(up, 1), swap(sent, "yh")
-    sent = sent_piece(here, 2)
-    kept = second_group(after(place, sent), 0, PIECES, lambda i, s: (s[0], 0))
-    down, up, piece, kept, sent = join(down, up, piece, kept, sent)
+    down, up = add(down, full[2]), add(up, full[3])
+    down, up, going = join(down, up, sent[1])
+
+    here, near = after(place, down), after(near, down)
+    down, up, piece = shift(down, -1), shift(up, 1), swap(going, "yh")
+    (kept,) = make(here, 1, (1, Z), [lambda i, s: (s[0], 0)], 1, [ORDER])
+    down, up, piece, kept = join(down, up, piece, kept)
     got.append(piece)
-    down = add(down, chunk(full, along + 6, 1))
-    up = add(up, chunk(full, along + 1, 1))
-    down, up, sent = join(down, up, sent)
-
-    here = after(place, down)
-    down, up, piece = shift(down, -1), shift(up, 1), swap(sent, "yh")
-    sent = sent_piece(here, 3)
-    down, up, piece, sent = join(down, up, piece, sent)
+    down, up = add(down, full[4]), add(up, full[5])
+    down, up, going = join(down, up, sent[2])
+
+    near = after(near, down).reshape(2 * Z, -1, near.shape[-1])
+    down, up, piece = shift(down, -1), shift(up, 1), swap(going, "yh")
+    context = attend(place, queries, doc_ids, near, swap(near, "c"))
+    down, up, piece, context = join(down, up, piece, context)
     got.append(piece)
-    down = add(down, chunk(full, along + 7, 1))
-    down, sent = join(down, sent)
-
-    down, piece = shift(down, -1), swap(sent, "yh")
-    down, piece, near = join(down, piece, near)
+    down = add(down, full[6])
+    down, going, context = join(down, sent[3], context)
+
+    residual = lax.all_to_all(context, EXP, split_axis=0, concat_axis=1, tiled=True)
+    down, piece = shift(down, -1), swap(going, "yh")
+    down, piece = join(down, piece)
     got.append(piece)
-    first = add(down, up, chunk(full, along, 1))
-
-    def second_term(offset):
-        received = jnp.concatenate([chunk(piece, along + offset, 0) for piece in got], axis=1)
-        return chunk(kept, along + offset, 0), received
+    first = add(down, up, full[7])
+
+    def second_term(order):
+        return kept[order], got[order // 2][order % 2]
 
     going = chunk_of(first, 1 - high)
-    down, up = add(*second_term(4)), add(*second_term(3))
+    down, up = add(*second_term(0)), add(*second_term(1))
     down, up, going = join(down, up, going)
     down, up, moved = shift(down, -1), shift(up, 1), swap(going, "yh")
-    near = near.reshape(2 * Z, -1, near.shape[-1])
-    context = attend(place, queries, doc_ids, near, swap(near, "c"))
-    down, up, context = join(down, up, context)
-    residual = lax.all_to_all(context, EXP, split_axis=0, concat_axis=1, tiled=True)
-    down, up = add(down, *second_term(5)), add(up, *second_term(2))
+    down, up = join(down, up)
+    down, up = add(down, *second_term(2)), add(up, *second_term(3))
     down, up = shift(down, -1), shift(up, 1)
     down, up, moved = join(down, up, moved)
     first = add(chunk_of(first, high), moved)
-    down, up = add(down, *second_term(6)), add(up, *second_term(1))
+    down, up = add(down, *second_term(4)), add(up, *second_term(5))
     down, up = shift(down, -1), shift(up, 1)
-    down, up, residual = join(down, up, residual)
-    down = add(down, *second_term(7))
-    second = add(shift(down, -1), up, *second_term(0))
+    down, up = join(down, up)
+    down = add(down, *second_term(6))
+    second = add(shift(down, -1), up, *second_term(7))
 
     tokens = routes.shape[0]
     capacity = first.shape[0] // (2 * EXPERTS)
@@ -276,6 +316,8 @@
         home = lax.all_to_all(
             rows.reshape(2 * EXPERTS, capacity, -1), ("c",) + EXP, split_axis=0, concat_axis=0, tiled=True
         )
+        if rows is first:
+            home = after(home, second)
         home = home.reshape(2, EXPERTS * capacity, -1)
         both = jnp.einsum("tr,crn->tcn", mix, home, preferred_element_type=jnp.float32)
         mixed.append(both[:tokens] + both[tokens:])

time: 206 us -> 274 us (1.33)
  Pallas kernels: 41.1 us -> 127 us
  local copies, waits for them, and re-layouts: 28.5 us -> 7.58 us
  waiting for transfers between devices: 49.2 us -> 66.6 us
  starting transfers between devices: 48.4 us -> 41.5 us
  other arithmetic: 22.1 us -> 16.1 us
    pallas_call x8 -> x5, Pallas kernels: 30.5 us -> 117 us  [the longest x1 97.2 us: other_columns(): pl.pallas_call(slice_kernel, out_shape=[jax.ShapeDtypeStruct((weight.shap...]
    ppermute x14, waiting for transfers between devices: 23.2 us -> 37.9 us  [shift(): return lax.ppermute(value, 'z', [(i, (i + step) % Z) for i in range(Z)])]
    unnamed x33 -> x39, local copies, waits for them, and re-layouts: 13.4 us -> 5.28 us
    dynamic_slice x2 -> x0, local copies, waits for them, and re-layouts: 6.25 us -> none  [the longest x1 3.49 us: shards(): lax.dynamic_slice(weight, (0, at), (depth, columns))]
    squeeze x3 -> x0, local copies, waits for them, and re-layouts: 5.89 us -> none  [chunk(): return lax.dynamic_index_in_dim(array, at % Z, axis, keepdims=False)]
    convert_element_type x10, other arithmetic: 18.8 us -> 13.7 us  [add(): return total.astype(jnp.bfloat16)]
    ppermute x14, starting transfers between devices: 26.6 us -> 22 us  [shift(): return lax.ppermute(value, 'z', [(i, (i + step) % Z) for i in range(Z)])]
    all_to_all x1, waiting for transfers between devices: 6.58 us -> 2.13 us  [shards(): lax.all_to_all(context, EXP, split_axis=0, concat_axis=1, tiled=True)]
  transfers between devices with their start and end apart: 28 -> 28, of which waited for: 12 -> 20; matrix products, arithmetic and copies ran while one was open for 14% -> 5% of each run, Pallas kernels for 19% -> 11%
where the time goes in v2:
time: 274 us
  Pallas kernels  127 us (46%)
  waiting for transfers between devices  66.6 us (24%)
  starting transfers between devices  41.5 us (15%)
  other arithmetic  16.1 us (6%)
  between operations  14.3 us (5%)
  local copies, waits for them, and re-layouts  7.58 us (3%)
    pallas_call x1, Pallas kernels, other_columns(): pl.pallas_call(slice_kernel, out_shape=[jax.ShapeDtypeStruct((weight.shap...  97.2 us
    ppermute x14, waiting for transfers between devices, shift(): return lax.ppermute(value, 'z', [(i, (i + step) % Z) for i in range(Z)])  37.9 us
    ppermute x14, starting transfers between devices, shift(): return lax.ppermute(value, 'z', [(i, (i + step) % Z) for i in range(Z)])  22 us
    pallas_call x4, Pallas kernels, product(): pl.pallas_call(lambda *refs: product_kernel(len(picks), offsets, *refs),...  20.2 us
    all_to_all x2, waiting for transfers between devices, shards(): lax.all_to_all(rows.reshape(2 * EXPERTS, capacity, -1), ('c',) + EXP, spl...  16.5 us
    convert_element_type x10, other arithmetic, add(): return total.astype(jnp.bfloat16)  13.7 us
    ppermute x10, waiting for transfers between devices, swap(): return lax.ppermute(value, axis, [(0, 1), (1, 0)])  9.94 us
    pallas_call x1, Pallas kernels, attend(): pl.pallas_call(lambda *refs: attention_kernel(head, *refs), out_shape=jax...  9.66 us
  transfers between devices with their start and end apart: 28, of which 20 were waited for; matrix products, arithmetic and copies ran while one was open for 5% of the time, Pallas kernels for 11%

profile of v2, /device:TPU:16, one launch (start us, length us, event | category | flops | bytes accessed | tf_op | source)
XLA Modules:
  0.0 273.6 jit_solution(17643199929632370734)
XLA Ops:
  7.8 97.2 %columns.1 = (bf16[512,1536]{1,0:T(8,128)(2,1)}, bf16[512,1536]{1,0:T(8,128)(2,1)}) custom-call(s32[3]{0:T(128)} %pad_add_fusion.place.refs_0_, bf16[512,6144]{1,0:T(8,128)(2,1)} %bitcast.108), custom_call_target="tpu_custom_call" | custom-call | tf_op jit(solution)/shard_map/columns/pallas_call | solution.py:154
  105.8 2.2 collective-permute-start.2
  108.0 4.0 %collective-permute-done.2 = bf16[144,1,256]{2,0,1:T(8,128)(2,1)S(1)} collective-permute-done((bf16[144,1,256]{2,0,1:T(8,128)(2,1)S(1)}, bf16[144,1,256]{2,0,1:T(8,128)(2,1)S(1)}, u32[]{:S(2)}, u32[]{:S(2)}) %collective-permute-start.2) | collective-permute-done | bytes 73760 | tf_op jit(solution)/shard_map/ppermute | solution.py:29
  115.9 3.2 %product.4 = (bf16[2,1,80,1536]{3,2,1,0:T(8,128)(2,1)S(1)}, bf16[2,1,80,1536]{3,2,1,0:T(8,128)(2,1)S(1)}) custom-call(s32[3]{0:T(128)S(1)} %copy-done.9, bf16[2,8,80,512]{3,2,1,0:T(8,128)(2,1)S(1)} %bitcast.93, bf16[2,8,80,512]{3,2,1,0:T(8,128)(2,1)S(1)} %bitcast.94, bf16[2,8,80,512]{3,2,1,0:T(8,128)(2,1)S(1)} %bitcast.98, ...), custom_call_target="tpu_custom_call" | custom-call | tf_op jit(solution)/shard_map/product/pallas_call | solution.py:206
  119.1 5.9 %collective-permute-start.3 = (bf16[2,80,1536]{2,1,0:T(8,128)(2,1)S(1)}, bf16[2,80,1536]{2,1,0:T(8,128)(2,1)S(1)}, u32[]{:S(2)}, u32[]{:S(2)}) collective-permute-start(bf16[2,80,1536]{2,1,0:T(8,128)(2,1)S(1)} %bitcast.107), channel_id=1, source_target_pairs={{0,112},{16,0},{32,16},{48,32},{64,48},{80,64},{96,80},{112,96},{1... | collective-permute-start | bytes 1474568 | tf_op jit(solution)/shard_map/ppermute | solution.py:25
  125.1 5.3 %product.5 = (bf16[2,80,1536]{2,1,0:T(8,128)(2,1)S(1)}, bf16[2,80,1536]{2,1,0:T(8,128)(2,1)S(1)}, bf16[2,80,1536]{2,1,0:T(8,128)(2,1)}, bf16[2,80,1536]{2,1,0:T(8,128)(2,1)S(1)}) custom-call(s32[3]{0:T(128)S(1)} %copy-done.9, bf16[2,8,80,512]{3,2,1,0:T(8,128)(2,1)S(1)} %bitcast.95, bf16[2,8,80,512]{3,2,1,0:T(8,128)(2,1)S(1)} %bitcast.100, ...), custom_call_target="tpu_custom_call" | custom-call | tf_op jit(solution)/shard_map/product/pallas_call | solution.py:206
  130.7 7.1 %product.6 = bf16[8,2,80,1536]{3,2,1,0:T(8,128)(2,1)S(1)} custom-call(s32[3]{0:T(128)S(1)} %copy-done.9, bf16[2,8,80,512]{3,2,1,0:T(8,128)(2,1)S(1)} %bitcast.96, bf16[2,8,80,512]{3,2,1,0:T(8,128)(2,1)S(1)} %bitcast.101, bf16[512,6144]{1,0:T(8,128)(2,1)} %bitcast.111, bf16[512,1536]{1,0:T(8,128)(2,1)S(1)} %copy-done.6), custom_call_target="tpu_custom_call" | custom-call | tf_op jit(solution)/shard_map/product/pallas_call | solution.py:206
  137.9 2.4 collective-permute-done.3
  140.2 4.6 %collective-permute-done.4 = bf16[2,80,1536]{2,1,0:T(8,128)(2,1)S(1)} collective-permute-done((bf16[2,80,1536]{2,1,0:T(8,128)(2,1)S(1)}, bf16[2,80,1536]{2,1,0:T(8,128)(2,1)S(1)}, u32[]{:S(2)}, u32[]{:S(2)}) %collective-permute-start.4) | collective-permute-done | bytes 491552 | tf_op jit(solution)/shard_map/ppermute | solution.py:25
  145.2 3.0 %collective-permute-start.7 = (bf16[2,80,1536]{2,1,0:T(8,128)(2,1)S(1)}, bf16[2,80,1536]{2,1,0:T(8,128)(2,1)S(1)}, u32[]{:S(2)}, u32[]{:S(2)}) collective-permute-start(bf16[2,80,1536]{2,1,0:T(8,128)(2,1)S(1)} %get-tuple-element.67), channel_id=1, source_target_pairs={{0,112},{16,0},{32,16},{48,32},{64,48},{80,64},{96,80},{112,96},{1... | collective-permute-start | bytes 1474568 | tf_op jit(solution)/shard_map/ppermute | solution.py:25
  148.6 4.6 %product.7 = bf16[8,80,1536]{2,1,0:T(8,128)(2,1)S(1)} custom-call(s32[3]{0:T(128)S(1)} %copy-done.9, bf16[2,8,80,512]{3,2,1,0:T(8,128)(2,1)S(1)} %bitcast.97, bf16[2,8,80,512]{3,2,1,0:T(8,128)(2,1)S(1)} %bitcast.102, bf16[512,6144]{1,0:T(8,128)(2,1)} %bitcast.112, bf16[512,1536]{1,0:T(8,128)(2,1)} %collective-permute-done.5.refs_4_), custom_call_target="tpu_custom_call" | custom-call | tf_op jit(solution)/shard_map/product/pallas_call | solution.py:206
  154.5 7.1 %collective-permute-done.7 = bf16[2,80,1536]{2,1,0:T(8,128)(2,1)S(1)} collective-permute-done((bf16[2,80,1536]{2,1,0:T(8,128)(2,1)S(1)}, bf16[2,80,1536]{2,1,0:T(8,128)(2,1)S(1)}, u32[]{:S(2)}, u32[]{:S(2)}) %collective-permute-start.7) | collective-permute-done | bytes 491552 | tf_op jit(solution)/shard_map/ppermute | solution.py:25
  161.6 2.0 collective-permute-done.8
  169.2 9.7 %attention.1 = bf16[128,768]{1,0:T(8,128)(2,1)} custom-call(s32[3]{0:T(128)S(1)} %copy-done.9, bf16[128,768]{1,0:T(8,128)(2,1)S(1)} %copy-done.8, s32[1,128]{1,0:T(1,128)S(1)} %bitcast.105, bf16[16,144,256]{2,1,0:T(8,128)(2,1)S(1)} %bitcast.104, bf16[16,144,256]{2,1,0:T(8,128)(2,1)S(1)} %collective-permute-done.13.refs_4_), custom_call_target="tpu_custom_call" | custom-call | tf_op jit(solution)/shard_map/attention/pallas_call | solution.py:118
  178.8 2.0 collective-permute-done.11
  183.0 4.7 %collective-permute-start.14 = (bf16[2,80,1536]{2,1,0:T(8,128)(2,1)S(1)}, bf16[2,80,1536]{2,1,0:T(8,128)(2,1)}, u32[]{:S(2)}, u32[]{:S(2)}) collective-permute-start(bf16[2,80,1536]{2,1,0:T(8,128)(2,1)S(1)} %fusion.1), channel_id=1, source_target_pairs={{0,112},{16,0},{32,16},{48,32},{64,48},{80,64},{96,80},{112,96},{1... | collective-permute-start | bytes 1474568 | tf_op jit(solution)/shard_map/ppermute | solution.py:25
  187.7 1.9 fusion.14
  189.7 8.9 %collective-permute-done.14 = bf16[2,80,1536]{2,1,0:T(8,128)(2,1)} collective-permute-done((bf16[2,80,1536]{2,1,0:T(8,128)(2,1)S(1)}, bf16[2,80,1536]{2,1,0:T(8,128)(2,1)}, u32[]{:S(2)}, u32[]{:S(2)}) %collective-permute-start.14) | collective-permute-done | bytes 491552 | tf_op jit(solution)/shard_map/ppermute | solution.py:25
  198.5 3.8 %collective-permute-done.15 = bf16[2,80,1536]{2,1,0:T(8,128)(2,1)} collective-permute-done((bf16[2,80,1536]{2,1,0:T(8,128)(2,1)S(1)}, bf16[2,80,1536]{2,1,0:T(8,128)(2,1)}, u32[]{:S(2)}, u32[]{:S(2)}) %collective-permute-start.15) | collective-permute-done | bytes 491552 | tf_op jit(solution)/shard_map/ppermute | solution.py:29
  204.4 1.6 collective-permute-start.17
  206.8 4.4 %collective-permute-done.16 = bf16[80,1536]{1,0:T(8,128)(2,1)} collective-permute-done((bf16[80,1536]{1,0:T(8,128)(2,1)}, bf16[80,1536]{1,0:T(8,128)(2,1)}, u32[]{:S(2)}, u32[]{:S(2)}) %collective-permute-start.16) | collective-permute-done | bytes 245792 | tf_op jit(solution)/shard_map/ppermute | solution.py:25
  212.6 2.3 fusion.10
  217.0 5.8 %all-to-all-start = ((bf16[8,16,768]{2,1,0:T(8,128)(2,1)}), bf16[8,16,768]{2,1,0:T(8,128)(2,1)S(1)}, u32[]{:S(2)}, u32[]{:S(2)}) async-start(bf16[8,16,768]{2,1,0:T(8,128)(2,1)} %bitcast.18), calls=%async_computation | async-start | bytes 393216 | tf_op jit(solution)/shard_map/all_to_all | solution.py:287
  223.1 2.2 fusion.8
  227.3 2.1 all-to-all-done
  229.5 2.3 collective-permute-done.21
  231.8 2.6 collective-permute-done.22
  234.4 1.9 fusion.7
  237.3 5.8 %all-to-all-start.1 = ((bf16[16,5,1536]{2,1,0:T(8,128)(2,1)}), bf16[16,5,1536]{2,1,0:T(8,128)(2,1)S(1)}, u32[]{:S(2)}, u32[]{:S(2)}) async-start(bf16[16,5,1536]{2,1,0:T(8,128)(2,1)} %reshape.86), calls=%async_computation.1 | async-start | bytes 786432 | tf_op jit(solution)/shard_map/all_to_all | solution.py:316
  245.2 7.4 %all-to-all-done.1 = bf16[16,5,1536]{2,1,0:T(8,128)(2,1)S(1)} async-done(((bf16[16,5,1536]{2,1,0:T(8,128)(2,1)}), bf16[16,5,1536]{2,1,0:T(8,128)(2,1)S(1)}, u32[]{:S(2)}, u32[]{:S(2)}) %all-to-all-start.1) | async-done | bytes 245792 | tf_op jit(solution)/shard_map/all_to_all | solution.py:316
  252.6 3.6 %all-to-all-start.2 = ((bf16[16,5,1536]{2,1,0:T(8,128)(2,1)}), bf16[16,5,1536]{2,1,0:T(8,128)(2,1)S(1)}, u32[]{:S(2)}, u32[]{:S(2)}) async-start(bf16[16,5,1536]{2,1,0:T(8,128)(2,1)} %reshape.88), calls=%async_computation.2 | async-start | bytes 786432 | tf_op jit(solution)/shard_map/all_to_all | solution.py:316
  256.4 9.1 %all-to-all-done.2 = bf16[16,5,1536]{2,1,0:T(8,128)(2,1)S(1)} async-done(((bf16[16,5,1536]{2,1,0:T(8,128)(2,1)}), bf16[16,5,1536]{2,1,0:T(8,128)(2,1)S(1)}, u32[]{:S(2)}, u32[]{:S(2)}) %all-to-all-start.2) | async-done | bytes 245792 | tf_op jit(solution)/shard_map/all_to_all | solution.py:316
  (105 shorter events, 28.7 us)
Async XLA Ops:
  7.2 157.7 %all-gather.2.cloned.1.call-start = ((), (), s32[]{:S(2)}) async-start(), calls=%async_computation.3 | async-start | bytes 1327104 | tf_op jit(solution)/shard_map/all_gather | solution.py:252
  7.8 97.8 %copy-start = (bf16[1,1280,512]{2,1,0:T(8,128)(2,1)S(1)}, bf16[1,1280,512]{2,1,0:T(8,128)(2,1)}, u32[]{:S(2)}) copy-start(bf16[1,1280,512]{2,1,0:T(8,128)(2,1)} %param.10) | copy-start | bytes 3932164
  7.8 97.9 %copy-start.10 = (s32[128]{0:T(128)S(1)}, s32[128]{0:T(128)}, u32[]{:S(2)}) copy-start(s32[128]{0:T(128)} %param.9) | copy-start | bytes 1540
  7.8 98.0 %copy-start.14 = (bf16[128,1,256]{2,0,1:T(8,128)(2,1)S(1)}, bf16[128,1,256]{2,0,1:T(8,128)(2,1)}, u32[]{:S(2)}) copy-start(bf16[128,1,256]{2,0,1:T(8,128)(2,1)} %param.8) | copy-start | bytes 196612
  7.8 106.7 %copy-start.9 = (s32[3]{0:T(128)S(1)}, s32[3]{0:T(128)}, u32[]{:S(2)}) copy-start(s32[3]{0:T(128)} %pad_add_fusion.place.refs_0_) | copy-start | bytes 40
  105.1 7.6 %collective-permute-start.1 = (bf16[512,1536]{1,0:T(8,128)(2,1)}, bf16[512,1536]{1,0:T(8,128)(2,1)S(1)}, u32[]{:S(2)}, u32[]{:S(2)}) collective-permute-start(bf16[512,1536]{1,0:T(8,128)(2,1)} %get-tuple-element.53), channel_id=1, source_target_pairs={{0,8},{8,0},{1,9},{9,1},{2,10},{10,2},{3,11},{11,3},{4,12},{12,4},... | collective-permute-start | bytes 4718600 | tf_op jit(solution)/shard_map/ppermute | solution.py:29
  105.2 19.9 %collective-permute-start.5 = (bf16[512,1536]{1,0:T(8,128)(2,1)}, bf16[512,1536]{1,0:T(8,128)(2,1)}, u32[]{:S(2)}, u32[]{:S(2)}) collective-permute-start(bf16[512,1536]{1,0:T(8,128)(2,1)} %get-tuple-element.54), channel_id=1, source_target_pairs={{0,8},{8,0},{1,9},{9,1},{2,10},{10,2},{3,11},{11,3},{4,12},{12,4},... | collective-permute-start | bytes 4718600 | tf_op jit(solution)/shard_map/ppermute | solution.py:29
  105.7 7.0 %collective-permute-start = (bf16[1280,512]{1,0:T(8,128)(2,1)S(1)}, bf16[1280,512]{1,0:T(8,128)(2,1)S(1)}, u32[]{:S(2)}, u32[]{:S(2)}) collective-permute-start(bf16[1280,512]{1,0:T(8,128)(2,1)S(1)} %bitcast.92), channel_id=1, source_target_pairs={{0,8},{8,0},{1,9},{9,1},{2,10},{10,2},{3,11},{11,3},{4,12},{12,4},... | collective-permute-start | bytes 3932168 | tf_op jit(solution)/shard_map/ppermute | solution.py:29
  105.8 6.2 %collective-permute-start.2 = (bf16[144,1,256]{2,0,1:T(8,128)(2,1)S(1)}, bf16[144,1,256]{2,0,1:T(8,128)(2,1)S(1)}, u32[]{:S(2)}, u32[]{:S(2)}) collective-permute-start(bf16[144,1,256]{2,0,1:T(8,128)(2,1)S(1)} %pad_maximum_fusion.1), channel_id=1, source_target_pairs={{0,128},{128,0},{1,129},{129,1},{2,130},{130,2},{3,131},{131,3},{4... | collective-permute-start | bytes 221192 | tf_op jit(solution)/shard_map/ppermute | solution.py:29
  119.1 21.1 %collective-permute-start.3 = (bf16[2,80,1536]{2,1,0:T(8,128)(2,1)S(1)}, bf16[2,80,1536]{2,1,0:T(8,128)(2,1)S(1)}, u32[]{:S(2)}, u32[]{:S(2)}) collective-permute-start(bf16[2,80,1536]{2,1,0:T(8,128)(2,1)S(1)} %bitcast.107), channel_id=1, source_target_pairs={{0,112},{16,0},{32,16},{48,32},{64,48},{80,64},{96,80},{112,96},{1... | collective-permute-start | bytes 1474568 | tf_op jit(solution)/shard_map/ppermute | solution.py:25
  125.1 19.8 %collective-permute-start.4 = (bf16[2,80,1536]{2,1,0:T(8,128)(2,1)S(1)}, bf16[2,80,1536]{2,1,0:T(8,128)(2,1)S(1)}, u32[]{:S(2)}, u32[]{:S(2)}) collective-permute-start(bf16[2,80,1536]{2,1,0:T(8,128)(2,1)S(1)} %bitcast.106), channel_id=1, source_target_pairs={{0,16},{16,32},{32,48},{48,64},{64,80},{80,96},{96,112},{112,0},{1... | collective-permute-start | bytes 1474568 | tf_op jit(solution)/shard_map/ppermute | solution.py:25
  130.4 14.6 %collective-permute-start.6 = (bf16[2,80,1536]{2,1,0:T(8,128)(2,1)S(1)}, bf16[2,80,1536]{2,1,0:T(8,128)(2,1)}, u32[]{:S(2)}, u32[]{:S(2)}) collective-permute-start(bf16[2,80,1536]{2,1,0:T(8,128)(2,1)S(1)} %get-tuple-element.61), channel_id=1, source_target_pairs={{0,128},{128,0},{1,129},{129,1},{2,130},{130,2},{3,131},{131,3},{4... | collective-permute-start | bytes 1474568 | tf_op jit(solution)/shard_map/ppermute | solution.py:29
  145.2 16.4 %collective-permute-start.7 = (bf16[2,80,1536]{2,1,0:T(8,128)(2,1)S(1)}, bf16[2,80,1536]{2,1,0:T(8,128)(2,1)S(1)}, u32[]{:S(2)}, u32[]{:S(2)}) collective-permute-start(bf16[2,80,1536]{2,1,0:T(8,128)(2,1)S(1)} %get-tuple-element.67), channel_id=1, source_target_pairs={{0,112},{16,0},{32,16},{48,32},{64,48},{80,64},{96,80},{112,96},{1... | collective-permute-start | bytes 1474568 | tf_op jit(solution)/shard_map/ppermute | solution.py:25
  148.2 15.4 %collective-permute-start.8 = (bf16[2,80,1536]{2,1,0:T(8,128)(2,1)S(1)}, bf16[2,80,1536]{2,1,0:T(8,128)(2,1)S(1)}, u32[]{:S(2)}, u32[]{:S(2)}) collective-permute-start(bf16[2,80,1536]{2,1,0:T(8,128)(2,1)S(1)} %get-tuple-element.68), channel_id=1, source_target_pairs={{0,16},{16,32},{32,48},{48,64},{64,80},{80,96},{96,112},{112,0},{1... | collective-permute-start | bytes 1474568 | tf_op jit(solution)/shard_map/ppermute | solution.py:25
  148.2 15.4 %collective-permute-start.9 = (bf16[2,80,1536]{2,1,0:T(8,128)(2,1)S(1)}, bf16[2,80,1536]{2,1,0:T(8,128)(2,1)S(1)}, u32[]{:S(2)}, u32[]{:S(2)}) collective-permute-start(bf16[2,80,1536]{2,1,0:T(8,128)(2,1)S(1)} %get-tuple-element.69), channel_id=1, source_target_pairs={{0,128},{128,0},{1,129},{129,1},{2,130},{130,2},{3,131},{131,3},{4... | collective-permute-start | bytes 1474568 | tf_op jit(solution)/shard_map/ppermute | solution.py:29
  164.8 3.1 %collective-permute-start.13 = (bf16[16,144,256]{2,1,0:T(8,128)(2,1)}, bf16[16,144,256]{2,1,0:T(8,128)(2,1)S(1)}, u32[]{:S(2)}, u32[]{:S(2)}) collective-permute-start(bf16[16,144,256]{2,1,0:T(8,128)(2,1)} %bitcast.103), channel_id=1, source_target_pairs={{0,8},{8,0},{1,9},{9,1},{2,10},{10,2},{3,11},{11,3},{4,12},{12,4},... | collective-permute-start | bytes 3538952 | tf_op jit(solution)/shard_map/ppermute | solution.py:29
  164.8 14.0 %collective-permute-start.10 = (bf16[2,80,1536]{2,1,0:T(8,128)(2,1)}, bf16[2,80,1536]{2,1,0:T(8,128)(2,1)S(1)}, u32[]{:S(2)}, u32[]{:S(2)}) collective-permute-start(bf16[2,80,1536]{2,1,0:T(8,128)(2,1)} %get-tuple-element.74), channel_id=1, source_target_pairs={{0,112},{16,0},{32,16},{48,32},{64,48},{80,64},{96,80},{112,96},{1... | collective-permute-start | bytes 1474568 | tf_op jit(solution)/shard_map/ppermute | solution.py:25
  166.1 14.7 %collective-permute-start.11 = (bf16[2,80,1536]{2,1,0:T(8,128)(2,1)}, bf16[2,80,1536]{2,1,0:T(8,128)(2,1)S(1)}, u32[]{:S(2)}, u32[]{:S(2)}) collective-permute-start(bf16[2,80,1536]{2,1,0:T(8,128)(2,1)} %get-tuple-element.75), channel_id=1, source_target_pairs={{0,16},{16,32},{32,48},{48,64},{64,80},{80,96},{96,112},{112,0},{1... | collective-permute-start | bytes 1474568 | tf_op jit(solution)/shard_map/ppermute | solution.py:25
  167.0 14.7 %collective-permute-start.12 = (bf16[2,80,1536]{2,1,0:T(8,128)(2,1)}, bf16[2,80,1536]{2,1,0:T(8,128)(2,1)S(1)}, u32[]{:S(2)}, u32[]{:S(2)}) collective-permute-start(bf16[2,80,1536]{2,1,0:T(8,128)(2,1)} %get-tuple-element.76), channel_id=1, source_target_pairs={{0,128},{128,0},{1,129},{129,1},{2,130},{130,2},{3,131},{131,3},{4... | collective-permute-start | bytes 1474568 | tf_op jit(solution)/shard_map/ppermute | solution.py:29
  183.0 15.5 %collective-permute-start.14 = (bf16[2,80,1536]{2,1,0:T(8,128)(2,1)S(1)}, bf16[2,80,1536]{2,1,0:T(8,128)(2,1)}, u32[]{:S(2)}, u32[]{:S(2)}) collective-permute-start(bf16[2,80,1536]{2,1,0:T(8,128)(2,1)S(1)} %fusion.1), channel_id=1, source_target_pairs={{0,112},{16,0},{32,16},{48,32},{64,48},{80,64},{96,80},{112,96},{1... | collective-permute-start | bytes 1474568 | tf_op jit(solution)/shard_map/ppermute | solution.py:25
  187.7 14.6 %collective-permute-start.15 = (bf16[2,80,1536]{2,1,0:T(8,128)(2,1)S(1)}, bf16[2,80,1536]{2,1,0:T(8,128)(2,1)}, u32[]{:S(2)}, u32[]{:S(2)}) collective-permute-start(bf16[2,80,1536]{2,1,0:T(8,128)(2,1)S(1)} %get-tuple-element.85), channel_id=1, source_target_pairs={{0,128},{128,0},{1,129},{129,1},{2,130},{130,2},{3,131},{131,3},{4... | collective-permute-start | bytes 1474568 | tf_op jit(solution)/shard_map/ppermute | solution.py:29
  203.9 7.3 %collective-permute-start.16 = (bf16[80,1536]{1,0:T(8,128)(2,1)}, bf16[80,1536]{1,0:T(8,128)(2,1)}, u32[]{:S(2)}, u32[]{:S(2)}) collective-permute-start(bf16[80,1536]{1,0:T(8,128)(2,1)} %get-tuple-element.90), channel_id=1, source_target_pairs={{0,112},{16,0},{32,16},{48,32},{64,48},{80,64},{96,80},{112,96},{1... | collective-permute-start | bytes 737288 | tf_op jit(solution)/shard_map/ppermute | solution.py:25
  204.4 8.3 %collective-permute-start.17 = (bf16[80,1536]{1,0:T(8,128)(2,1)S(1)}, bf16[80,1536]{1,0:T(8,128)(2,1)}, u32[]{:S(2)}, u32[]{:S(2)}) collective-permute-start(bf16[80,1536]{1,0:T(8,128)(2,1)S(1)} %get-tuple-element.91), channel_id=1, source_target_pairs={{0,16},{16,32},{32,48},{48,64},{64,80},{80,96},{96,112},{112,0},{1... | collective-permute-start | bytes 737288 | tf_op jit(solution)/shard_map/ppermute | solution.py:25
  206.5 16.2 %collective-permute-start.20 = (bf16[80,1536]{1,0:T(8,128)(2,1)S(1)}, bf16[80,1536]{1,0:T(8,128)(2,1)S(1)}, u32[]{:S(2)}, u32[]{:S(2)}) collective-permute-start(bf16[80,1536]{1,0:T(8,128)(2,1)S(1)} %dynamic-slice_bitcast_fusion), channel_id=1, source_target_pairs={{0,128},{128,0},{1,129},{129,1},{2,130},{130,2},{3,131},{131,3},{4... | collective-permute-start | bytes 737288 | tf_op jit(solution)/shard_map/ppermute | solution.py:29
  214.9 7.9 %collective-permute-start.18 = (bf16[80,1536]{1,0:T(8,128)(2,1)}, bf16[80,1536]{1,0:T(8,128)(2,1)S(1)}, u32[]{:S(2)}, u32[]{:S(2)}) collective-permute-start(bf16[80,1536]{1,0:T(8,128)(2,1)} %get-tuple-element.111), channel_id=1, source_target_pairs={{0,112},{16,0},{32,16},{48,32},{64,48},{80,64},{96,80},{112,96},{1... | collective-permute-start | bytes 737288 | tf_op jit(solution)/shard_map/ppermute | solution.py:25
  215.4 7.7 %collective-permute-start.19 = (bf16[80,1536]{1,0:T(8,128)(2,1)}, bf16[80,1536]{1,0:T(8,128)(2,1)}, u32[]{:S(2)}, u32[]{:S(2)}) collective-permute-start(bf16[80,1536]{1,0:T(8,128)(2,1)} %get-tuple-element.110), channel_id=1, source_target_pairs={{0,16},{16,32},{32,48},{48,64},{64,80},{80,96},{96,112},{112,0},{1... | collective-permute-start | bytes 737288 | tf_op jit(solution)/shard_map/ppermute | solution.py:25
  217.0 12.4 %all-to-all-start = ((bf16[8,16,768]{2,1,0:T(8,128)(2,1)}), bf16[8,16,768]{2,1,0:T(8,128)(2,1)S(1)}, u32[]{:S(2)}, u32[]{:S(2)}) async-start(bf16[8,16,768]{2,1,0:T(8,128)(2,1)} %bitcast.18), calls=%async_computation | async-start | bytes 393216 | tf_op jit(solution)/shard_map/all_to_all | solution.py:287
  225.3 6.5 %collective-permute-start.21 = (bf16[80,1536]{1,0:T(8,128)(2,1)}, bf16[80,1536]{1,0:T(8,128)(2,1)}, u32[]{:S(2)}, u32[]{:S(2)}) collective-permute-start(bf16[80,1536]{1,0:T(8,128)(2,1)} %get-tuple-element.109), channel_id=1, source_target_pairs={{0,112},{16,0},{32,16},{48,32},{64,48},{80,64},{96,80},{112,96},{1... | collective-permute-start | bytes 737288 | tf_op jit(solution)/shard_map/ppermute | solution.py:25
  226.8 7.6 %collective-permute-start.22 = (bf16[80,1536]{1,0:T(8,128)(2,1)}, bf16[80,1536]{1,0:T(8,128)(2,1)S(1)}, u32[]{:S(2)}, u32[]{:S(2)}) collective-permute-start(bf16[80,1536]{1,0:T(8,128)(2,1)} %get-tuple-element.108), channel_id=1, source_target_pairs={{0,16},{16,32},{32,48},{48,64},{64,80},{80,96},{96,112},{112,0},{1... | collective-permute-start | bytes 737288 | tf_op jit(solution)/shard_map/ppermute | solution.py:25
  236.2 6.9 %collective-permute-start.23 = (bf16[80,1536]{1,0:T(8,128)(2,1)}, bf16[80,1536]{1,0:T(8,128)(2,1)}, u32[]{:S(2)}, u32[]{:S(2)}) collective-permute-start(bf16[80,1536]{1,0:T(8,128)(2,1)} %fusion.7), channel_id=1, source_target_pairs={{0,112},{16,0},{32,16},{48,32},{64,48},{80,64},{96,80},{112,96},{1... | collective-permute-start | bytes 737288 | tf_op jit(solution)/shard_map/ppermute | solution.py:25
  237.3 15.3 %all-to-all-start.1 = ((bf16[16,5,1536]{2,1,0:T(8,128)(2,1)}), bf16[16,5,1536]{2,1,0:T(8,128)(2,1)S(1)}, u32[]{:S(2)}, u32[]{:S(2)}) async-start(bf16[16,5,1536]{2,1,0:T(8,128)(2,1)} %reshape.86), calls=%async_computation.1 | async-start | bytes 786432 | tf_op jit(solution)/shard_map/all_to_all | solution.py:316
  252.6 13.0 %all-to-all-start.2 = ((bf16[16,5,1536]{2,1,0:T(8,128)(2,1)}), bf16[16,5,1536]{2,1,0:T(8,128)(2,1)S(1)}, u32[]{:S(2)}, u32[]{:S(2)}) async-start(bf16[16,5,1536]{2,1,0:T(8,128)(2,1)} %reshape.88), calls=%async_computation.2 | async-start | bytes 786432 | tf_op jit(solution)/shard_map/all_to_all | solution.py:316
  (15 other events, 139.1 us)
Sparse Core Ops, SparseCore 0:
  114.6 44.3 all-gather.1

commit v3 on v2

--- a/solution.py
+++ b/solution.py
@@ -132,33 +132,28 @@
     )(place, queries, doc_ids[None, :], near, far)
 
 
-def slice_kernel(place, weight_ref, *refs):
-    outs, sems = refs[:-1], refs[-1]
-    columns, strip = outs[0].shape[1], outs[0].shape[0] // 2
-    copies = []
-    for i, out in enumerate(outs):
-        at = pl.multiple_of(((1 - place[2]) * len(outs) + i) * columns, columns)
-        for k in range(2):
-            rows = pl.ds(k * strip, strip)
-            copies.append(
-                pltpu.make_async_copy(weight_ref.at[rows, pl.ds(at, columns)], out.at[rows, :], sems.at[2 * i + k])
-            )
-    for copy in copies:
-        copy.start()
-    for copy in copies:
-        copy.wait()
+def slice_kernel(place, *refs):
+    for i in range(GROUPS):
+        refs[GROUPS + i][...] = refs[i][...]
 
 
 def other_columns(place, weight, columns):
-    any_spec = pl.BlockSpec(memory_space=pl.ANY)
+    depth, strips = weight.shape[0], 4
+    rows = depth // strips
     return pl.pallas_call(
         slice_kernel,
-        out_shape=[jax.ShapeDtypeStruct((weight.shape[0], columns), weight.dtype)] * GROUPS,
-        in_specs=[pl.BlockSpec(memory_space=pltpu.SMEM), any_spec],
-        out_specs=[any_spec] * GROUPS,
-        scratch_shapes=[pltpu.SemaphoreType.DMA((2 * GROUPS,))],
+        out_shape=[jax.ShapeDtypeStruct((depth, columns), weight.dtype)] * GROUPS,
+        grid_spec=pltpu.PrefetchScalarGridSpec(
+            num_scalar_prefetch=1,
+            grid=(strips,),
+            in_specs=[
+                pl.BlockSpec((rows, columns), lambda i, s, g=g: (i, (1 - s[2]) * GROUPS + g)) for g in range(GROUPS)
+            ],
+            out_specs=[pl.BlockSpec((rows, columns), lambda i, s: (i, 0))] * GROUPS,
+        ),
+        compiler_params=pltpu.CompilerParams(vmem_limit_bytes=PRODUCT_VMEM),
         name="columns",
-    )(place, weight)
+    )(place, *([pltpu.with_memory_space_constraint(weight, pltpu.HBM)] * GROUPS))
 
 
 def product_kernel(count, offsets, place, *refs):
@@ -249,46 +244,47 @@
     block_other = swap(block, "yh")
     acts_other, other[0], block_other = join(acts_other, other[0], block_other)
     acts_other = acts_other.reshape(2, Z, -1, depth)
-    near = lax.all_gather(jnp.concatenate([block, block_other], axis=0), "z", axis=0, tiled=True)
+    pair = jnp.concatenate([block, block_other], axis=0)
+    near = lax.all_gather(pair, "z", axis=0, tiled=True)
 
     def make(where, group, block, picks, steps=1, offsets=None, split=False):
         return product(where, acts, acts_other, weight, other[group], group, block, picks, steps, offsets, split)
 
-    down, up = make(
-        place, 0, (2, 1), [lambda i, s: (0, lax.rem(s[1] + 4, Z)), lambda i, s: (0, lax.rem(s[1] + 3, Z))]
-    )
-    down, up = down[:, 0], up[:, 0]
+    def first_terms(where, orders):
+        picks = [lambda i, s, k=ORDER[order]: (0, lax.rem(s[1] + k, Z)) for order in orders]
+        return [term[:, 0] for term in make(where, 0, (2, 1), picks)]
+
+    down, up = first_terms(after(place, pair), (0, 1))
     sent = make(after(place, down), 1, (1, Z), [lambda i, s: (1 - s[0], 0)], 1, [ORDER[k : k + 2] for k in (0, 2, 4, 6)])
     got = []
 
     down, up, piece = shift(down, -1), shift(up, 1), swap(sent[0], "yh")
-    (full,) = make(after(place, sent[0]), 0, (1, Z), [lambda i, s: (i, 0)], 2, [ORDER], True)
-    down, up, piece, full = join(down, up, piece, full)
+    down_term, up_term = first_terms(after(place, sent[0]), (2, 3))
+    down, up, piece, down_term, up_term = join(down, up, piece, down_term, up_term)
     got.append(piece)
-    down, up = add(down, full[2]), add(up, full[3])
+    down, up = add(down, down_term), add(up, up_term)
     down, up, going = join(down, up, sent[1])
 
-    here, near = after(place, down), after(near, down)
+    here = after(place, down)
     down, up, piece = shift(down, -1), shift(up, 1), swap(going, "yh")
     (kept,) = make(here, 1, (1, Z), [lambda i, s: (s[0], 0)], 1, [ORDER])
-    down, up, piece, kept = join(down, up, piece, kept)
+    terms = first_terms(after(place, kept), (4, 5, 6, 7))
+    down, up, piece, *terms = join(down, up, piece, *terms)
     got.append(piece)
-    down, up = add(down, full[4]), add(up, full[5])
+    down, up = add(down, terms[0]), add(up, terms[1])
     down, up, going = join(down, up, sent[2])
 
-    near = after(near, down).reshape(2 * Z, -1, near.shape[-1])
     down, up, piece = shift(down, -1), shift(up, 1), swap(going, "yh")
+    down, up, piece, near = join(down, up, piece, near)
+    got.append(piece)
+    down = add(down, terms[2])
+    down, going, near = join(down, sent[3], near)
+
+    near = near.reshape(2 * Z, -1, near.shape[-1])
+    down, last = shift(down, -1), swap(going, "yh")
     context = attend(place, queries, doc_ids, near, swap(near, "c"))
-    down, up, piece, context = join(down, up, piece, context)
-    got.append(piece)
-    down = add(down, full[6])
-    down, going, context = join(down, sent[3], context)
-
-    residual = lax.all_to_all(context, EXP, split_axis=0, concat_axis=1, tiled=True)
-    down, piece = shift(down, -1), swap(going, "yh")
-    down, piece = join(down, piece)
-    got.append(piece)
-    first = add(down, up, full[7])
+    down, context = join(down, context)
+    first = add(down, up, terms[3])
 
     def second_term(order):
         return kept[order], got[order // 2][order % 2]
@@ -297,31 +293,28 @@
     down, up = add(*second_term(0)), add(*second_term(1))
     down, up, going = join(down, up, going)
     down, up, moved = shift(down, -1), shift(up, 1), swap(going, "yh")
+    residual = lax.all_to_all(context, EXP, split_axis=0, concat_axis=1, tiled=True)
     down, up = join(down, up)
     down, up = add(down, *second_term(2)), add(up, *second_term(3))
     down, up = shift(down, -1), shift(up, 1)
-    down, up, moved = join(down, up, moved)
+    down, up, moved, last = join(down, up, moved, last)
+    got.append(last)
     first = add(chunk_of(first, high), moved)
     down, up = add(down, *second_term(4)), add(up, *second_term(5))
     down, up = shift(down, -1), shift(up, 1)
     down, up = join(down, up)
     down = add(down, *second_term(6))
-    second = add(shift(down, -1), up, *second_term(7))
+    down, residual = join(shift(down, -1), residual)
+    second = add(down, up, *second_term(7))
 
     tokens = routes.shape[0]
     capacity = first.shape[0] // (2 * EXPERTS)
     mix = mixing(routes, route_weights, capacity)
-    mixed = []
-    for rows in (first, second):
-        home = lax.all_to_all(
-            rows.reshape(2 * EXPERTS, capacity, -1), ("c",) + EXP, split_axis=0, concat_axis=0, tiled=True
-        )
-        if rows is first:
-            home = after(home, second)
-        home = home.reshape(2, EXPERTS * capacity, -1)
-        both = jnp.einsum("tr,crn->tcn", mix, home, preferred_element_type=jnp.float32)
-        mixed.append(both[:tokens] + both[tokens:])
-    mixed = jnp.concatenate(mixed, axis=2).reshape(tokens, -1)
+    rows = jnp.concatenate([first, second], axis=1).reshape(2 * EXPERTS, capacity, -1)
+    home = lax.all_to_all(rows, ("c",) + EXP, split_axis=0, concat_axis=0, tiled=True)
+    home = home.reshape(2, EXPERTS * capacity, -1)
+    both = jnp.einsum("tr,crn->tcn", mix, home, preferred_element_type=jnp.float32)
+    mixed = (both[:tokens] + both[tokens:]).reshape(tokens, -1)
     moe_out = residual.astype(jnp.float32) + mixed
     return (context, moe_out.astype(jnp.bfloat16))
 

time: 274 us -> 193 us (0.70)
  Pallas kernels: 127 us -> 36.1 us
  waiting for transfers between devices: 66.6 us -> 72.5 us
  local copies, waits for them, and re-layouts: 7.58 us -> 11 us
  starting transfers between devices: 41.5 us -> 44.6 us
    pallas_call x1, Pallas kernels: 97.2 us -> 4.44 us  [other_columns(): pl.pallas_call(slice_kernel, out_shape=[jax.ShapeDtypeStruct((depth, colu...]
    ppermute x10, waiting for transfers between devices: 9.94 us -> 21.8 us  [swap(): return lax.ppermute(value, axis, [(0, 1), (1, 0)])]
    ppermute x14, waiting for transfers between devices: 37.9 us -> 30.1 us  [shift(): return lax.ppermute(value, 'z', [(i, (i + step) % Z) for i in range(Z)])]
    ppermute x14, starting transfers between devices: 22 us -> 28.2 us  [shift(): return lax.ppermute(value, 'z', [(i, (i + step) % Z) for i in range(Z)])]
    all_to_all x2 -> x1, starting transfers between devices: 9.36 us -> 3.61 us  [shards(): lax.all_to_all(rows, ('c',) + EXP, split_axis=0, concat_axis=0, tiled=True)]
    unnamed x39 -> x55, local copies, waits for them, and re-layouts: 5.28 us -> 9.37 us
    all_to_all x1, waiting for transfers between devices: 2.13 us -> 6.14 us  [shards(): lax.all_to_all(context, EXP, split_axis=0, concat_axis=1, tiled=True)]
    ppermute x10, starting transfers between devices: 4.35 us -> 7.33 us  [swap(): return lax.ppermute(value, axis, [(0, 1), (1, 0)])]
  transfers between devices with their start and end apart: 28 -> 27, of which waited for: 20 -> 18; matrix products, arithmetic and copies ran while one was open for 5% -> 3% of each run, Pallas kernels for 11% -> 16%
where the time goes in v3:
time: 193 us; the launch traced here: 192 us
  waiting for transfers between devices  72.5 us (38%)
  starting transfers between devices  44.6 us (23%)
  Pallas kernels  36.1 us (19%)
  between operations  14.4 us (7%)
  other arithmetic  13.5 us (7%)
  local copies, waits for them, and re-layouts  11 us (6%)
    ppermute x14, waiting for transfers between devices, shift(): return lax.ppermute(value, 'z', [(i, (i + step) % Z) for i in range(Z)])  30.1 us
    ppermute x14, starting transfers between devices, shift(): return lax.ppermute(value, 'z', [(i, (i + step) % Z) for i in range(Z)])  28.2 us
    ppermute x10, waiting for transfers between devices, swap(): return lax.ppermute(value, axis, [(0, 1), (1, 0)])  21.8 us
    pallas_call x5, Pallas kernels, product(): pl.pallas_call(lambda *refs: product_kernel(len(picks), offsets, *refs),...  21.3 us
    all_to_all x1, waiting for transfers between devices, shards(): lax.all_to_all(rows, ('c',) + EXP, split_axis=0, concat_axis=0, tiled=True)  14.4 us
    convert_element_type x11, other arithmetic, add(): return total.astype(jnp.bfloat16)  11.7 us
    pallas_call x1, Pallas kernels, attend(): pl.pallas_call(lambda *refs: attention_kernel(head, *refs), out_shape=jax...  10.4 us
    unnamed x55, local copies, waits for them, and re-layouts  9.37 us
  transfers between devices with their start and end apart: 27, of which 18 were waited for; matrix products, arithmetic and copies ran while one was open for 3% of the time, Pallas kernels for 16%

profile of v3, /device:TPU:16, one launch (start us, length us, event | category | flops | bytes accessed | tf_op | source)
XLA Modules:
  0.0 192.3 jit_solution(16877398914570232607)
XLA Ops:
  7.3 4.4 %columns.1 = (bf16[512,1536]{1,0:T(8,128)(2,1)S(1)}, bf16[512,1536]{1,0:T(8,128)(2,1)}) custom-call(s32[3]{0:T(128)S(1)} %pad_add_fusion.place.refs_0_, bf16[512,6144]{1,0:T(8,128)(2,1)} %bitcast.119, bf16[512,6144]{1,0:T(8,128)(2,1)} %bitcast.120), custom_call_target="tpu_custom_call" | custom-call | tf_op jit(solution)/shard_map/columns/pallas_call | solution.py:143
  12.3 2.2 %collective-permute-start.2 = (bf16[144,1,256]{2,0,1:T(8,128)(2,1)S(1)}, bf16[144,1,256]{2,0,1:T(8,128)(2,1)S(1)}, u32[]{:S(2)}, u32[]{:S(2)}) collective-permute-start(bf16[144,1,256]{2,0,1:T(8,128)(2,1)S(1)} %pad_maximum_fusion.2), channel_id=1, source_target_pairs={{0,128},{128,0},{1,129},{129,1},{2,130},{130,2},{3,131},{131,3},{4... | collective-permute-start | bytes 221192 | tf_op jit(solution)/shard_map/ppermute | solution.py:29
  14.5 4.1 %collective-permute-done.2 = bf16[144,1,256]{2,0,1:T(8,128)(2,1)S(1)} collective-permute-done((bf16[144,1,256]{2,0,1:T(8,128)(2,1)S(1)}, bf16[144,1,256]{2,0,1:T(8,128)(2,1)S(1)}, u32[]{:S(2)}, u32[]{:S(2)}) %collective-permute-start.2) | collective-permute-done | bytes 73760 | tf_op jit(solution)/shard_map/ppermute | solution.py:29
  22.5 3.9 %product.5 = (bf16[2,1,80,1536]{3,2,1,0:T(8,128)(2,1)}, bf16[2,1,80,1536]{3,2,1,0:T(8,128)(2,1)}) custom-call(s32[3]{0:T(128)S(1)} %pad_add_fusion.place.refs_0_, bf16[2,8,80,512]{3,2,1,0:T(8,128)(2,1)S(1)} %bitcast.90, bf16[2,8,80,512]{3,2,1,0:T(8,128)(2,1)S(1)} %bitcast.91, bf16[2,8,80,512]{3,2,1,0:T(8,128)(2,1)S(1)} %bitcast.100, ...), custom_call_target="tpu_custom_call" | custom-call | tf_op jit(solution)/shard_map/product/pallas_call | solution.py:201
  26.4 5.9 %collective-permute-start.3 = (bf16[2,80,1536]{2,1,0:T(8,128)(2,1)}, bf16[2,80,1536]{2,1,0:T(8,128)(2,1)}, u32[]{:S(2)}, u32[]{:S(2)}) collective-permute-start(bf16[2,80,1536]{2,1,0:T(8,128)(2,1)} %bitcast.9), channel_id=1, source_target_pairs={{0,112},{16,0},{32,16},{48,32},{64,48},{80,64},{96,80},{112,96},{1... | collective-permute-start | bytes 1474568 | tf_op jit(solution)/shard_map/ppermute | solution.py:25
  32.3 5.2 %product.6 = (bf16[2,80,1536]{2,1,0:T(8,128)(2,1)}, bf16[2,80,1536]{2,1,0:T(8,128)(2,1)S(1)}, bf16[2,80,1536]{2,1,0:T(8,128)(2,1)S(1)}, bf16[2,80,1536]{2,1,0:T(8,128)(2,1)S(1)}) custom-call(s32[3]{0:T(128)S(1)} %pad_add_fusion.place.refs_0_, bf16[2,8,80,512]{3,2,1,0:T(8,128)(2,1)S(1)} %bitcast.92, bf16[2,8,80,512]{3,2,1,0:T(8,128)(2,1)S(1)} %bitcast.102, ...), custom_call_target="tpu_custom_call" | custom-call | tf_op jit(solution)/shard_map/product/pallas_call | solution.py:201
  40.9 3.2 %product.7 = (bf16[2,1,80,1536]{3,2,1,0:T(8,128)(2,1)S(1)}, bf16[2,1,80,1536]{3,2,1,0:T(8,128)(2,1)S(1)}) custom-call(s32[3]{0:T(128)S(1)} %pad_add_fusion.place.refs_0_, bf16[2,8,80,512]{3,2,1,0:T(8,128)(2,1)S(1)} %bitcast.93, bf16[2,8,80,512]{3,2,1,0:T(8,128)(2,1)S(1)} %bitcast.94, bf16[2,8,80,512]{3,2,1,0:T(8,128)(2,1)S(1)} %bitcast.103, ...), custom_call_target="tpu_custom_call" | custom-call | tf_op jit(solution)/shard_map/product/pallas_call | solution.py:201
  44.1 2.6 %collective-permute-done.4 = bf16[2,80,1536]{2,1,0:T(8,128)(2,1)} collective-permute-done((bf16[2,80,1536]{2,1,0:T(8,128)(2,1)}, bf16[2,80,1536]{2,1,0:T(8,128)(2,1)}, u32[]{:S(2)}, u32[]{:S(2)}) %collective-permute-start.4) | collective-permute-done | bytes 491552 | tf_op jit(solution)/shard_map/ppermute | solution.py:25
  46.8 7.2 %collective-permute-done.6 = bf16[2,80,1536]{2,1,0:T(8,128)(2,1)} collective-permute-done((bf16[2,80,1536]{2,1,0:T(8,128)(2,1)}, bf16[2,80,1536]{2,1,0:T(8,128)(2,1)}, u32[]{:S(2)}, u32[]{:S(2)}) %collective-permute-start.6) | collective-permute-done | bytes 491552 | tf_op jit(solution)/shard_map/ppermute | solution.py:29
  55.4 3.0 %collective-permute-start.7 = (bf16[2,80,1536]{2,1,0:T(8,128)(2,1)S(1)}, bf16[2,80,1536]{2,1,0:T(8,128)(2,1)S(1)}, u32[]{:S(2)}, u32[]{:S(2)}) collective-permute-start(bf16[2,80,1536]{2,1,0:T(8,128)(2,1)S(1)} %get-tuple-element.84), channel_id=1, source_target_pairs={{0,112},{16,0},{32,16},{48,32},{64,48},{80,64},{96,80},{112,96},{1... | collective-permute-start | bytes 1474568 | tf_op jit(solution)/shard_map/ppermute | solution.py:25
  58.8 4.6 %product.8 = bf16[8,80,1536]{2,1,0:T(8,128)(2,1)S(1)} custom-call(s32[3]{0:T(128)S(1)} %pad_add_fusion.place.refs_0_, bf16[2,8,80,512]{3,2,1,0:T(8,128)(2,1)S(1)} %bitcast.95, bf16[2,8,80,512]{3,2,1,0:T(8,128)(2,1)S(1)} %bitcast.105, bf16[512,6144]{1,0:T(8,128)(2,1)} %bitcast.124, bf16[512,1536]{1,0:T(8,128)(2,1)} %collective-permute-done.5.refs_4_), custom_call_target="tpu_custom_call" | custom-call | tf_op jit(solution)/shard_map/product/pallas_call | solution.py:201
  64.7 4.4 %product.9 = (bf16[2,1,80,1536]{3,2,1,0:T(8,128)(2,1)S(1)}, bf16[2,1,80,1536]{3,2,1,0:T(8,128)(2,1)S(1)}, bf16[2,1,80,1536]{3,2,1,0:T(8,128)(2,1)S(1)}, bf16[2,1,80,1536]{3,2,1,0:T(8,128)(2,1)S(1)}) custom-call(s32[3]{0:T(128)S(1)} %pad_add_fusion.place.refs_0_, bf16[2,8,80,512]{3,2,1,0:T(8,128)(2,1)S(1)} %bitcast.96, bf16[2,8,80,512]{3,2,1,0:T(8,128)(2,1)S(1)} %bitcast.97, ...), custom_call_target="tpu_custom_call" | custom-call | tf_op jit(solution)/shard_map/product/pallas_call | solution.py:201
  69.9 5.4 %collective-permute-done.7 = bf16[2,80,1536]{2,1,0:T(8,128)(2,1)S(1)} collective-permute-done((bf16[2,80,1536]{2,1,0:T(8,128)(2,1)S(1)}, bf16[2,80,1536]{2,1,0:T(8,128)(2,1)S(1)}, u32[]{:S(2)}, u32[]{:S(2)}) %collective-permute-start.7) | collective-permute-done | bytes 491552 | tf_op jit(solution)/shard_map/ppermute | solution.py:25
  75.3 2.8 %collective-permute-done.8 = bf16[2,80,1536]{2,1,0:T(8,128)(2,1)S(1)} collective-permute-done((bf16[2,80,1536]{2,1,0:T(8,128)(2,1)S(1)}, bf16[2,80,1536]{2,1,0:T(8,128)(2,1)S(1)}, u32[]{:S(2)}, u32[]{:S(2)}) %collective-permute-start.8) | collective-permute-done | bytes 491552 | tf_op jit(solution)/shard_map/ppermute | solution.py:25
  81.1 9.2 %collective-permute-done.10 = bf16[2,80,1536]{2,1,0:T(8,128)(2,1)} collective-permute-done((bf16[2,80,1536]{2,1,0:T(8,128)(2,1)S(1)}, bf16[2,80,1536]{2,1,0:T(8,128)(2,1)}, u32[]{:S(2)}, u32[]{:S(2)}) %collective-permute-start.10) | collective-permute-done | bytes 491552 | tf_op jit(solution)/shard_map/ppermute | solution.py:25
  93.3 2.2 %add_convert_fusion.1 = bf16[2,80,1536]{2,1,0:T(8,128)(2,1)} fusion(bf16[2,80,1536]{2,1,0:T(8,128)(2,1)} %bitcast.112, bf16[2,80,1536]{2,1,0:T(8,128)(2,1)} %collective-permute-done.10), kind=kLoop, calls=%fused_computation.1 | loop fusion | flops 983040 | bytes 1474560 | tf_op jit(solution)/shard_map/convert_element_type | solution.py:225
  98.6 10.4 %attention.1 = bf16[128,768]{1,0:T(8,128)(2,1)} custom-call(s32[3]{0:T(128)S(1)} %pad_add_fusion.place.refs_0_, bf16[128,768]{1,0:T(8,128)(2,1)S(1)} %copy-done.11, s32[1,128]{1,0:T(1,128)S(1)} %bitcast.118, bf16[16,144,256]{2,1,0:T(8,128)(2,1)S(1)} %bitcast.111, bf16[16,144,256]{2,1,0:T(8,128)(2,1)} %collective-permute-done.14.refs_4_), custom_call_target="tpu_custom_call" | custom-call | tf_op jit(solution)/shard_map/attention/pallas_call | solution.py:118
  110.6 7.1 %collective-permute-start.15 = (bf16[80,1536]{1,0:T(8,128)(2,1)S(1)}, bf16[80,1536]{1,0:T(8,128)(2,1)S(1)}, u32[]{:S(2)}, u32[]{:S(2)}) collective-permute-start(bf16[80,1536]{1,0:T(8,128)(2,1)S(1)} %get-tuple-element.112), channel_id=1, source_target_pairs={{0,112},{16,0},{32,16},{48,32},{64,48},{80,64},{96,80},{112,96},{1... | collective-permute-start | bytes 737288 | tf_op jit(solution)/shard_map/ppermute | solution.py:25
  117.8 3.5 %collective-permute-start.19 = (bf16[80,1536]{1,0:T(8,128)(2,1)S(1)}, bf16[80,1536]{1,0:T(8,128)(2,1)S(1)}, u32[]{:S(2)}, u32[]{:S(2)}) collective-permute-start(bf16[80,1536]{1,0:T(8,128)(2,1)S(1)} %dynamic-slice_bitcast_fusion), channel_id=1, source_target_pairs={{0,128},{128,0},{1,129},{129,1},{2,130},{130,2},{3,131},{131,3},{4... | collective-permute-start | bytes 737288 | tf_op jit(solution)/shard_map/ppermute | solution.py:29
  121.3 2.4 %collective-permute-done.15 = bf16[80,1536]{1,0:T(8,128)(2,1)S(1)} collective-permute-done((bf16[80,1536]{1,0:T(8,128)(2,1)S(1)}, bf16[80,1536]{1,0:T(8,128)(2,1)S(1)}, u32[]{:S(2)}, u32[]{:S(2)}) %collective-permute-start.15) | collective-permute-done | bytes 245792 | tf_op jit(solution)/shard_map/ppermute | solution.py:25
  123.7 3.4 %collective-permute-done.16 = bf16[80,1536]{1,0:T(8,128)(2,1)S(1)} collective-permute-done((bf16[80,1536]{1,0:T(8,128)(2,1)S(1)}, bf16[80,1536]{1,0:T(8,128)(2,1)S(1)}, u32[]{:S(2)}, u32[]{:S(2)}) %collective-permute-start.16) | collective-permute-done | bytes 245792 | tf_op jit(solution)/shard_map/ppermute | solution.py:25
  127.7 1.7 collective-permute-start.18
  129.4 3.9 %collective-permute-done.20 = bf16[2,80,1536]{2,1,0:T(8,128)(2,1)S(1)} collective-permute-done((bf16[2,80,1536]{2,1,0:T(8,128)(2,1)S(1)}, bf16[2,80,1536]{2,1,0:T(8,128)(2,1)S(1)}, u32[]{:S(2)}, u32[]{:S(2)}) %collective-permute-start.20) | collective-permute-done | bytes 491552 | tf_op jit(solution)/shard_map/ppermute | solution.py:29
  133.3 4.6 %collective-permute-done.19 = bf16[80,1536]{1,0:T(8,128)(2,1)S(1)} collective-permute-done((bf16[80,1536]{1,0:T(8,128)(2,1)S(1)}, bf16[80,1536]{1,0:T(8,128)(2,1)S(1)}, u32[]{:S(2)}, u32[]{:S(2)}) %collective-permute-start.19) | collective-permute-done | bytes 245792 | tf_op jit(solution)/shard_map/ppermute | solution.py:29
  138.6 2.1 %fusion.3 = (bf16[80,1536]{1,0:T(8,128)(2,1)}, bf16[80,1536]{1,0:T(8,128)(2,1)}) fusion(bf16[80,1536]{1,0:T(8,128)(2,1)S(1)} %collective-permute-done.18, bf16[8,80,1536]{2,1,0:T(8,128)(2,1)S(1)} %copy-done.6, bf16[2,80,1536]{2,1,0:T(8,128)(2,1)} %collective-permute-done.12, bf16[80,1536]{1,0:T(8,128)(2,1)S(1)} %collective-permute-done.17), kind=kLoop, calls=%fused_computation.16 | loop fusion | flops 1474560 | bytes 1966080 | tf_op jit(solution)/shard_map/convert_element_type | solution.py:225
  140.7 3.0 %collective-permute-start.21 = (bf16[80,1536]{1,0:T(8,128)(2,1)}, bf16[80,1536]{1,0:T(8,128)(2,1)}, u32[]{:S(2)}, u32[]{:S(2)}) collective-permute-start(bf16[80,1536]{1,0:T(8,128)(2,1)} %get-tuple-element.131), channel_id=1, source_target_pairs={{0,112},{16,0},{32,16},{48,32},{64,48},{80,64},{96,80},{112,96},{1... | collective-permute-start | bytes 737288 | tf_op jit(solution)/shard_map/ppermute | solution.py:25
  143.7 5.4 %all-to-all-start = ((bf16[8,16,768]{2,1,0:T(8,128)(2,1)}), bf16[8,16,768]{2,1,0:T(8,128)(2,1)S(1)}, u32[]{:S(2)}, u32[]{:S(2)}) async-start(bf16[8,16,768]{2,1,0:T(8,128)(2,1)} %bitcast.32), calls=%async_computation | async-start | bytes 393216 | tf_op jit(solution)/shard_map/all_to_all | solution.py:296
  149.6 6.1 %all-to-all-done = bf16[8,16,768]{2,1,0:T(8,128)(2,1)S(1)} async-done(((bf16[8,16,768]{2,1,0:T(8,128)(2,1)}), bf16[8,16,768]{2,1,0:T(8,128)(2,1)S(1)}, u32[]{:S(2)}, u32[]{:S(2)}) %all-to-all-start) | async-done | bytes 196640 | tf_op jit(solution)/shard_map/all_to_all | solution.py:296
  156.8 3.3 %collective-permute-start.23 = (bf16[80,1536]{1,0:T(8,128)(2,1)S(1)}, bf16[80,1536]{1,0:T(8,128)(2,1)S(1)}, u32[]{:S(2)}, u32[]{:S(2)}) collective-permute-start(bf16[80,1536]{1,0:T(8,128)(2,1)S(1)} %fusion.2), channel_id=1, source_target_pairs={{0,112},{16,0},{32,16},{48,32},{64,48},{80,64},{96,80},{112,96},{1... | collective-permute-start | bytes 737288 | tf_op jit(solution)/shard_map/ppermute | solution.py:25
  161.1 2.7 %collective-permute-done.23 = bf16[80,1536]{1,0:T(8,128)(2,1)S(1)} collective-permute-done((bf16[80,1536]{1,0:T(8,128)(2,1)S(1)}, bf16[80,1536]{1,0:T(8,128)(2,1)S(1)}, u32[]{:S(2)}, u32[]{:S(2)}) %collective-permute-start.23) | collective-permute-done | bytes 245792 | tf_op jit(solution)/shard_map/ppermute | solution.py:25
  166.1 3.6 %all-to-all-start.1 = ((bf16[16,5,3072]{2,1,0:T(8,128)(2,1)}), bf16[16,5,3072]{2,1,0:T(8,128)(2,1)S(1)}, u32[]{:S(2)}, u32[]{:S(2)}) async-start(bf16[16,5,3072]{2,1,0:T(8,128)(2,1)} %reshape.66), calls=%async_computation.1 | async-start | bytes 1572864 | tf_op jit(solution)/shard_map/all_to_all | solution.py:314
  169.8 14.4 %all-to-all-done.1 = bf16[16,5,3072]{2,1,0:T(8,128)(2,1)S(1)} async-done(((bf16[16,5,3072]{2,1,0:T(8,128)(2,1)}), bf16[16,5,3072]{2,1,0:T(8,128)(2,1)S(1)}, u32[]{:S(2)}, u32[]{:S(2)}) %all-to-all-start.1) | async-done | bytes 491552 | tf_op jit(solution)/shard_map/all_to_all | solution.py:314
  (117 shorter events, 30.1 us)
Async XLA Ops:
  7.2 86.1 %all-gather.2.cloned.1.call-start = ((), (), s32[]{:S(2)}) async-start(), calls=%async_computation.2 | async-start | bytes 1327104 | tf_op jit(solution)/shard_map/all_gather | solution.py:248
  11.7 7.5 %collective-permute-start.1 = (bf16[512,1536]{1,0:T(8,128)(2,1)S(1)}, bf16[512,1536]{1,0:T(8,128)(2,1)S(1)}, u32[]{:S(2)}, u32[]{:S(2)}) collective-permute-start(bf16[512,1536]{1,0:T(8,128)(2,1)S(1)} %get-tuple-element.65), channel_id=1, source_target_pairs={{0,8},{8,0},{1,9},{9,1},{2,10},{10,2},{3,11},{11,3},{4,12},{12,4},... | collective-permute-start | bytes 4718600 | tf_op jit(solution)/shard_map/ppermute | solution.py:29
  11.7 20.5 %collective-permute-start.5 = (bf16[512,1536]{1,0:T(8,128)(2,1)}, bf16[512,1536]{1,0:T(8,128)(2,1)}, u32[]{:S(2)}, u32[]{:S(2)}) collective-permute-start(bf16[512,1536]{1,0:T(8,128)(2,1)} %get-tuple-element.66), channel_id=1, source_target_pairs={{0,8},{8,0},{1,9},{9,1},{2,10},{10,2},{3,11},{11,3},{4,12},{12,4},... | collective-permute-start | bytes 4718600 | tf_op jit(solution)/shard_map/ppermute | solution.py:29
  12.2 7.0 %collective-permute-start = (bf16[1280,512]{1,0:T(8,128)(2,1)S(1)}, bf16[1280,512]{1,0:T(8,128)(2,1)S(1)}, u32[]{:S(2)}, u32[]{:S(2)}) collective-permute-start(bf16[1280,512]{1,0:T(8,128)(2,1)S(1)} %bitcast.89), channel_id=1, source_target_pairs={{0,8},{8,0},{1,9},{9,1},{2,10},{10,2},{3,11},{11,3},{4,12},{12,4},... | collective-permute-start | bytes 3932168 | tf_op jit(solution)/shard_map/ppermute | solution.py:29
  12.3 6.3 %collective-permute-start.2 = (bf16[144,1,256]{2,0,1:T(8,128)(2,1)S(1)}, bf16[144,1,256]{2,0,1:T(8,128)(2,1)S(1)}, u32[]{:S(2)}, u32[]{:S(2)}) collective-permute-start(bf16[144,1,256]{2,0,1:T(8,128)(2,1)S(1)} %pad_maximum_fusion.2), channel_id=1, source_target_pairs={{0,128},{128,0},{1,129},{129,1},{2,130},{130,2},{3,131},{131,3},{4... | collective-permute-start | bytes 221192 | tf_op jit(solution)/shard_map/ppermute | solution.py:29
  26.4 17.7 %collective-permute-start.3 = (bf16[2,80,1536]{2,1,0:T(8,128)(2,1)}, bf16[2,80,1536]{2,1,0:T(8,128)(2,1)}, u32[]{:S(2)}, u32[]{:S(2)}) collective-permute-start(bf16[2,80,1536]{2,1,0:T(8,128)(2,1)} %bitcast.9), channel_id=1, source_target_pairs={{0,112},{16,0},{32,16},{48,32},{64,48},{80,64},{96,80},{112,96},{1... | collective-permute-start | bytes 1474568 | tf_op jit(solution)/shard_map/ppermute | solution.py:25
  32.3 14.5 %collective-permute-start.4 = (bf16[2,80,1536]{2,1,0:T(8,128)(2,1)}, bf16[2,80,1536]{2,1,0:T(8,128)(2,1)}, u32[]{:S(2)}, u32[]{:S(2)}) collective-permute-start(bf16[2,80,1536]{2,1,0:T(8,128)(2,1)} %bitcast.10), channel_id=1, source_target_pairs={{0,16},{16,32},{32,48},{48,64},{64,80},{80,96},{96,112},{112,0},{1... | collective-permute-start | bytes 1474568 | tf_op jit(solution)/shard_map/ppermute | solution.py:25
  39.1 14.8 %collective-permute-start.6 = (bf16[2,80,1536]{2,1,0:T(8,128)(2,1)}, bf16[2,80,1536]{2,1,0:T(8,128)(2,1)}, u32[]{:S(2)}, u32[]{:S(2)}) collective-permute-start(bf16[2,80,1536]{2,1,0:T(8,128)(2,1)} %get-tuple-element.75), channel_id=1, source_target_pairs={{0,128},{128,0},{1,129},{129,1},{2,130},{130,2},{3,131},{131,3},{4... | collective-permute-start | bytes 1474568 | tf_op jit(solution)/shard_map/ppermute | solution.py:29
  44.1 14.3 %copy-start.18 = (bf16[2,80,1536]{2,1,0:T(8,128)(2,1)S(1)}, bf16[2,80,1536]{2,1,0:T(8,128)(2,1)}, u32[]{:S(2)}) copy-start(bf16[2,80,1536]{2,1,0:T(8,128)(2,1)} %copy-done.17) | copy-start | bytes 1474564
  55.4 19.9 %collective-permute-start.7 = (bf16[2,80,1536]{2,1,0:T(8,128)(2,1)S(1)}, bf16[2,80,1536]{2,1,0:T(8,128)(2,1)S(1)}, u32[]{:S(2)}, u32[]{:S(2)}) collective-permute-start(bf16[2,80,1536]{2,1,0:T(8,128)(2,1)S(1)} %get-tuple-element.84), channel_id=1, source_target_pairs={{0,112},{16,0},{32,16},{48,32},{64,48},{80,64},{96,80},{112,96},{1... | collective-permute-start | bytes 1474568 | tf_op jit(solution)/shard_map/ppermute | solution.py:25
  58.4 19.7 %collective-permute-start.8 = (bf16[2,80,1536]{2,1,0:T(8,128)(2,1)S(1)}, bf16[2,80,1536]{2,1,0:T(8,128)(2,1)S(1)}, u32[]{:S(2)}, u32[]{:S(2)}) collective-permute-start(bf16[2,80,1536]{2,1,0:T(8,128)(2,1)S(1)} %get-tuple-element.85), channel_id=1, source_target_pairs={{0,16},{16,32},{32,48},{48,64},{64,80},{80,96},{96,112},{112,0},{1... | collective-permute-start | bytes 1474568 | tf_op jit(solution)/shard_map/ppermute | solution.py:25
  58.4 19.7 %collective-permute-start.9 = (bf16[2,80,1536]{2,1,0:T(8,128)(2,1)S(1)}, bf16[2,80,1536]{2,1,0:T(8,128)(2,1)S(1)}, u32[]{:S(2)}, u32[]{:S(2)}) collective-permute-start(bf16[2,80,1536]{2,1,0:T(8,128)(2,1)S(1)} %copy-done.18), channel_id=1, source_target_pairs={{0,128},{128,0},{1,129},{129,1},{2,130},{130,2},{3,131},{131,3},{4... | collective-permute-start | bytes 1474568 | tf_op jit(solution)/shard_map/ppermute | solution.py:29
  78.2 18.8 %copy-start.6 = (bf16[8,80,1536]{2,1,0:T(8,128)(2,1)S(1)}, bf16[8,80,1536]{2,1,0:T(8,128)(2,1)}, u32[]{:S(2)}) copy-start(bf16[8,80,1536]{2,1,0:T(8,128)(2,1)} %copy-done.5) | copy-start | bytes 5898244
  78.4 20.3 %copy-start.11 = (bf16[128,768]{1,0:T(8,128)(2,1)S(1)}, bf16[128,768]{1,0:T(8,128)(2,1)}, u32[]{:S(2)}) copy-start(bf16[128,768]{1,0:T(8,128)(2,1)} %refs_1_.1) | copy-start | bytes 589828
  78.4 11.9 %collective-permute-start.10 = (bf16[2,80,1536]{2,1,0:T(8,128)(2,1)S(1)}, bf16[2,80,1536]{2,1,0:T(8,128)(2,1)}, u32[]{:S(2)}, u32[]{:S(2)}) collective-permute-start(bf16[2,80,1536]{2,1,0:T(8,128)(2,1)S(1)} %add_convert_fusion.3), channel_id=1, source_target_pairs={{0,112},{16,0},{32,16},{48,32},{64,48},{80,64},{96,80},{112,96},{1... | collective-permute-start | bytes 1474568 | tf_op jit(solution)/shard_map/ppermute | solution.py:25
  79.5 12.0 %collective-permute-start.11 = (bf16[2,80,1536]{2,1,0:T(8,128)(2,1)S(1)}, bf16[2,80,1536]{2,1,0:T(8,128)(2,1)S(1)}, u32[]{:S(2)}, u32[]{:S(2)}) collective-permute-start(bf16[2,80,1536]{2,1,0:T(8,128)(2,1)S(1)} %add_convert_fusion.2), channel_id=1, source_target_pairs={{0,16},{16,32},{32,48},{48,64},{64,80},{80,96},{96,112},{112,0},{1... | collective-permute-start | bytes 1474568 | tf_op jit(solution)/shard_map/ppermute | solution.py:25
  80.7 12.6 %collective-permute-start.12 = (bf16[2,80,1536]{2,1,0:T(8,128)(2,1)S(1)}, bf16[2,80,1536]{2,1,0:T(8,128)(2,1)}, u32[]{:S(2)}, u32[]{:S(2)}) collective-permute-start(bf16[2,80,1536]{2,1,0:T(8,128)(2,1)S(1)} %copy-done.16), channel_id=1, source_target_pairs={{0,128},{128,0},{1,129},{129,1},{2,130},{130,2},{3,131},{131,3},{4... | collective-permute-start | bytes 1474568 | tf_op jit(solution)/shard_map/ppermute | solution.py:29
  95.4 3.2 %collective-permute-start.14 = (bf16[16,144,256]{2,1,0:T(8,128)(2,1)}, bf16[16,144,256]{2,1,0:T(8,128)(2,1)}, u32[]{:S(2)}, u32[]{:S(2)}) collective-permute-start(bf16[16,144,256]{2,1,0:T(8,128)(2,1)} %bitcast.110), channel_id=1, source_target_pairs={{0,8},{8,0},{1,9},{9,1},{2,10},{10,2},{3,11},{11,3},{4,12},{12,4},... | collective-permute-start | bytes 3538952 | tf_op jit(solution)/shard_map/ppermute | solution.py:29
  95.4 13.9 %collective-permute-start.13 = (bf16[2,80,1536]{2,1,0:T(8,128)(2,1)}, bf16[2,80,1536]{2,1,0:T(8,128)(2,1)}, u32[]{:S(2)}, u32[]{:S(2)}) collective-permute-start(bf16[2,80,1536]{2,1,0:T(8,128)(2,1)} %add_convert_fusion.1), channel_id=1, source_target_pairs={{0,112},{16,0},{32,16},{48,32},{64,48},{80,64},{96,80},{112,96},{1... | collective-permute-start | bytes 1474568 | tf_op jit(solution)/shard_map/ppermute | solution.py:25
  109.0 18.0 %copy-start.20 = (bf16[2,80,1536]{2,1,0:T(8,128)(2,1)S(1)}, bf16[2,80,1536]{2,1,0:T(8,128)(2,1)}, u32[]{:S(2)}) copy-start(bf16[2,80,1536]{2,1,0:T(8,128)(2,1)} %copy-done.19) | copy-start | bytes 1474564
  110.6 13.0 %collective-permute-start.15 = (bf16[80,1536]{1,0:T(8,128)(2,1)S(1)}, bf16[80,1536]{1,0:T(8,128)(2,1)S(1)}, u32[]{:S(2)}, u32[]{:S(2)}) collective-permute-start(bf16[80,1536]{1,0:T(8,128)(2,1)S(1)} %get-tuple-element.112), channel_id=1, source_target_pairs={{0,112},{16,0},{32,16},{48,32},{64,48},{80,64},{96,80},{112,96},{1... | collective-permute-start | bytes 737288 | tf_op jit(solution)/shard_map/ppermute | solution.py:25
  117.7 9.3 %collective-permute-start.16 = (bf16[80,1536]{1,0:T(8,128)(2,1)S(1)}, bf16[80,1536]{1,0:T(8,128)(2,1)S(1)}, u32[]{:S(2)}, u32[]{:S(2)}) collective-permute-start(bf16[80,1536]{1,0:T(8,128)(2,1)S(1)} %get-tuple-element.113), channel_id=1, source_target_pairs={{0,16},{16,32},{32,48},{48,64},{64,80},{80,96},{96,112},{112,0},{1... | collective-permute-start | bytes 737288 | tf_op jit(solution)/shard_map/ppermute | solution.py:25
  117.7 15.6 %collective-permute-start.20 = (bf16[2,80,1536]{2,1,0:T(8,128)(2,1)S(1)}, bf16[2,80,1536]{2,1,0:T(8,128)(2,1)S(1)}, u32[]{:S(2)}, u32[]{:S(2)}) collective-permute-start(bf16[2,80,1536]{2,1,0:T(8,128)(2,1)S(1)} %copy-done.14), channel_id=1, source_target_pairs={{0,128},{128,0},{1,129},{129,1},{2,130},{130,2},{3,131},{131,3},{4... | collective-permute-start | bytes 1474568 | tf_op jit(solution)/shard_map/ppermute | solution.py:29
  117.8 20.1 %collective-permute-start.19 = (bf16[80,1536]{1,0:T(8,128)(2,1)S(1)}, bf16[80,1536]{1,0:T(8,128)(2,1)S(1)}, u32[]{:S(2)}, u32[]{:S(2)}) collective-permute-start(bf16[80,1536]{1,0:T(8,128)(2,1)S(1)} %dynamic-slice_bitcast_fusion), channel_id=1, source_target_pairs={{0,128},{128,0},{1,129},{129,1},{2,130},{130,2},{3,131},{131,3},{4... | collective-permute-start | bytes 737288 | tf_op jit(solution)/shard_map/ppermute | solution.py:29
  127.3 21.8 %copy-start.25 = (s32[16,2]{0,1:T(2,128)S(1)}, s32[16,2]{0,1:T(2,128)}, u32[]{:S(2)}) copy-start(s32[16,2]{0,1:T(2,128)} %param.12) | copy-start | bytes 388
  127.3 11.3 %collective-permute-start.17 = (bf16[80,1536]{1,0:T(8,128)(2,1)S(1)}, bf16[80,1536]{1,0:T(8,128)(2,1)S(1)}, u32[]{:S(2)}, u32[]{:S(2)}) collective-permute-start(bf16[80,1536]{1,0:T(8,128)(2,1)S(1)} %get-tuple-element.133), channel_id=1, source_target_pairs={{0,112},{16,0},{32,16},{48,32},{64,48},{80,64},{96,80},{112,96},{1... | collective-permute-start | bytes 737288 | tf_op jit(solution)/shard_map/ppermute | solution.py:25
  127.7 11.0 %collective-permute-start.18 = (bf16[80,1536]{1,0:T(8,128)(2,1)S(1)}, bf16[80,1536]{1,0:T(8,128)(2,1)S(1)}, u32[]{:S(2)}, u32[]{:S(2)}) collective-permute-start(bf16[80,1536]{1,0:T(8,128)(2,1)S(1)} %get-tuple-element.132), channel_id=1, source_target_pairs={{0,16},{16,32},{32,48},{48,64},{64,80},{80,96},{96,112},{112,0},{1... | collective-permute-start | bytes 737288 | tf_op jit(solution)/shard_map/ppermute | solution.py:25
  140.7 15.0 %collective-permute-start.21 = (bf16[80,1536]{1,0:T(8,128)(2,1)}, bf16[80,1536]{1,0:T(8,128)(2,1)}, u32[]{:S(2)}, u32[]{:S(2)}) collective-permute-start(bf16[80,1536]{1,0:T(8,128)(2,1)} %get-tuple-element.131), channel_id=1, source_target_pairs={{0,112},{16,0},{32,16},{48,32},{64,48},{80,64},{96,80},{112,96},{1... | collective-permute-start | bytes 737288 | tf_op jit(solution)/shard_map/ppermute | solution.py:25
  143.7 12.1 %collective-permute-start.22 = (bf16[80,1536]{1,0:T(8,128)(2,1)}, bf16[80,1536]{1,0:T(8,128)(2,1)}, u32[]{:S(2)}, u32[]{:S(2)}) collective-permute-start(bf16[80,1536]{1,0:T(8,128)(2,1)} %get-tuple-element.130), channel_id=1, source_target_pairs={{0,16},{16,32},{32,48},{48,64},{64,80},{80,96},{96,112},{112,0},{1... | collective-permute-start | bytes 737288 | tf_op jit(solution)/shard_map/ppermute | solution.py:25
  143.7 12.0 %all-to-all-start = ((bf16[8,16,768]{2,1,0:T(8,128)(2,1)}), bf16[8,16,768]{2,1,0:T(8,128)(2,1)S(1)}, u32[]{:S(2)}, u32[]{:S(2)}) async-start(bf16[8,16,768]{2,1,0:T(8,128)(2,1)} %bitcast.32), calls=%async_computation | async-start | bytes 393216 | tf_op jit(solution)/shard_map/all_to_all | solution.py:296
  156.8 7.0 %collective-permute-start.23 = (bf16[80,1536]{1,0:T(8,128)(2,1)S(1)}, bf16[80,1536]{1,0:T(8,128)(2,1)S(1)}, u32[]{:S(2)}, u32[]{:S(2)}) collective-permute-start(bf16[80,1536]{1,0:T(8,128)(2,1)S(1)} %fusion.2), channel_id=1, source_target_pairs={{0,112},{16,0},{32,16},{48,32},{64,48},{80,64},{96,80},{112,96},{1... | collective-permute-start | bytes 737288 | tf_op jit(solution)/shard_map/ppermute | solution.py:25
  166.1 18.1 %all-to-all-start.1 = ((bf16[16,5,3072]{2,1,0:T(8,128)(2,1)}), bf16[16,5,3072]{2,1,0:T(8,128)(2,1)S(1)}, u32[]{:S(2)}, u32[]{:S(2)}) async-start(bf16[16,5,3072]{2,1,0:T(8,128)(2,1)} %reshape.66), calls=%async_computation.1 | async-start | bytes 1572864 | tf_op jit(solution)/shard_map/all_to_all | solution.py:314
  (22 other events, 112.3 us)
Sparse Core Ops, SparseCore 0:
  39.6 40.1 all-gather.1

commit v4 on v3

--- a/solution.py
+++ b/solution.py
@@ -132,28 +132,25 @@
     )(place, queries, doc_ids[None, :], near, far)
 
 
-def slice_kernel(place, *refs):
-    for i in range(GROUPS):
-        refs[GROUPS + i][...] = refs[i][...]
-
-
-def other_columns(place, weight, columns):
+def slice_kernel(place, w_ref, o_ref):
+    o_ref[...] = w_ref[...]
+
+
+def other_columns(place, weight, columns, group):
     depth, strips = weight.shape[0], 4
     rows = depth // strips
     return pl.pallas_call(
         slice_kernel,
-        out_shape=[jax.ShapeDtypeStruct((depth, columns), weight.dtype)] * GROUPS,
+        out_shape=jax.ShapeDtypeStruct((depth, columns), weight.dtype),
         grid_spec=pltpu.PrefetchScalarGridSpec(
             num_scalar_prefetch=1,
             grid=(strips,),
-            in_specs=[
-                pl.BlockSpec((rows, columns), lambda i, s, g=g: (i, (1 - s[2]) * GROUPS + g)) for g in range(GROUPS)
-            ],
-            out_specs=[pl.BlockSpec((rows, columns), lambda i, s: (i, 0))] * GROUPS,
+            in_specs=[pl.BlockSpec((rows, columns), lambda i, s: (i, (1 - s[2]) * GROUPS + group))],
+            out_specs=pl.BlockSpec((rows, columns), lambda i, s: (i, 0)),
         ),
         compiler_params=pltpu.CompilerParams(vmem_limit_bytes=PRODUCT_VMEM),
         name="columns",
-    )(place, *([pltpu.with_memory_space_constraint(weight, pltpu.HBM)] * GROUPS))
+    )(place, pltpu.with_memory_space_constraint(weight, pltpu.HBM))
 
 
 def product_kernel(count, offsets, place, *refs):
@@ -238,52 +235,55 @@
     acts = gate_up[0].reshape(2, Z, -1, depth)
 
     acts_other = swap(gate_up[0], "c")
-    parts = other_columns(place, weight, columns)
-    other = [swap(part, "c") for part in parts]
-    block = key_block(keys_values, after(doc_ids, *parts))
-    block_other = swap(block, "yh")
-    acts_other, other[0], block_other = join(acts_other, other[0], block_other)
+    part = other_columns(place, weight, columns, 0)
+    other = [swap(part, "c")]
+    part = other_columns(after(place, part), weight, columns, 1)
+    acts_other, other[0], part = join(acts_other, other[0], part)
+    other.append(swap(part, "c"))
     acts_other = acts_other.reshape(2, Z, -1, depth)
-    pair = jnp.concatenate([block, block_other], axis=0)
-    near = lax.all_gather(pair, "z", axis=0, tiled=True)
-
-    def make(where, group, block, picks, steps=1, offsets=None, split=False):
-        return product(where, acts, acts_other, weight, other[group], group, block, picks, steps, offsets, split)
+
+    def make(where, group, block, picks, offsets=None):
+        return product(where, acts, acts_other, weight, other[group], group, block, picks, 1, offsets, False)
 
     def first_terms(where, orders):
         picks = [lambda i, s, k=ORDER[order]: (0, lax.rem(s[1] + k, Z)) for order in orders]
         return [term[:, 0] for term in make(where, 0, (2, 1), picks)]
 
-    down, up = first_terms(after(place, pair), (0, 1))
-    sent = make(after(place, down), 1, (1, Z), [lambda i, s: (1 - s[0], 0)], 1, [ORDER[k : k + 2] for k in (0, 2, 4, 6)])
-    got = []
-
-    down, up, piece = shift(down, -1), shift(up, 1), swap(sent[0], "yh")
-    down_term, up_term = first_terms(after(place, sent[0]), (2, 3))
-    down, up, piece, down_term, up_term = join(down, up, piece, down_term, up_term)
-    got.append(piece)
+    down, up = first_terms(place, (0, 1))
+    block = key_block(keys_values, after(doc_ids, down))
+    pair = jnp.concatenate([block, swap(block, "yh")], axis=0)
+    near = lax.all_gather(pair, "z", axis=0, tiled=True)
+    here = after(place, block)
+    down, up = shift(down, -1), shift(up, 1)
+    down_term, up_term = first_terms(here, (2, 3))
+    sent = make(
+        after(place, down_term), 1, (1, Z), [lambda i, s: (1 - s[0], 0)], [ORDER[k : k + 2] for k in (0, 2, 4, 6)]
+    )
+    down, up, down_term, up_term, pair, *sent = join(down, up, down_term, up_term, pair, *sent)
     down, up = add(down, down_term), add(up, up_term)
-    down, up, going = join(down, up, sent[1])
+    down, up, sent[0] = join(down, up, sent[0])
 
     here = after(place, down)
-    down, up, piece = shift(down, -1), shift(up, 1), swap(going, "yh")
-    (kept,) = make(here, 1, (1, Z), [lambda i, s: (s[0], 0)], 1, [ORDER])
-    terms = first_terms(after(place, kept), (4, 5, 6, 7))
-    down, up, piece, *terms = join(down, up, piece, *terms)
-    got.append(piece)
+    down, up = shift(down, -1), shift(up, 1)
+    got = [swap(sent[0], "yh")]
+    terms = first_terms(here, (4, 5, 6, 7))
+    down, up, *terms = join(down, up, *terms)
     down, up = add(down, terms[0]), add(up, terms[1])
-    down, up, going = join(down, up, sent[2])
-
-    down, up, piece = shift(down, -1), shift(up, 1), swap(going, "yh")
-    down, up, piece, near = join(down, up, piece, near)
-    got.append(piece)
+    down, up, sent[1] = join(down, up, sent[1])
+
+    here = after(place, down)
+    down, up = shift(down, -1), shift(up, 1)
+    got.append(swap(after(sent[1], got[0]), "yh"))
+    (kept,) = make(here, 1, (1, Z), [lambda i, s: (s[0], 0)], [ORDER])
+    down, up, near, kept, got[0] = join(down, up, near, kept, got[0])
     down = add(down, terms[2])
-    down, going, near = join(down, sent[3], near)
+    down, sent[2], near = join(down, sent[2], near)
 
     near = near.reshape(2 * Z, -1, near.shape[-1])
-    down, last = shift(down, -1), swap(going, "yh")
+    down = shift(down, -1)
+    got.append(swap(after(sent[2], got[1]), "yh"))
     context = attend(place, queries, doc_ids, near, swap(near, "c"))
-    down, context = join(down, context)
+    down, context, got[1] = join(down, context, got[1])
     first = add(down, up, terms[3])
 
     def second_term(order):
@@ -291,19 +291,21 @@
 
     going = chunk_of(first, 1 - high)
     down, up = add(*second_term(0)), add(*second_term(1))
+    down, up, going, sent[3] = join(down, up, going, sent[3])
+    down, up = shift(down, -1), shift(up, 1)
+    got.append(swap(after(sent[3], got[2]), "yh"))
+    residual = lax.all_to_all(context, EXP, split_axis=0, concat_axis=1, tiled=True)
+    down, up, got[2] = join(down, up, got[2])
+    down, up = add(down, *second_term(2)), add(up, *second_term(3))
     down, up, going = join(down, up, going)
-    down, up, moved = shift(down, -1), shift(up, 1), swap(going, "yh")
-    residual = lax.all_to_all(context, EXP, split_axis=0, concat_axis=1, tiled=True)
+    down, up, moved = shift(down, -1), shift(up, 1), swap(after(going, got[3]), "yh")
+    down, up, got[3] = join(down, up, got[3])
+    down, up = add(down, *second_term(4)), add(up, *second_term(5))
     down, up = join(down, up)
-    down, up = add(down, *second_term(2)), add(up, *second_term(3))
-    down, up = shift(down, -1), shift(up, 1)
-    down, up, moved, last = join(down, up, moved, last)
-    got.append(last)
+    down, up = shift(down, -1), shift(up, 1)
+    down, up, moved = join(down, up, moved)
+    down = add(down, *second_term(6))
     first = add(chunk_of(first, high), moved)
-    down, up = add(down, *second_term(4)), add(up, *second_term(5))
-    down, up = shift(down, -1), shift(up, 1)
-    down, up = join(down, up)
-    down = add(down, *second_term(6))
     down, residual = join(shift(down, -1), residual)
     second = add(down, up, *second_term(7))
 

time: 193 us -> 189 us (0.979)
  local copies, waits for them, and re-layouts: 11 us -> 4.61 us
  starting transfers between devices: 44.6 us -> 39.5 us
  waiting for transfers between devices: 72.5 us -> 76.5 us
    ppermute x14, waiting for transfers between devices: 30.1 us -> 38.5 us  [shift(): return lax.ppermute(value, 'z', [(i, (i + step) % Z) for i in range(Z)])]
    unnamed x55 -> x39, local copies, waits for them, and re-layouts: 9.37 us -> 2.29 us
    ppermute x14, starting transfers between devices: 28.2 us -> 23.4 us  [shift(): return lax.ppermute(value, 'z', [(i, (i + step) % Z) for i in range(Z)])]
    ppermute x10, waiting for transfers between devices: 21.8 us -> 17.4 us  [swap(): return lax.ppermute(value, axis, [(0, 1), (1, 0)])]
    pallas_call x1 -> x2, Pallas kernels: 4.44 us -> 6.88 us  [other_columns(): pl.pallas_call(slice_kernel, out_shape=jax.ShapeDtypeStruct((depth, colum...]
  transfers between devices with their start and end apart: 27 -> 27, of which waited for: 18 -> 16; matrix products, arithmetic and copies ran while one was open for 3% -> 6% of each run, Pallas kernels for 16% -> 18%
where the time goes in v4:
time: 189 us; the launch traced here: 187 us
  waiting for transfers between devices  76.5 us (40%)
  starting transfers between devices  39.5 us (21%)
  Pallas kernels  37.2 us (20%)
  between operations  14.4 us (8%)
  other arithmetic  14.3 us (8%)
  local copies, waits for them, and re-layouts  4.61 us (2%)
    ppermute x14, waiting for transfers between devices, shift(): return lax.ppermute(value, 'z', [(i, (i + step) % Z) for i in range(Z)])  38.5 us
    ppermute x14, starting transfers between devices, shift(): return lax.ppermute(value, 'z', [(i, (i + step) % Z) for i in range(Z)])  23.4 us
    pallas_call x5, Pallas kernels, product(): pl.pallas_call(lambda *refs: product_kernel(len(picks), offsets, *refs),...  20.7 us
    ppermute x10, waiting for transfers between devices, swap(): return lax.ppermute(value, axis, [(0, 1), (1, 0)])  17.4 us
    all_to_all x1, waiting for transfers between devices, shards(): lax.all_to_all(rows, ('c',) + EXP, split_axis=0, concat_axis=0, tiled=True)  14.4 us
    convert_element_type x11, other arithmetic, add(): return total.astype(jnp.bfloat16)  12.5 us
    pallas_call x1, Pallas kernels, attend(): pl.pallas_call(lambda *refs: attention_kernel(head, *refs), out_shape=jax...  9.65 us
    ppermute x10, starting transfers between devices, swap(): return lax.ppermute(value, axis, [(0, 1), (1, 0)])  6.96 us
  transfers between devices with their start and end apart: 27, of which 16 were waited for; matrix products, arithmetic and copies ran while one was open for 6% of the time, Pallas kernels for 18%

profile of v4, /device:TPU:16, one launch (start us, length us, event | category | flops | bytes accessed | tf_op | source)
XLA Modules:
  0.0 186.8 jit_solution(5981705360662679840)
XLA Ops:
  7.3 2.8 %columns.2 = bf16[512,1536]{1,0:T(8,128)(2,1)S(1)} custom-call(s32[3]{0:T(128)S(1)} %pad_add_fusion.place.refs_0_, bf16[512,6144]{1,0:T(8,128)(2,1)} %bitcast.107), custom_call_target="tpu_custom_call" | custom-call | tf_op jit(solution)/shard_map/columns/pallas_call | solution.py:142
  10.7 4.1 %columns.3 = bf16[512,1536]{1,0:T(8,128)(2,1)} custom-call(s32[3]{0:T(128)S(1)} %pad_add_fusion.place.refs_0_, bf16[512,6144]{1,0:T(8,128)(2,1)} %bitcast.108), custom_call_target="tpu_custom_call" | custom-call | tf_op jit(solution)/shard_map/columns/pallas_call | solution.py:142
  15.6 3.9 %product.5 = (bf16[2,1,80,1536]{3,2,1,0:T(8,128)(2,1)}, bf16[2,1,80,1536]{3,2,1,0:T(8,128)(2,1)}) custom-call(s32[3]{0:T(128)S(1)} %pad_add_fusion.place.refs_0_, bf16[2,8,80,512]{3,2,1,0:T(8,128)(2,1)S(1)} %bitcast.78, bf16[2,8,80,512]{3,2,1,0:T(8,128)(2,1)S(1)} %bitcast.79, bf16[2,8,80,512]{3,2,1,0:T(8,128)(2,1)S(1)} %bitcast.88, ...), custom_call_target="tpu_custom_call" | custom-call | tf_op jit(solution)/shard_map/product/pallas_call | solution.py:198
  19.5 5.9 %collective-permute-start.2 = (bf16[2,80,1536]{2,1,0:T(8,128)(2,1)}, bf16[2,80,1536]{2,1,0:T(8,128)(2,1)}, u32[]{:S(2)}, u32[]{:S(2)}) collective-permute-start(bf16[2,80,1536]{2,1,0:T(8,128)(2,1)} %bitcast.7), channel_id=1, source_target_pairs={{0,112},{16,0},{32,16},{48,32},{64,48},{80,64},{96,80},{112,96},{1... | collective-permute-start | bytes 1474568 | tf_op jit(solution)/shard_map/ppermute | solution.py:25
  25.8 3.2 %product.6 = (bf16[2,1,80,1536]{3,2,1,0:T(8,128)(2,1)S(1)}, bf16[2,1,80,1536]{3,2,1,0:T(8,128)(2,1)S(1)}) custom-call(s32[3]{0:T(128)S(1)} %pad_add_fusion.place.refs_0_, bf16[2,8,80,512]{3,2,1,0:T(8,128)(2,1)S(1)} %bitcast.80, bf16[2,8,80,512]{3,2,1,0:T(8,128)(2,1)S(1)} %bitcast.81, bf16[2,8,80,512]{3,2,1,0:T(8,128)(2,1)S(1)} %bitcast.90, ...), custom_call_target="tpu_custom_call" | custom-call | tf_op jit(solution)/shard_map/product/pallas_call | solution.py:198
  32.1 4.6 %product.7 = (bf16[2,80,1536]{2,1,0:T(8,128)(2,1)S(1)}, bf16[2,80,1536]{2,1,0:T(8,128)(2,1)S(1)}, bf16[2,80,1536]{2,1,0:T(8,128)(2,1)S(1)}, bf16[2,80,1536]{2,1,0:T(8,128)(2,1)S(1)}) custom-call(s32[3]{0:T(128)S(1)} %pad_add_fusion.place.refs_0_, bf16[2,8,80,512]{3,2,1,0:T(8,128)(2,1)S(1)} %bitcast.82, bf16[2,8,80,512]{3,2,1,0:T(8,128)(2,1)S(1)} %bitcast.92, ...), custom_call_target="tpu_custom_call" | custom-call | tf_op jit(solution)/shard_map/product/pallas_call | solution.py:198
  36.8 3.3 %collective-permute-done.3 = bf16[2,80,1536]{2,1,0:T(8,128)(2,1)} collective-permute-done((bf16[2,80,1536]{2,1,0:T(8,128)(2,1)}, bf16[2,80,1536]{2,1,0:T(8,128)(2,1)}, u32[]{:S(2)}, u32[]{:S(2)}) %collective-permute-start.3) | collective-permute-done | bytes 491552 | tf_op jit(solution)/shard_map/ppermute | solution.py:25
  43.7 4.4 %product.8 = (bf16[2,1,80,1536]{3,2,1,0:T(8,128)(2,1)S(1)}, bf16[2,1,80,1536]{3,2,1,0:T(8,128)(2,1)S(1)}, bf16[2,1,80,1536]{3,2,1,0:T(8,128)(2,1)S(1)}, bf16[2,1,80,1536]{3,2,1,0:T(8,128)(2,1)S(1)}) custom-call(s32[3]{0:T(128)S(1)} %pad_add_fusion.place.refs_0_, bf16[2,8,80,512]{3,2,1,0:T(8,128)(2,1)S(1)} %bitcast.83, bf16[2,8,80,512]{3,2,1,0:T(8,128)(2,1)S(1)} %bitcast.84, ...), custom_call_target="tpu_custom_call" | custom-call | tf_op jit(solution)/shard_map/product/pallas_call | solution.py:198
  48.5 11.8 %collective-permute-done.6 = bf16[2,80,1536]{2,1,0:T(8,128)(2,1)S(1)} collective-permute-done((bf16[2,80,1536]{2,1,0:T(8,128)(2,1)S(1)}, bf16[2,80,1536]{2,1,0:T(8,128)(2,1)S(1)}, u32[]{:S(2)}, u32[]{:S(2)}) %collective-permute-start.6) | collective-permute-done | bytes 491552 | tf_op jit(solution)/shard_map/ppermute | solution.py:25
  60.3 3.2 %collective-permute-done.7 = bf16[2,80,1536]{2,1,0:T(8,128)(2,1)S(1)} collective-permute-done((bf16[2,80,1536]{2,1,0:T(8,128)(2,1)S(1)}, bf16[2,80,1536]{2,1,0:T(8,128)(2,1)S(1)}, u32[]{:S(2)}, u32[]{:S(2)}) %collective-permute-start.7) | collective-permute-done | bytes 491552 | tf_op jit(solution)/shard_map/ppermute | solution.py:25
  65.3 2.0 %collective-permute-start.9 = (bf16[2,80,1536]{2,1,0:T(8,128)(2,1)}, bf16[2,80,1536]{2,1,0:T(8,128)(2,1)}, u32[]{:S(2)}, u32[]{:S(2)}) collective-permute-start(bf16[2,80,1536]{2,1,0:T(8,128)(2,1)} %add_convert_fusion.2), channel_id=1, source_target_pairs={{0,16},{16,32},{32,48},{48,64},{64,80},{80,96},{96,112},{112,0},{1... | collective-permute-start | bytes 1474568 | tf_op jit(solution)/shard_map/ppermute | solution.py:25
  67.4 4.6 %product.9 = bf16[8,80,1536]{2,1,0:T(8,128)(2,1)S(1)} custom-call(s32[3]{0:T(128)S(1)} %pad_add_fusion.place.refs_0_, bf16[2,8,80,512]{3,2,1,0:T(8,128)(2,1)S(1)} %bitcast.87, bf16[2,8,80,512]{3,2,1,0:T(8,128)(2,1)S(1)} %bitcast.97, bf16[512,6144]{1,0:T(8,128)(2,1)} %bitcast.113, bf16[512,1536]{1,0:T(8,128)(2,1)} %collective-permute-done.5.refs_4_), custom_call_target="tpu_custom_call" | custom-call | tf_op jit(solution)/shard_map/product/pallas_call | solution.py:198
  73.3 4.8 %collective-permute-done.8 = bf16[2,80,1536]{2,1,0:T(8,128)(2,1)} collective-permute-done((bf16[2,80,1536]{2,1,0:T(8,128)(2,1)}, bf16[2,80,1536]{2,1,0:T(8,128)(2,1)}, u32[]{:S(2)}, u32[]{:S(2)}) %collective-permute-start.8) | collective-permute-done | bytes 491552 | tf_op jit(solution)/shard_map/ppermute | solution.py:25
  78.9 2.0 %add_convert_fusion.1 = bf16[2,80,1536]{2,1,0:T(8,128)(2,1)} fusion(bf16[2,80,1536]{2,1,0:T(8,128)(2,1)S(1)} %bitcast.100, bf16[2,80,1536]{2,1,0:T(8,128)(2,1)} %collective-permute-done.8), kind=kLoop, calls=%fused_computation.1 | loop fusion | flops 983040 | bytes 1474560 | tf_op jit(solution)/shard_map/convert_element_type | solution.py:222
  80.9 2.5 %collective-permute-start.13 = (bf16[2,80,1536]{2,1,0:T(8,128)(2,1)}, bf16[2,80,1536]{2,1,0:T(8,128)(2,1)S(1)}, u32[]{:S(2)}, u32[]{:S(2)}) collective-permute-start(bf16[2,80,1536]{2,1,0:T(8,128)(2,1)} %copy-done.15), channel_id=1, source_target_pairs={{0,128},{128,0},{1,129},{129,1},{2,130},{130,2},{3,131},{131,3},{4... | collective-permute-start | bytes 1474568 | tf_op jit(solution)/shard_map/ppermute | solution.py:29
  84.4 11.9 %collective-permute-done.13 = bf16[2,80,1536]{2,1,0:T(8,128)(2,1)S(1)} collective-permute-done((bf16[2,80,1536]{2,1,0:T(8,128)(2,1)}, bf16[2,80,1536]{2,1,0:T(8,128)(2,1)S(1)}, u32[]{:S(2)}, u32[]{:S(2)}) %collective-permute-start.13) | collective-permute-done | bytes 491552 | tf_op jit(solution)/shard_map/ppermute | solution.py:29
  96.3 2.5 %collective-permute-start.16 = (bf16[2,80,1536]{2,1,0:T(8,128)(2,1)}, bf16[2,80,1536]{2,1,0:T(8,128)(2,1)S(1)}, u32[]{:S(2)}, u32[]{:S(2)}) collective-permute-start(bf16[2,80,1536]{2,1,0:T(8,128)(2,1)} %copy-done.14), channel_id=1, source_target_pairs={{0,128},{128,0},{1,129},{129,1},{2,130},{130,2},{3,131},{131,3},{4... | collective-permute-start | bytes 1474568 | tf_op jit(solution)/shard_map/ppermute | solution.py:29
  100.2 9.6 %attention.1 = bf16[128,768]{1,0:T(8,128)(2,1)} custom-call(s32[3]{0:T(128)S(1)} %pad_add_fusion.place.refs_0_, bf16[128,768]{1,0:T(8,128)(2,1)S(1)} %copy-done.10, s32[1,128]{1,0:T(1,128)S(1)} %bitcast.106, bf16[16,144,256]{2,1,0:T(8,128)(2,1)S(1)} %bitcast.99, bf16[16,144,256]{2,1,0:T(8,128)(2,1)S(1)} %collective-permute-done.12.refs_4_), custom_call_target="tpu_custom_call" | custom-call | tf_op jit(solution)/shard_map/attention/pallas_call | solution.py:118
  109.9 1.5 add_convert_fusion
  112.1 6.6 %collective-permute-start.14 = (bf16[80,1536]{1,0:T(8,128)(2,1)S(1)}, bf16[80,1536]{1,0:T(8,128)(2,1)S(1)}, u32[]{:S(2)}, u32[]{:S(2)}) collective-permute-start(bf16[80,1536]{1,0:T(8,128)(2,1)S(1)} %get-tuple-element.129), channel_id=1, source_target_pairs={{0,112},{16,0},{32,16},{48,32},{64,48},{80,64},{96,80},{112,96},{1... | collective-permute-start | bytes 737288 | tf_op jit(solution)/shard_map/ppermute | solution.py:25
  118.9 5.1 %collective-permute-done.14 = bf16[80,1536]{1,0:T(8,128)(2,1)S(1)} collective-permute-done((bf16[80,1536]{1,0:T(8,128)(2,1)S(1)}, bf16[80,1536]{1,0:T(8,128)(2,1)S(1)}, u32[]{:S(2)}, u32[]{:S(2)}) %collective-permute-start.14) | collective-permute-done | bytes 245792 | tf_op jit(solution)/shard_map/ppermute | solution.py:25
  124.0 3.4 %collective-permute-done.15 = bf16[80,1536]{1,0:T(8,128)(2,1)S(1)} collective-permute-done((bf16[80,1536]{1,0:T(8,128)(2,1)S(1)}, bf16[80,1536]{1,0:T(8,128)(2,1)S(1)}, u32[]{:S(2)}, u32[]{:S(2)}) %collective-permute-start.15) | collective-permute-done | bytes 245792 | tf_op jit(solution)/shard_map/ppermute | solution.py:25
  128.0 1.7 collective-permute-start.18
  129.7 3.4 %collective-permute-done.19 = bf16[2,80,1536]{2,1,0:T(8,128)(2,1)S(1)} collective-permute-done((bf16[2,80,1536]{2,1,0:T(8,128)(2,1)S(1)}, bf16[2,80,1536]{2,1,0:T(8,128)(2,1)S(1)}, u32[]{:S(2)}, u32[]{:S(2)}) %collective-permute-start.19) | collective-permute-done | bytes 491552 | tf_op jit(solution)/shard_map/ppermute | solution.py:29
  134.2 1.5 collective-permute-done.18
  137.2 1.6 collective-permute-start.21
  138.8 5.5 %all-to-all-start = ((bf16[8,16,768]{2,1,0:T(8,128)(2,1)}), bf16[8,16,768]{2,1,0:T(8,128)(2,1)S(1)}, u32[]{:S(2)}, u32[]{:S(2)}) async-start(bf16[8,16,768]{2,1,0:T(8,128)(2,1)} %bitcast.32), calls=%async_computation | async-start | bytes 393216 | tf_op jit(solution)/shard_map/all_to_all | solution.py:297
  144.8 6.1 %all-to-all-done = bf16[8,16,768]{2,1,0:T(8,128)(2,1)S(1)} async-done(((bf16[8,16,768]{2,1,0:T(8,128)(2,1)}), bf16[8,16,768]{2,1,0:T(8,128)(2,1)S(1)}, u32[]{:S(2)}, u32[]{:S(2)}) %all-to-all-start) | async-done | bytes 196640 | tf_op jit(solution)/shard_map/all_to_all | solution.py:297
  152.1 1.7 collective-permute-start.23
  154.7 3.6 %collective-permute-done.23 = bf16[80,1536]{1,0:T(8,128)(2,1)S(1)} collective-permute-done((bf16[80,1536]{1,0:T(8,128)(2,1)S(1)}, bf16[80,1536]{1,0:T(8,128)(2,1)S(1)}, u32[]{:S(2)}, u32[]{:S(2)}) %collective-permute-start.23) | collective-permute-done | bytes 245792 | tf_op jit(solution)/shard_map/ppermute | solution.py:25
  160.5 3.6 %all-to-all-start.1 = ((bf16[16,5,3072]{2,1,0:T(8,128)(2,1)}), bf16[16,5,3072]{2,1,0:T(8,128)(2,1)S(1)}, u32[]{:S(2)}, u32[]{:S(2)}) async-start(bf16[16,5,3072]{2,1,0:T(8,128)(2,1)} %reshape.66), calls=%async_computation.1 | async-start | bytes 1572864 | tf_op jit(solution)/shard_map/all_to_all | solution.py:316
  164.3 14.4 %all-to-all-done.1 = bf16[16,5,3072]{2,1,0:T(8,128)(2,1)S(1)} async-done(((bf16[16,5,3072]{2,1,0:T(8,128)(2,1)}), bf16[16,5,3072]{2,1,0:T(8,128)(2,1)S(1)}, u32[]{:S(2)}, u32[]{:S(2)}) %all-to-all-start.1) | async-done | bytes 491552 | tf_op jit(solution)/shard_map/all_to_all | solution.py:316
  (102 shorter events, 25.4 us)
Async XLA Ops:
  7.2 66.2 %all-gather.2.cloned.1.call-start = ((), (), s32[]{:S(2)}) async-start(), calls=%async_computation.2 | async-start | bytes 1327104 | tf_op jit(solution)/shard_map/all_gather | solution.py:255
  10.1 5.4 %collective-permute-start.1 = (bf16[512,1536]{1,0:T(8,128)(2,1)S(1)}, bf16[512,1536]{1,0:T(8,128)(2,1)S(1)}, u32[]{:S(2)}, u32[]{:S(2)}) collective-permute-start(bf16[512,1536]{1,0:T(8,128)(2,1)S(1)} %columns.2), channel_id=1, source_target_pairs={{0,8},{8,0},{1,9},{9,1},{2,10},{10,2},{3,11},{11,3},{4,12},{12,4},... | collective-permute-start | bytes 4718600 | tf_op jit(solution)/shard_map/ppermute | solution.py:29
  10.2 5.3 %collective-permute-start = (bf16[1280,512]{1,0:T(8,128)(2,1)S(1)}, bf16[1280,512]{1,0:T(8,128)(2,1)S(1)}, u32[]{:S(2)}, u32[]{:S(2)}) collective-permute-start(bf16[1280,512]{1,0:T(8,128)(2,1)S(1)} %bitcast.77), channel_id=1, source_target_pairs={{0,8},{8,0},{1,9},{9,1},{2,10},{10,2},{3,11},{11,3},{4,12},{12,4},... | collective-permute-start | bytes 3932168 | tf_op jit(solution)/shard_map/ppermute | solution.py:29
  15.5 16.6 %collective-permute-start.5 = (bf16[512,1536]{1,0:T(8,128)(2,1)}, bf16[512,1536]{1,0:T(8,128)(2,1)}, u32[]{:S(2)}, u32[]{:S(2)}) collective-permute-start(bf16[512,1536]{1,0:T(8,128)(2,1)} %columns.3), channel_id=1, source_target_pairs={{0,8},{8,0},{1,9},{9,1},{2,10},{10,2},{3,11},{11,3},{4,12},{12,4},... | collective-permute-start | bytes 4718600 | tf_op jit(solution)/shard_map/ppermute | solution.py:29
  19.5 17.3 %collective-permute-start.2 = (bf16[2,80,1536]{2,1,0:T(8,128)(2,1)}, bf16[2,80,1536]{2,1,0:T(8,128)(2,1)}, u32[]{:S(2)}, u32[]{:S(2)}) collective-permute-start(bf16[2,80,1536]{2,1,0:T(8,128)(2,1)} %bitcast.7), channel_id=1, source_target_pairs={{0,112},{16,0},{32,16},{48,32},{64,48},{80,64},{96,80},{112,96},{1... | collective-permute-start | bytes 1474568 | tf_op jit(solution)/shard_map/ppermute | solution.py:25
  25.4 14.7 %collective-permute-start.3 = (bf16[2,80,1536]{2,1,0:T(8,128)(2,1)}, bf16[2,80,1536]{2,1,0:T(8,128)(2,1)}, u32[]{:S(2)}, u32[]{:S(2)}) collective-permute-start(bf16[2,80,1536]{2,1,0:T(8,128)(2,1)} %bitcast.8), channel_id=1, source_target_pairs={{0,16},{16,32},{32,48},{48,64},{64,80},{80,96},{96,112},{112,0},{1... | collective-permute-start | bytes 1474568 | tf_op jit(solution)/shard_map/ppermute | solution.py:25
  25.4 5.9 %collective-permute-start.4 = (bf16[144,1,256]{2,0,1:T(8,128)(2,1)S(1)}, bf16[144,1,256]{2,0,1:T(8,128)(2,1)S(1)}, u32[]{:S(2)}, u32[]{:S(2)}) collective-permute-start(bf16[144,1,256]{2,0,1:T(8,128)(2,1)S(1)} %pad_maximum_fusion.2), channel_id=1, source_target_pairs={{0,128},{128,0},{1,129},{129,1},{2,130},{130,2},{3,131},{131,3},{4... | collective-permute-start | bytes 221192 | tf_op jit(solution)/shard_map/ppermute | solution.py:29
  41.5 18.8 %collective-permute-start.6 = (bf16[2,80,1536]{2,1,0:T(8,128)(2,1)S(1)}, bf16[2,80,1536]{2,1,0:T(8,128)(2,1)S(1)}, u32[]{:S(2)}, u32[]{:S(2)}) collective-permute-start(bf16[2,80,1536]{2,1,0:T(8,128)(2,1)S(1)} %get-tuple-element.98), channel_id=1, source_target_pairs={{0,112},{16,0},{32,16},{48,32},{64,48},{80,64},{96,80},{112,96},{1... | collective-permute-start | bytes 1474568 | tf_op jit(solution)/shard_map/ppermute | solution.py:25
  42.5 21.0 %collective-permute-start.7 = (bf16[2,80,1536]{2,1,0:T(8,128)(2,1)S(1)}, bf16[2,80,1536]{2,1,0:T(8,128)(2,1)S(1)}, u32[]{:S(2)}, u32[]{:S(2)}) collective-permute-start(bf16[2,80,1536]{2,1,0:T(8,128)(2,1)S(1)} %get-tuple-element.99), channel_id=1, source_target_pairs={{0,16},{16,32},{32,48},{48,64},{64,80},{80,96},{96,112},{112,0},{1... | collective-permute-start | bytes 1474568 | tf_op jit(solution)/shard_map/ppermute | solution.py:25
  48.0 17.3 %copy-start.8 = (bf16[2,1,80,1536]{3,2,1,0:T(8,128)(2,1)}, bf16[2,1,80,1536]{3,2,1,0:T(8,128)(2,1)S(1)}, u32[]{:S(2)}) copy-start(bf16[2,1,80,1536]{3,2,1,0:T(8,128)(2,1)S(1)} %get-tuple-element.104) | copy-start | bytes 1474564
  48.0 25.3 %collective-permute-start.10 = (bf16[2,80,1536]{2,1,0:T(8,128)(2,1)S(1)}, bf16[2,80,1536]{2,1,0:T(8,128)(2,1)}, u32[]{:S(2)}, u32[]{:S(2)}) collective-permute-start(bf16[2,80,1536]{2,1,0:T(8,128)(2,1)S(1)} %get-tuple-element.113), channel_id=1, source_target_pairs={{0,128},{128,0},{1,129},{129,1},{2,130},{130,2},{3,131},{131,3},{4... | collective-permute-start | bytes 1474568 | tf_op jit(solution)/shard_map/ppermute | solution.py:29
  65.3 12.8 %collective-permute-start.8 = (bf16[2,80,1536]{2,1,0:T(8,128)(2,1)}, bf16[2,80,1536]{2,1,0:T(8,128)(2,1)}, u32[]{:S(2)}, u32[]{:S(2)}) collective-permute-start(bf16[2,80,1536]{2,1,0:T(8,128)(2,1)} %add_convert_fusion.3), channel_id=1, source_target_pairs={{0,112},{16,0},{32,16},{48,32},{64,48},{80,64},{96,80},{112,96},{1... | collective-permute-start | bytes 1474568 | tf_op jit(solution)/shard_map/ppermute | solution.py:25
  65.3 13.6 %collective-permute-start.9 = (bf16[2,80,1536]{2,1,0:T(8,128)(2,1)}, bf16[2,80,1536]{2,1,0:T(8,128)(2,1)}, u32[]{:S(2)}, u32[]{:S(2)}) collective-permute-start(bf16[2,80,1536]{2,1,0:T(8,128)(2,1)} %add_convert_fusion.2), channel_id=1, source_target_pairs={{0,16},{16,32},{32,48},{48,64},{64,80},{80,96},{96,112},{112,0},{1... | collective-permute-start | bytes 1474568 | tf_op jit(solution)/shard_map/ppermute | solution.py:25
  73.3 26.9 %copy-start.10 = (bf16[128,768]{1,0:T(8,128)(2,1)S(1)}, bf16[128,768]{1,0:T(8,128)(2,1)}, u32[]{:S(2)}) copy-start(bf16[128,768]{1,0:T(8,128)(2,1)} %refs_1_.1) | copy-start | bytes 589828
  73.3 26.9 %copy-start.5 = (bf16[2304,1,256]{2,0,1:T(8,128)(2,1)S(1)}, bf16[2304,1,256]{2,0,1:T(8,128)(2,1)}, u32[]{:S(2)}) copy-start(bf16[2304,1,256]{2,0,1:T(8,128)(2,1)} %all-gather.2.cloned.1.call-done) | copy-start | bytes 3538948
  80.9 19.3 %collective-permute-start.12 = (bf16[16,144,256]{2,1,0:T(8,128)(2,1)}, bf16[16,144,256]{2,1,0:T(8,128)(2,1)S(1)}, u32[]{:S(2)}, u32[]{:S(2)}) collective-permute-start(bf16[16,144,256]{2,1,0:T(8,128)(2,1)} %bitcast.98), channel_id=1, source_target_pairs={{0,8},{8,0},{1,9},{9,1},{2,10},{10,2},{3,11},{11,3},{4,12},{12,4},... | collective-permute-start | bytes 3538952 | tf_op jit(solution)/shard_map/ppermute | solution.py:29
  80.9 15.3 %collective-permute-start.13 = (bf16[2,80,1536]{2,1,0:T(8,128)(2,1)}, bf16[2,80,1536]{2,1,0:T(8,128)(2,1)S(1)}, u32[]{:S(2)}, u32[]{:S(2)}) collective-permute-start(bf16[2,80,1536]{2,1,0:T(8,128)(2,1)} %copy-done.15), channel_id=1, source_target_pairs={{0,128},{128,0},{1,129},{129,1},{2,130},{130,2},{3,131},{131,3},{4... | collective-permute-start | bytes 1474568 | tf_op jit(solution)/shard_map/ppermute | solution.py:29
  83.4 26.5 %collective-permute-start.11 = (bf16[2,80,1536]{2,1,0:T(8,128)(2,1)}, bf16[2,80,1536]{2,1,0:T(8,128)(2,1)}, u32[]{:S(2)}, u32[]{:S(2)}) collective-permute-start(bf16[2,80,1536]{2,1,0:T(8,128)(2,1)} %add_convert_fusion.1), channel_id=1, source_target_pairs={{0,112},{16,0},{32,16},{48,32},{64,48},{80,64},{96,80},{112,96},{1... | collective-permute-start | bytes 1474568 | tf_op jit(solution)/shard_map/ppermute | solution.py:25
  96.3 22.5 %collective-permute-start.16 = (bf16[2,80,1536]{2,1,0:T(8,128)(2,1)}, bf16[2,80,1536]{2,1,0:T(8,128)(2,1)S(1)}, u32[]{:S(2)}, u32[]{:S(2)}) collective-permute-start(bf16[2,80,1536]{2,1,0:T(8,128)(2,1)} %copy-done.14), channel_id=1, source_target_pairs={{0,128},{128,0},{1,129},{129,1},{2,130},{130,2},{3,131},{131,3},{4... | collective-permute-start | bytes 1474568 | tf_op jit(solution)/shard_map/ppermute | solution.py:29
  109.9 17.5 %copy-start.4 = (bf16[8,80,1536]{2,1,0:T(8,128)(2,1)S(1)}, bf16[8,80,1536]{2,1,0:T(8,128)(2,1)}, u32[]{:S(2)}) copy-start(bf16[8,80,1536]{2,1,0:T(8,128)(2,1)} %copy-done.3) | copy-start | bytes 5898244
  112.1 11.9 %collective-permute-start.14 = (bf16[80,1536]{1,0:T(8,128)(2,1)S(1)}, bf16[80,1536]{1,0:T(8,128)(2,1)S(1)}, u32[]{:S(2)}, u32[]{:S(2)}) collective-permute-start(bf16[80,1536]{1,0:T(8,128)(2,1)S(1)} %get-tuple-element.129), channel_id=1, source_target_pairs={{0,112},{16,0},{32,16},{48,32},{64,48},{80,64},{96,80},{112,96},{1... | collective-permute-start | bytes 737288 | tf_op jit(solution)/shard_map/ppermute | solution.py:25
  118.8 8.7 %collective-permute-start.15 = (bf16[80,1536]{1,0:T(8,128)(2,1)S(1)}, bf16[80,1536]{1,0:T(8,128)(2,1)S(1)}, u32[]{:S(2)}, u32[]{:S(2)}) collective-permute-start(bf16[80,1536]{1,0:T(8,128)(2,1)S(1)} %get-tuple-element.130), channel_id=1, source_target_pairs={{0,16},{16,32},{32,48},{48,64},{64,80},{80,96},{96,112},{112,0},{1... | collective-permute-start | bytes 737288 | tf_op jit(solution)/shard_map/ppermute | solution.py:25
  118.8 14.3 %collective-permute-start.19 = (bf16[2,80,1536]{2,1,0:T(8,128)(2,1)S(1)}, bf16[2,80,1536]{2,1,0:T(8,128)(2,1)S(1)}, u32[]{:S(2)}, u32[]{:S(2)}) collective-permute-start(bf16[2,80,1536]{2,1,0:T(8,128)(2,1)S(1)} %copy-done.13), channel_id=1, source_target_pairs={{0,128},{128,0},{1,129},{129,1},{2,130},{130,2},{3,131},{131,3},{4... | collective-permute-start | bytes 1474568 | tf_op jit(solution)/shard_map/ppermute | solution.py:29
  127.6 16.7 %copy-start.17 = (s32[16,2]{0,1:T(2,128)S(1)}, s32[16,2]{0,1:T(2,128)}, u32[]{:S(2)}) copy-start(s32[16,2]{0,1:T(2,128)} %param.12) | copy-start | bytes 388
  127.6 6.6 %collective-permute-start.17 = (bf16[80,1536]{1,0:T(8,128)(2,1)S(1)}, bf16[80,1536]{1,0:T(8,128)(2,1)S(1)}, u32[]{:S(2)}, u32[]{:S(2)}) collective-permute-start(bf16[80,1536]{1,0:T(8,128)(2,1)S(1)} %get-tuple-element.137), channel_id=1, source_target_pairs={{0,112},{16,0},{32,16},{48,32},{64,48},{80,64},{96,80},{112,96},{1... | collective-permute-start | bytes 737288 | tf_op jit(solution)/shard_map/ppermute | solution.py:25
  128.0 7.8 %collective-permute-start.18 = (bf16[80,1536]{1,0:T(8,128)(2,1)S(1)}, bf16[80,1536]{1,0:T(8,128)(2,1)S(1)}, u32[]{:S(2)}, u32[]{:S(2)}) collective-permute-start(bf16[80,1536]{1,0:T(8,128)(2,1)S(1)} %get-tuple-element.138), channel_id=1, source_target_pairs={{0,16},{16,32},{32,48},{48,64},{64,80},{80,96},{96,112},{112,0},{1... | collective-permute-start | bytes 737288 | tf_op jit(solution)/shard_map/ppermute | solution.py:25
  133.1 17.9 %collective-permute-start.22 = (bf16[80,1536]{1,0:T(8,128)(2,1)}, bf16[80,1536]{1,0:T(8,128)(2,1)}, u32[]{:S(2)}, u32[]{:S(2)}) collective-permute-start(bf16[80,1536]{1,0:T(8,128)(2,1)} %dynamic-slice_bitcast_fusion), channel_id=1, source_target_pairs={{0,128},{128,0},{1,129},{129,1},{2,130},{130,2},{3,131},{131,3},{4... | collective-permute-start | bytes 737288 | tf_op jit(solution)/shard_map/ppermute | solution.py:29
  136.7 14.3 %collective-permute-start.20 = (bf16[80,1536]{1,0:T(8,128)(2,1)}, bf16[80,1536]{1,0:T(8,128)(2,1)}, u32[]{:S(2)}, u32[]{:S(2)}) collective-permute-start(bf16[80,1536]{1,0:T(8,128)(2,1)} %get-tuple-element.144), channel_id=1, source_target_pairs={{0,112},{16,0},{32,16},{48,32},{64,48},{80,64},{96,80},{112,96},{1... | collective-permute-start | bytes 737288 | tf_op jit(solution)/shard_map/ppermute | solution.py:25
  137.2 13.8 %collective-permute-start.21 = (bf16[80,1536]{1,0:T(8,128)(2,1)}, bf16[80,1536]{1,0:T(8,128)(2,1)}, u32[]{:S(2)}, u32[]{:S(2)}) collective-permute-start(bf16[80,1536]{1,0:T(8,128)(2,1)} %get-tuple-element.145), channel_id=1, source_target_pairs={{0,16},{16,32},{32,48},{48,64},{64,80},{80,96},{96,112},{112,0},{1... | collective-permute-start | bytes 737288 | tf_op jit(solution)/shard_map/ppermute | solution.py:25
  138.8 12.2 %all-to-all-start = ((bf16[8,16,768]{2,1,0:T(8,128)(2,1)}), bf16[8,16,768]{2,1,0:T(8,128)(2,1)S(1)}, u32[]{:S(2)}, u32[]{:S(2)}) async-start(bf16[8,16,768]{2,1,0:T(8,128)(2,1)} %bitcast.32), calls=%async_computation | async-start | bytes 393216 | tf_op jit(solution)/shard_map/all_to_all | solution.py:297
  152.1 6.3 %collective-permute-start.23 = (bf16[80,1536]{1,0:T(8,128)(2,1)S(1)}, bf16[80,1536]{1,0:T(8,128)(2,1)S(1)}, u32[]{:S(2)}, u32[]{:S(2)}) collective-permute-start(bf16[80,1536]{1,0:T(8,128)(2,1)S(1)} %fusion.2), channel_id=1, source_target_pairs={{0,112},{16,0},{32,16},{48,32},{64,48},{80,64},{96,80},{112,96},{1... | collective-permute-start | bytes 737288 | tf_op jit(solution)/shard_map/ppermute | solution.py:25
  160.5 18.1 %all-to-all-start.1 = ((bf16[16,5,3072]{2,1,0:T(8,128)(2,1)}), bf16[16,5,3072]{2,1,0:T(8,128)(2,1)S(1)}, u32[]{:S(2)}, u32[]{:S(2)}) async-start(bf16[16,5,3072]{2,1,0:T(8,128)(2,1)} %reshape.66), calls=%async_computation.1 | async-start | bytes 1572864 | tf_op jit(solution)/shard_map/all_to_all | solution.py:316
  (14 other events, 101.6 us)
Sparse Core Ops, SparseCore 0:
  32.2 40.2 all-gather.1

commit v5 on v4

--- a/solution.py
+++ b/solution.py
@@ -256,34 +256,32 @@
     here = after(place, block)
     down, up = shift(down, -1), shift(up, 1)
     down_term, up_term = first_terms(here, (2, 3))
-    sent = make(
-        after(place, down_term), 1, (1, Z), [lambda i, s: (1 - s[0], 0)], [ORDER[k : k + 2] for k in (0, 2, 4, 6)]
-    )
-    down, up, down_term, up_term, pair, *sent = join(down, up, down_term, up_term, pair, *sent)
+    down, up, down_term, up_term, pair = join(down, up, down_term, up_term, pair)
     down, up = add(down, down_term), add(up, up_term)
-    down, up, sent[0] = join(down, up, sent[0])
+    down, up = join(down, up)
 
     here = after(place, down)
     down, up = shift(down, -1), shift(up, 1)
+    sent = list(make(here, 1, (1, Z), [lambda i, s: (1 - s[0], 0)], [ORDER[k : k + 2] for k in (0, 2, 4, 6)]))
     got = [swap(sent[0], "yh")]
-    terms = first_terms(here, (4, 5, 6, 7))
-    down, up, *terms = join(down, up, *terms)
+    terms = first_terms(after(place, sent[0]), (4, 5, 6, 7))
+    down, up, got[0], *terms = join(down, up, got[0], *terms)
     down, up = add(down, terms[0]), add(up, terms[1])
     down, up, sent[1] = join(down, up, sent[1])
 
     here = after(place, down)
     down, up = shift(down, -1), shift(up, 1)
-    got.append(swap(after(sent[1], got[0]), "yh"))
+    got.append(swap(sent[1], "yh"))
     (kept,) = make(here, 1, (1, Z), [lambda i, s: (s[0], 0)], [ORDER])
-    down, up, near, kept, got[0] = join(down, up, near, kept, got[0])
+    down, up, near, kept, got[1] = join(down, up, near, kept, got[1])
     down = add(down, terms[2])
     down, sent[2], near = join(down, sent[2], near)
 
     near = near.reshape(2 * Z, -1, near.shape[-1])
     down = shift(down, -1)
-    got.append(swap(after(sent[2], got[1]), "yh"))
+    got.append(swap(sent[2], "yh"))
     context = attend(place, queries, doc_ids, near, swap(near, "c"))
-    down, context, got[1] = join(down, context, got[1])
+    down, context, got[2] = join(down, context, got[2])
     first = add(down, up, terms[3])
 
     def second_term(order):
@@ -293,9 +291,9 @@
     down, up = add(*second_term(0)), add(*second_term(1))
     down, up, going, sent[3] = join(down, up, going, sent[3])
     down, up = shift(down, -1), shift(up, 1)
-    got.append(swap(after(sent[3], got[2]), "yh"))
+    got.append(swap(sent[3], "yh"))
     residual = lax.all_to_all(context, EXP, split_axis=0, concat_axis=1, tiled=True)
-    down, up, got[2] = join(down, up, got[2])
+    down, up = join(down, up)
     down, up = add(down, *second_term(2)), add(up, *second_term(3))
     down, up, going = join(down, up, going)
     down, up, moved = shift(down, -1), shift(up, 1), swap(after(going, got[3]), "yh")

time: 189 us -> 177 us (0.937)
  waiting for transfers between devices: 76.5 us -> 65 us
    ppermute x10, waiting for transfers between devices: 17.4 us -> 5.49 us  [swap(): return lax.ppermute(value, axis, [(0, 1), (1, 0)])]
    ppermute x10, starting transfers between devices: 6.96 us -> 5.03 us  [swap(): return lax.ppermute(value, axis, [(0, 1), (1, 0)])]
  transfers between devices with their start and end apart: 27 -> 27, of which waited for: 16 -> 16; matrix products, arithmetic and copies ran while one was open for 6% -> 5% of each run, Pallas kernels for 18% -> 20%
where the time goes in v5:
time: 177 us; the launch traced here: 176 us
  waiting for transfers between devices  65 us (37%)
  starting transfers between devices  37.9 us (21%)
  Pallas kernels  37.9 us (21%)
  other arithmetic  15.3 us (9%)
  between operations  14.3 us (8%)
  local copies, waits for them, and re-layouts  5.35 us (3%)
    ppermute x14, waiting for transfers between devices, shift(): return lax.ppermute(value, 'z', [(i, (i + step) % Z) for i in range(Z)])  39 us
    ppermute x14, starting transfers between devices, shift(): return lax.ppermute(value, 'z', [(i, (i + step) % Z) for i in range(Z)])  24 us
    pallas_call x5, Pallas kernels, product(): pl.pallas_call(lambda *refs: product_kernel(len(picks), offsets, *refs),...  21.3 us
    all_to_all x1, waiting for transfers between devices, shards(): lax.all_to_all(rows, ('c',) + EXP, split_axis=0, concat_axis=0, tiled=True)  14.4 us
    convert_element_type x11, other arithmetic, add(): return total.astype(jnp.bfloat16)  13.5 us
    pallas_call x1, Pallas kernels, attend(): pl.pallas_call(lambda *refs: attention_kernel(head, *refs), out_shape=jax...  9.66 us
    pallas_call x2, Pallas kernels, other_columns(): pl.pallas_call(slice_kernel, out_shape=jax.ShapeDtypeStruct((depth, colum...  6.89 us
    all_to_all x1, waiting for transfers between devices, shards(): lax.all_to_all(context, EXP, split_axis=0, concat_axis=1, tiled=True)  6.14 us
  transfers between devices with their start and end apart: 27, of which 16 were waited for; matrix products, arithmetic and copies ran while one was open for 5% of the time, Pallas kernels for 20%

profile of v5, /device:TPU:16, one launch (start us, length us, event | category | flops | bytes accessed | tf_op | source)
XLA Modules:
  0.0 176.1 jit_solution(17424532502779098262)
XLA Ops:
  7.3 2.8 %columns.2 = bf16[512,1536]{1,0:T(8,128)(2,1)S(1)} custom-call(s32[3]{0:T(128)S(1)} %pad_add_fusion.place.refs_0_, bf16[512,6144]{1,0:T(8,128)(2,1)} %bitcast.107), custom_call_target="tpu_custom_call" | custom-call | tf_op jit(solution)/shard_map/columns/pallas_call | solution.py:142
  10.7 4.1 %columns.3 = bf16[512,1536]{1,0:T(8,128)(2,1)} custom-call(s32[3]{0:T(128)S(1)} %pad_add_fusion.place.refs_0_, bf16[512,6144]{1,0:T(8,128)(2,1)} %bitcast.108), custom_call_target="tpu_custom_call" | custom-call | tf_op jit(solution)/shard_map/columns/pallas_call | solution.py:142
  15.6 3.9 %product.5 = (bf16[2,1,80,1536]{3,2,1,0:T(8,128)(2,1)}, bf16[2,1,80,1536]{3,2,1,0:T(8,128)(2,1)}) custom-call(s32[3]{0:T(128)S(1)} %pad_add_fusion.place.refs_0_, bf16[2,8,80,512]{3,2,1,0:T(8,128)(2,1)S(1)} %bitcast.78, bf16[2,8,80,512]{3,2,1,0:T(8,128)(2,1)S(1)} %bitcast.79, bf16[2,8,80,512]{3,2,1,0:T(8,128)(2,1)S(1)} %bitcast.88, ...), custom_call_target="tpu_custom_call" | custom-call | tf_op jit(solution)/shard_map/product/pallas_call | solution.py:198
  19.5 5.9 %collective-permute-start.2 = (bf16[2,80,1536]{2,1,0:T(8,128)(2,1)}, bf16[2,80,1536]{2,1,0:T(8,128)(2,1)}, u32[]{:S(2)}, u32[]{:S(2)}) collective-permute-start(bf16[2,80,1536]{2,1,0:T(8,128)(2,1)} %bitcast.7), channel_id=1, source_target_pairs={{0,112},{16,0},{32,16},{48,32},{64,48},{80,64},{96,80},{112,96},{1... | collective-permute-start | bytes 1474568 | tf_op jit(solution)/shard_map/ppermute | solution.py:25
  25.8 3.2 %product.6 = (bf16[2,1,80,1536]{3,2,1,0:T(8,128)(2,1)S(1)}, bf16[2,1,80,1536]{3,2,1,0:T(8,128)(2,1)S(1)}) custom-call(s32[3]{0:T(128)S(1)} %pad_add_fusion.place.refs_0_, bf16[2,8,80,512]{3,2,1,0:T(8,128)(2,1)S(1)} %bitcast.80, bf16[2,8,80,512]{3,2,1,0:T(8,128)(2,1)S(1)} %bitcast.81, bf16[2,8,80,512]{3,2,1,0:T(8,128)(2,1)S(1)} %bitcast.90, ...), custom_call_target="tpu_custom_call" | custom-call | tf_op jit(solution)/shard_map/product/pallas_call | solution.py:198
  32.0 4.6 %collective-permute-done.2 = bf16[2,80,1536]{2,1,0:T(8,128)(2,1)} collective-permute-done((bf16[2,80,1536]{2,1,0:T(8,128)(2,1)}, bf16[2,80,1536]{2,1,0:T(8,128)(2,1)}, u32[]{:S(2)}, u32[]{:S(2)}) %collective-permute-start.2) | collective-permute-done | bytes 491552 | tf_op jit(solution)/shard_map/ppermute | solution.py:25
  36.7 3.4 %collective-permute-done.3 = bf16[2,80,1536]{2,1,0:T(8,128)(2,1)} collective-permute-done((bf16[2,80,1536]{2,1,0:T(8,128)(2,1)}, bf16[2,80,1536]{2,1,0:T(8,128)(2,1)}, u32[]{:S(2)}, u32[]{:S(2)}) %collective-permute-start.3) | collective-permute-done | bytes 491552 | tf_op jit(solution)/shard_map/ppermute | solution.py:25
  40.1 1.6 add_convert_fusion.4
  42.0 1.7 collective-permute-start.6
  43.8 5.3 %product.7 = (bf16[2,80,1536]{2,1,0:T(8,128)(2,1)S(1)}, bf16[2,80,1536]{2,1,0:T(8,128)(2,1)}, bf16[2,80,1536]{2,1,0:T(8,128)(2,1)S(1)}, bf16[2,80,1536]{2,1,0:T(8,128)(2,1)S(1)}) custom-call(s32[3]{0:T(128)S(1)} %pad_add_fusion.place.refs_0_, bf16[2,8,80,512]{3,2,1,0:T(8,128)(2,1)S(1)} %bitcast.82, bf16[2,8,80,512]{3,2,1,0:T(8,128)(2,1)S(1)} %bitcast.92, ...), custom_call_target="tpu_custom_call" | custom-call | tf_op jit(solution)/shard_map/product/pallas_call | solution.py:198
  50.2 4.4 %product.8 = (bf16[2,1,80,1536]{3,2,1,0:T(8,128)(2,1)S(1)}, bf16[2,1,80,1536]{3,2,1,0:T(8,128)(2,1)S(1)}, bf16[2,1,80,1536]{3,2,1,0:T(8,128)(2,1)S(1)}, bf16[2,1,80,1536]{3,2,1,0:T(8,128)(2,1)S(1)}) custom-call(s32[3]{0:T(128)S(1)} %pad_add_fusion.place.refs_0_, bf16[2,8,80,512]{3,2,1,0:T(8,128)(2,1)S(1)} %bitcast.83, bf16[2,8,80,512]{3,2,1,0:T(8,128)(2,1)S(1)} %bitcast.84, ...), custom_call_target="tpu_custom_call" | custom-call | tf_op jit(solution)/shard_map/product/pallas_call | solution.py:198
  54.6 6.2 %collective-permute-done.5 = bf16[2,80,1536]{2,1,0:T(8,128)(2,1)S(1)} collective-permute-done((bf16[2,80,1536]{2,1,0:T(8,128)(2,1)S(1)}, bf16[2,80,1536]{2,1,0:T(8,128)(2,1)S(1)}, u32[]{:S(2)}, u32[]{:S(2)}) %collective-permute-start.5) | collective-permute-done | bytes 491552 | tf_op jit(solution)/shard_map/ppermute | solution.py:25
  60.7 2.8 %collective-permute-done.6 = bf16[2,80,1536]{2,1,0:T(8,128)(2,1)S(1)} collective-permute-done((bf16[2,80,1536]{2,1,0:T(8,128)(2,1)S(1)}, bf16[2,80,1536]{2,1,0:T(8,128)(2,1)S(1)}, u32[]{:S(2)}, u32[]{:S(2)}) %collective-permute-start.6) | collective-permute-done | bytes 491552 | tf_op jit(solution)/shard_map/ppermute | solution.py:25
  65.8 3.2 %collective-permute-start.9 = (bf16[2,80,1536]{2,1,0:T(8,128)(2,1)}, bf16[2,80,1536]{2,1,0:T(8,128)(2,1)}, u32[]{:S(2)}, u32[]{:S(2)}) collective-permute-start(bf16[2,80,1536]{2,1,0:T(8,128)(2,1)} %add_convert_fusion.3), channel_id=1, source_target_pairs={{0,112},{16,0},{32,16},{48,32},{64,48},{80,64},{96,80},{112,96},{1... | collective-permute-start | bytes 1474568 | tf_op jit(solution)/shard_map/ppermute | solution.py:25
  69.0 4.6 %product.9 = bf16[8,80,1536]{2,1,0:T(8,128)(2,1)S(1)} custom-call(s32[3]{0:T(128)S(1)} %pad_add_fusion.place.refs_0_, bf16[2,8,80,512]{3,2,1,0:T(8,128)(2,1)S(1)} %bitcast.87, bf16[2,8,80,512]{3,2,1,0:T(8,128)(2,1)S(1)} %bitcast.97, bf16[512,6144]{1,0:T(8,128)(2,1)} %bitcast.113, bf16[512,1536]{1,0:T(8,128)(2,1)} %collective-permute-done.7.refs_4_), custom_call_target="tpu_custom_call" | custom-call | tf_op jit(solution)/shard_map/product/pallas_call | solution.py:198
  75.0 4.5 %collective-permute-done.10 = bf16[2,80,1536]{2,1,0:T(8,128)(2,1)} collective-permute-done((bf16[2,80,1536]{2,1,0:T(8,128)(2,1)}, bf16[2,80,1536]{2,1,0:T(8,128)(2,1)}, u32[]{:S(2)}, u32[]{:S(2)}) %collective-permute-start.10) | collective-permute-done | bytes 491552 | tf_op jit(solution)/shard_map/ppermute | solution.py:25
  79.5 1.9 %add_convert_fusion.1 = bf16[2,80,1536]{2,1,0:T(8,128)(2,1)} fusion(bf16[2,80,1536]{2,1,0:T(8,128)(2,1)S(1)} %bitcast.100, bf16[2,80,1536]{2,1,0:T(8,128)(2,1)} %collective-permute-done.9), kind=kLoop, calls=%fused_computation.1 | loop fusion | flops 983040 | bytes 1474560 | tf_op jit(solution)/shard_map/convert_element_type | solution.py:222
  81.4 2.2 %collective-permute-start.12 = (bf16[2,80,1536]{2,1,0:T(8,128)(2,1)}, bf16[2,80,1536]{2,1,0:T(8,128)(2,1)}, u32[]{:S(2)}, u32[]{:S(2)}) collective-permute-start(bf16[2,80,1536]{2,1,0:T(8,128)(2,1)} %add_convert_fusion.1), channel_id=1, source_target_pairs={{0,112},{16,0},{32,16},{48,32},{64,48},{80,64},{96,80},{112,96},{1... | collective-permute-start | bytes 1474568 | tf_op jit(solution)/shard_map/ppermute | solution.py:25
  83.7 2.9 %collective-permute-start.14 = (bf16[2,80,1536]{2,1,0:T(8,128)(2,1)}, bf16[2,80,1536]{2,1,0:T(8,128)(2,1)S(1)}, u32[]{:S(2)}, u32[]{:S(2)}) collective-permute-start(bf16[2,80,1536]{2,1,0:T(8,128)(2,1)} %copy-done.13), channel_id=1, source_target_pairs={{0,128},{128,0},{1,129},{129,1},{2,130},{130,2},{3,131},{131,3},{4... | collective-permute-start | bytes 1474568 | tf_op jit(solution)/shard_map/ppermute | solution.py:29
  88.0 9.7 %attention.1 = bf16[128,768]{1,0:T(8,128)(2,1)} custom-call(s32[3]{0:T(128)S(1)} %pad_add_fusion.place.refs_0_, bf16[128,768]{1,0:T(8,128)(2,1)S(1)} %copy-done.9, s32[1,128]{1,0:T(1,128)S(1)} %bitcast.106, bf16[16,144,256]{2,1,0:T(8,128)(2,1)S(1)} %bitcast.99, bf16[16,144,256]{2,1,0:T(8,128)(2,1)S(1)} %collective-permute-done.13.refs_4_), custom_call_target="tpu_custom_call" | custom-call | tf_op jit(solution)/shard_map/attention/pallas_call | solution.py:118
  100.8 4.8 %collective-permute-start.15 = (bf16[80,1536]{1,0:T(8,128)(2,1)S(1)}, bf16[80,1536]{1,0:T(8,128)(2,1)S(1)}, u32[]{:S(2)}, u32[]{:S(2)}) collective-permute-start(bf16[80,1536]{1,0:T(8,128)(2,1)S(1)} %get-tuple-element.116), channel_id=1, source_target_pairs={{0,112},{16,0},{32,16},{48,32},{64,48},{80,64},{96,80},{112,96},{1... | collective-permute-start | bytes 737288 | tf_op jit(solution)/shard_map/ppermute | solution.py:25
  105.7 5.9 %collective-permute-done.15 = bf16[80,1536]{1,0:T(8,128)(2,1)S(1)} collective-permute-done((bf16[80,1536]{1,0:T(8,128)(2,1)S(1)}, bf16[80,1536]{1,0:T(8,128)(2,1)S(1)}, u32[]{:S(2)}, u32[]{:S(2)}) %collective-permute-start.15) | collective-permute-done | bytes 245792 | tf_op jit(solution)/shard_map/ppermute | solution.py:25
  111.6 3.4 %collective-permute-done.16 = bf16[80,1536]{1,0:T(8,128)(2,1)S(1)} collective-permute-done((bf16[80,1536]{1,0:T(8,128)(2,1)S(1)}, bf16[80,1536]{1,0:T(8,128)(2,1)S(1)}, u32[]{:S(2)}, u32[]{:S(2)}) %collective-permute-start.16) | collective-permute-done | bytes 245792 | tf_op jit(solution)/shard_map/ppermute | solution.py:25
  116.6 1.7 collective-permute-start.18
  118.4 2.2 %collective-permute-done.19 = bf16[2,80,1536]{2,1,0:T(8,128)(2,1)S(1)} collective-permute-done((bf16[2,80,1536]{2,1,0:T(8,128)(2,1)S(1)}, bf16[2,80,1536]{2,1,0:T(8,128)(2,1)S(1)}, u32[]{:S(2)}, u32[]{:S(2)}) %collective-permute-start.19) | collective-permute-done | bytes 491552 | tf_op jit(solution)/shard_map/ppermute | solution.py:29
  120.9 2.9 %collective-permute-done.17 = bf16[80,1536]{1,0:T(8,128)(2,1)S(1)} collective-permute-done((bf16[80,1536]{1,0:T(8,128)(2,1)S(1)}, bf16[80,1536]{1,0:T(8,128)(2,1)S(1)}, u32[]{:S(2)}, u32[]{:S(2)}) %collective-permute-start.17) | collective-permute-done | bytes 245792 | tf_op jit(solution)/shard_map/ppermute | solution.py:25
  126.6 1.7 collective-permute-start.21
  128.3 5.3 %all-to-all-start = ((bf16[8,16,768]{2,1,0:T(8,128)(2,1)}), bf16[8,16,768]{2,1,0:T(8,128)(2,1)S(1)}, u32[]{:S(2)}, u32[]{:S(2)}) async-start(bf16[8,16,768]{2,1,0:T(8,128)(2,1)} %bitcast.32), calls=%async_computation | async-start | bytes 393216 | tf_op jit(solution)/shard_map/all_to_all | solution.py:295
  134.1 6.1 %all-to-all-done = bf16[8,16,768]{2,1,0:T(8,128)(2,1)S(1)} async-done(((bf16[8,16,768]{2,1,0:T(8,128)(2,1)}), bf16[8,16,768]{2,1,0:T(8,128)(2,1)S(1)}, u32[]{:S(2)}, u32[]{:S(2)}) %all-to-all-start) | async-done | bytes 196640 | tf_op jit(solution)/shard_map/all_to_all | solution.py:295
  143.9 3.7 %collective-permute-done.23 = bf16[80,1536]{1,0:T(8,128)(2,1)S(1)} collective-permute-done((bf16[80,1536]{1,0:T(8,128)(2,1)S(1)}, bf16[80,1536]{1,0:T(8,128)(2,1)S(1)}, u32[]{:S(2)}, u32[]{:S(2)}) %collective-permute-start.23) | collective-permute-done | bytes 245792 | tf_op jit(solution)/shard_map/ppermute | solution.py:25
  149.9 3.6 %all-to-all-start.1 = ((bf16[16,5,3072]{2,1,0:T(8,128)(2,1)}), bf16[16,5,3072]{2,1,0:T(8,128)(2,1)S(1)}, u32[]{:S(2)}, u32[]{:S(2)}) async-start(bf16[16,5,3072]{2,1,0:T(8,128)(2,1)} %reshape.66), calls=%async_computation.1 | async-start | bytes 1572864 | tf_op jit(solution)/shard_map/all_to_all | solution.py:314
  153.6 14.4 %all-to-all-done.1 = bf16[16,5,3072]{2,1,0:T(8,128)(2,1)S(1)} async-done(((bf16[16,5,3072]{2,1,0:T(8,128)(2,1)}), bf16[16,5,3072]{2,1,0:T(8,128)(2,1)S(1)}, u32[]{:S(2)}, u32[]{:S(2)}) %all-to-all-start.1) | async-done | bytes 491552 | tf_op jit(solution)/shard_map/all_to_all | solution.py:314
  (100 shorter events, 27.1 us)
Async XLA Ops:
  7.2 67.8 %all-gather.2.cloned.1.call-start = ((), (), s32[]{:S(2)}) async-start(), calls=%async_computation.2 | async-start | bytes 1327104 | tf_op jit(solution)/shard_map/all_gather | solution.py:255
  10.1 5.4 %collective-permute-start.1 = (bf16[512,1536]{1,0:T(8,128)(2,1)S(1)}, bf16[512,1536]{1,0:T(8,128)(2,1)S(1)}, u32[]{:S(2)}, u32[]{:S(2)}) collective-permute-start(bf16[512,1536]{1,0:T(8,128)(2,1)S(1)} %columns.2), channel_id=1, source_target_pairs={{0,8},{8,0},{1,9},{9,1},{2,10},{10,2},{3,11},{11,3},{4,12},{12,4},... | collective-permute-start | bytes 4718600 | tf_op jit(solution)/shard_map/ppermute | solution.py:29
  10.2 5.3 %collective-permute-start = (bf16[1280,512]{1,0:T(8,128)(2,1)S(1)}, bf16[1280,512]{1,0:T(8,128)(2,1)S(1)}, u32[]{:S(2)}, u32[]{:S(2)}) collective-permute-start(bf16[1280,512]{1,0:T(8,128)(2,1)S(1)} %bitcast.77), channel_id=1, source_target_pairs={{0,8},{8,0},{1,9},{9,1},{2,10},{10,2},{3,11},{11,3},{4,12},{12,4},... | collective-permute-start | bytes 3932168 | tf_op jit(solution)/shard_map/ppermute | solution.py:29
  15.5 28.3 %collective-permute-start.7 = (bf16[512,1536]{1,0:T(8,128)(2,1)}, bf16[512,1536]{1,0:T(8,128)(2,1)}, u32[]{:S(2)}, u32[]{:S(2)}) collective-permute-start(bf16[512,1536]{1,0:T(8,128)(2,1)} %columns.3), channel_id=1, source_target_pairs={{0,8},{8,0},{1,9},{9,1},{2,10},{10,2},{3,11},{11,3},{4,12},{12,4},... | collective-permute-start | bytes 4718600 | tf_op jit(solution)/shard_map/ppermute | solution.py:29
  19.5 17.2 %collective-permute-start.2 = (bf16[2,80,1536]{2,1,0:T(8,128)(2,1)}, bf16[2,80,1536]{2,1,0:T(8,128)(2,1)}, u32[]{:S(2)}, u32[]{:S(2)}) collective-permute-start(bf16[2,80,1536]{2,1,0:T(8,128)(2,1)} %bitcast.7), channel_id=1, source_target_pairs={{0,112},{16,0},{32,16},{48,32},{64,48},{80,64},{96,80},{112,96},{1... | collective-permute-start | bytes 1474568 | tf_op jit(solution)/shard_map/ppermute | solution.py:25
  25.4 14.7 %collective-permute-start.3 = (bf16[2,80,1536]{2,1,0:T(8,128)(2,1)}, bf16[2,80,1536]{2,1,0:T(8,128)(2,1)}, u32[]{:S(2)}, u32[]{:S(2)}) collective-permute-start(bf16[2,80,1536]{2,1,0:T(8,128)(2,1)} %bitcast.8), channel_id=1, source_target_pairs={{0,16},{16,32},{32,48},{48,64},{64,80},{80,96},{96,112},{112,0},{1... | collective-permute-start | bytes 1474568 | tf_op jit(solution)/shard_map/ppermute | solution.py:25
  25.4 5.9 %collective-permute-start.4 = (bf16[144,1,256]{2,0,1:T(8,128)(2,1)S(1)}, bf16[144,1,256]{2,0,1:T(8,128)(2,1)S(1)}, u32[]{:S(2)}, u32[]{:S(2)}) collective-permute-start(bf16[144,1,256]{2,0,1:T(8,128)(2,1)S(1)} %pad_maximum_fusion.2), channel_id=1, source_target_pairs={{0,128},{128,0},{1,129},{129,1},{2,130},{130,2},{3,131},{131,3},{4... | collective-permute-start | bytes 221192 | tf_op jit(solution)/shard_map/ppermute | solution.py:29
  41.7 19.1 %collective-permute-start.5 = (bf16[2,80,1536]{2,1,0:T(8,128)(2,1)S(1)}, bf16[2,80,1536]{2,1,0:T(8,128)(2,1)S(1)}, u32[]{:S(2)}, u32[]{:S(2)}) collective-permute-start(bf16[2,80,1536]{2,1,0:T(8,128)(2,1)S(1)} %get-tuple-element.83), channel_id=1, source_target_pairs={{0,112},{16,0},{32,16},{48,32},{64,48},{80,64},{96,80},{112,96},{1... | collective-permute-start | bytes 1474568 | tf_op jit(solution)/shard_map/ppermute | solution.py:25
  42.0 21.5 %collective-permute-start.6 = (bf16[2,80,1536]{2,1,0:T(8,128)(2,1)S(1)}, bf16[2,80,1536]{2,1,0:T(8,128)(2,1)S(1)}, u32[]{:S(2)}, u32[]{:S(2)}) collective-permute-start(bf16[2,80,1536]{2,1,0:T(8,128)(2,1)S(1)} %get-tuple-element.84), channel_id=1, source_target_pairs={{0,16},{16,32},{32,48},{48,64},{64,80},{80,96},{96,112},{112,0},{1... | collective-permute-start | bytes 1474568 | tf_op jit(solution)/shard_map/ppermute | solution.py:25
  49.8 13.7 %collective-permute-start.8 = (bf16[2,80,1536]{2,1,0:T(8,128)(2,1)S(1)}, bf16[2,80,1536]{2,1,0:T(8,128)(2,1)S(1)}, u32[]{:S(2)}, u32[]{:S(2)}) collective-permute-start(bf16[2,80,1536]{2,1,0:T(8,128)(2,1)S(1)} %get-tuple-element.87), channel_id=1, source_target_pairs={{0,128},{128,0},{1,129},{129,1},{2,130},{130,2},{3,131},{131,3},{4... | collective-permute-start | bytes 1474568 | tf_op jit(solution)/shard_map/ppermute | solution.py:29
  54.6 11.2 %copy-start.7 = (bf16[2,1,80,1536]{3,2,1,0:T(8,128)(2,1)}, bf16[2,1,80,1536]{3,2,1,0:T(8,128)(2,1)S(1)}, u32[]{:S(2)}) copy-start(bf16[2,1,80,1536]{3,2,1,0:T(8,128)(2,1)S(1)} %get-tuple-element.92) | copy-start | bytes 1474564
  65.4 14.0 %collective-permute-start.10 = (bf16[2,80,1536]{2,1,0:T(8,128)(2,1)}, bf16[2,80,1536]{2,1,0:T(8,128)(2,1)}, u32[]{:S(2)}, u32[]{:S(2)}) collective-permute-start(bf16[2,80,1536]{2,1,0:T(8,128)(2,1)} %add_convert_fusion.2), channel_id=1, source_target_pairs={{0,16},{16,32},{32,48},{48,64},{64,80},{80,96},{96,112},{112,0},{1... | collective-permute-start | bytes 1474568 | tf_op jit(solution)/shard_map/ppermute | solution.py:25
  65.4 14.0 %collective-permute-start.11 = (bf16[2,80,1536]{2,1,0:T(8,128)(2,1)}, bf16[2,80,1536]{2,1,0:T(8,128)(2,1)}, u32[]{:S(2)}, u32[]{:S(2)}) collective-permute-start(bf16[2,80,1536]{2,1,0:T(8,128)(2,1)} %get-tuple-element.101), channel_id=1, source_target_pairs={{0,128},{128,0},{1,129},{129,1},{2,130},{130,2},{3,131},{131,3},{4... | collective-permute-start | bytes 1474568 | tf_op jit(solution)/shard_map/ppermute | solution.py:29
  65.8 13.7 %collective-permute-start.9 = (bf16[2,80,1536]{2,1,0:T(8,128)(2,1)}, bf16[2,80,1536]{2,1,0:T(8,128)(2,1)}, u32[]{:S(2)}, u32[]{:S(2)}) collective-permute-start(bf16[2,80,1536]{2,1,0:T(8,128)(2,1)} %add_convert_fusion.3), channel_id=1, source_target_pairs={{0,112},{16,0},{32,16},{48,32},{64,48},{80,64},{96,80},{112,96},{1... | collective-permute-start | bytes 1474568 | tf_op jit(solution)/shard_map/ppermute | solution.py:25
  75.0 13.0 %copy-start.9 = (bf16[128,768]{1,0:T(8,128)(2,1)S(1)}, bf16[128,768]{1,0:T(8,128)(2,1)}, u32[]{:S(2)}) copy-start(bf16[128,768]{1,0:T(8,128)(2,1)} %refs_1_.1) | copy-start | bytes 589828
  75.0 13.0 %copy-start.5 = (bf16[2304,1,256]{2,0,1:T(8,128)(2,1)S(1)}, bf16[2304,1,256]{2,0,1:T(8,128)(2,1)}, u32[]{:S(2)}) copy-start(bf16[2304,1,256]{2,0,1:T(8,128)(2,1)} %all-gather.2.cloned.1.call-done) | copy-start | bytes 3538948
  81.4 6.5 %collective-permute-start.13 = (bf16[16,144,256]{2,1,0:T(8,128)(2,1)}, bf16[16,144,256]{2,1,0:T(8,128)(2,1)S(1)}, u32[]{:S(2)}, u32[]{:S(2)}) collective-permute-start(bf16[16,144,256]{2,1,0:T(8,128)(2,1)} %bitcast.98), channel_id=1, source_target_pairs={{0,8},{8,0},{1,9},{9,1},{2,10},{10,2},{3,11},{11,3},{4,12},{12,4},... | collective-permute-start | bytes 3538952 | tf_op jit(solution)/shard_map/ppermute | solution.py:29
  81.4 16.2 %collective-permute-start.12 = (bf16[2,80,1536]{2,1,0:T(8,128)(2,1)}, bf16[2,80,1536]{2,1,0:T(8,128)(2,1)}, u32[]{:S(2)}, u32[]{:S(2)}) collective-permute-start(bf16[2,80,1536]{2,1,0:T(8,128)(2,1)} %add_convert_fusion.1), channel_id=1, source_target_pairs={{0,112},{16,0},{32,16},{48,32},{64,48},{80,64},{96,80},{112,96},{1... | collective-permute-start | bytes 1474568 | tf_op jit(solution)/shard_map/ppermute | solution.py:25
  83.7 15.1 %collective-permute-start.14 = (bf16[2,80,1536]{2,1,0:T(8,128)(2,1)}, bf16[2,80,1536]{2,1,0:T(8,128)(2,1)S(1)}, u32[]{:S(2)}, u32[]{:S(2)}) collective-permute-start(bf16[2,80,1536]{2,1,0:T(8,128)(2,1)} %copy-done.13), channel_id=1, source_target_pairs={{0,128},{128,0},{1,129},{129,1},{2,130},{130,2},{3,131},{131,3},{4... | collective-permute-start | bytes 1474568 | tf_op jit(solution)/shard_map/ppermute | solution.py:29
  97.6 17.4 %copy-start.4 = (bf16[8,80,1536]{2,1,0:T(8,128)(2,1)S(1)}, bf16[8,80,1536]{2,1,0:T(8,128)(2,1)}, u32[]{:S(2)}) copy-start(bf16[8,80,1536]{2,1,0:T(8,128)(2,1)} %copy-done.3) | copy-start | bytes 5898244
  100.8 10.8 %collective-permute-start.15 = (bf16[80,1536]{1,0:T(8,128)(2,1)S(1)}, bf16[80,1536]{1,0:T(8,128)(2,1)S(1)}, u32[]{:S(2)}, u32[]{:S(2)}) collective-permute-start(bf16[80,1536]{1,0:T(8,128)(2,1)S(1)} %get-tuple-element.116), channel_id=1, source_target_pairs={{0,112},{16,0},{32,16},{48,32},{64,48},{80,64},{96,80},{112,96},{1... | collective-permute-start | bytes 737288 | tf_op jit(solution)/shard_map/ppermute | solution.py:25
  105.6 9.4 %collective-permute-start.16 = (bf16[80,1536]{1,0:T(8,128)(2,1)S(1)}, bf16[80,1536]{1,0:T(8,128)(2,1)S(1)}, u32[]{:S(2)}, u32[]{:S(2)}) collective-permute-start(bf16[80,1536]{1,0:T(8,128)(2,1)S(1)} %get-tuple-element.117), channel_id=1, source_target_pairs={{0,16},{16,32},{32,48},{48,64},{64,80},{80,96},{96,112},{112,0},{1... | collective-permute-start | bytes 737288 | tf_op jit(solution)/shard_map/ppermute | solution.py:25
  105.6 15.0 %collective-permute-start.19 = (bf16[2,80,1536]{2,1,0:T(8,128)(2,1)S(1)}, bf16[2,80,1536]{2,1,0:T(8,128)(2,1)S(1)}, u32[]{:S(2)}, u32[]{:S(2)}) collective-permute-start(bf16[2,80,1536]{2,1,0:T(8,128)(2,1)S(1)} %copy-done.12), channel_id=1, source_target_pairs={{0,128},{128,0},{1,129},{129,1},{2,130},{130,2},{3,131},{131,3},{4... | collective-permute-start | bytes 1474568 | tf_op jit(solution)/shard_map/ppermute | solution.py:29
  116.3 17.3 %copy-start.16 = (s32[16,2]{0,1:T(2,128)S(1)}, s32[16,2]{0,1:T(2,128)}, u32[]{:S(2)}) copy-start(s32[16,2]{0,1:T(2,128)} %param.12) | copy-start | bytes 388
  116.3 7.5 %collective-permute-start.17 = (bf16[80,1536]{1,0:T(8,128)(2,1)S(1)}, bf16[80,1536]{1,0:T(8,128)(2,1)S(1)}, u32[]{:S(2)}, u32[]{:S(2)}) collective-permute-start(bf16[80,1536]{1,0:T(8,128)(2,1)S(1)} %get-tuple-element.122), channel_id=1, source_target_pairs={{0,112},{16,0},{32,16},{48,32},{64,48},{80,64},{96,80},{112,96},{1... | collective-permute-start | bytes 737288 | tf_op jit(solution)/shard_map/ppermute | solution.py:25
  116.6 8.6 %collective-permute-start.18 = (bf16[80,1536]{1,0:T(8,128)(2,1)S(1)}, bf16[80,1536]{1,0:T(8,128)(2,1)S(1)}, u32[]{:S(2)}, u32[]{:S(2)}) collective-permute-start(bf16[80,1536]{1,0:T(8,128)(2,1)S(1)} %get-tuple-element.123), channel_id=1, source_target_pairs={{0,16},{16,32},{32,48},{48,64},{64,80},{80,96},{96,112},{112,0},{1... | collective-permute-start | bytes 737288 | tf_op jit(solution)/shard_map/ppermute | solution.py:25
  120.6 19.7 %collective-permute-start.22 = (bf16[80,1536]{1,0:T(8,128)(2,1)}, bf16[80,1536]{1,0:T(8,128)(2,1)}, u32[]{:S(2)}, u32[]{:S(2)}) collective-permute-start(bf16[80,1536]{1,0:T(8,128)(2,1)} %dynamic-slice_bitcast_fusion), channel_id=1, source_target_pairs={{0,128},{128,0},{1,129},{129,1},{2,130},{130,2},{3,131},{131,3},{4... | collective-permute-start | bytes 737288 | tf_op jit(solution)/shard_map/ppermute | solution.py:29
  126.3 14.0 %collective-permute-start.20 = (bf16[80,1536]{1,0:T(8,128)(2,1)}, bf16[80,1536]{1,0:T(8,128)(2,1)}, u32[]{:S(2)}, u32[]{:S(2)}) collective-permute-start(bf16[80,1536]{1,0:T(8,128)(2,1)} %get-tuple-element.128), channel_id=1, source_target_pairs={{0,112},{16,0},{32,16},{48,32},{64,48},{80,64},{96,80},{112,96},{1... | collective-permute-start | bytes 737288 | tf_op jit(solution)/shard_map/ppermute | solution.py:25
  126.6 13.8 %collective-permute-start.21 = (bf16[80,1536]{1,0:T(8,128)(2,1)}, bf16[80,1536]{1,0:T(8,128)(2,1)}, u32[]{:S(2)}, u32[]{:S(2)}) collective-permute-start(bf16[80,1536]{1,0:T(8,128)(2,1)} %get-tuple-element.129), channel_id=1, source_target_pairs={{0,16},{16,32},{32,48},{48,64},{64,80},{80,96},{96,112},{112,0},{1... | collective-permute-start | bytes 737288 | tf_op jit(solution)/shard_map/ppermute | solution.py:25
  128.3 12.0 %all-to-all-start = ((bf16[8,16,768]{2,1,0:T(8,128)(2,1)}), bf16[8,16,768]{2,1,0:T(8,128)(2,1)S(1)}, u32[]{:S(2)}, u32[]{:S(2)}) async-start(bf16[8,16,768]{2,1,0:T(8,128)(2,1)} %bitcast.32), calls=%async_computation | async-start | bytes 393216 | tf_op jit(solution)/shard_map/all_to_all | solution.py:295
  141.4 6.3 %collective-permute-start.23 = (bf16[80,1536]{1,0:T(8,128)(2,1)S(1)}, bf16[80,1536]{1,0:T(8,128)(2,1)S(1)}, u32[]{:S(2)}, u32[]{:S(2)}) collective-permute-start(bf16[80,1536]{1,0:T(8,128)(2,1)S(1)} %fusion.2), channel_id=1, source_target_pairs={{0,112},{16,0},{32,16},{48,32},{64,48},{80,64},{96,80},{112,96},{1... | collective-permute-start | bytes 737288 | tf_op jit(solution)/shard_map/ppermute | solution.py:25
  149.9 18.1 %all-to-all-start.1 = ((bf16[16,5,3072]{2,1,0:T(8,128)(2,1)}), bf16[16,5,3072]{2,1,0:T(8,128)(2,1)S(1)}, u32[]{:S(2)}, u32[]{:S(2)}) async-start(bf16[16,5,3072]{2,1,0:T(8,128)(2,1)} %reshape.66), calls=%async_computation.1 | async-start | bytes 1572864 | tf_op jit(solution)/shard_map/all_to_all | solution.py:314
  (13 other events, 77.9 us)
Sparse Core Ops, SparseCore 0:
  32.2 39.9 all-gather.1

commit v6 on v5

--- a/solution.py
+++ b/solution.py
@@ -237,9 +237,6 @@
     acts_other = swap(gate_up[0], "c")
     part = other_columns(place, weight, columns, 0)
     other = [swap(part, "c")]
-    part = other_columns(after(place, part), weight, columns, 1)
-    acts_other, other[0], part = join(acts_other, other[0], part)
-    other.append(swap(part, "c"))
     acts_other = acts_other.reshape(2, Z, -1, depth)
 
     def make(where, group, block, picks, offsets=None):
@@ -250,6 +247,7 @@
         return [term[:, 0] for term in make(where, 0, (2, 1), picks)]
 
     down, up = first_terms(place, (0, 1))
+    other.append(swap(other_columns(after(place, down), weight, columns, 1), "c"))
     block = key_block(keys_values, after(doc_ids, down))
     pair = jnp.concatenate([block, swap(block, "yh")], axis=0)
     near = lax.all_gather(pair, "z", axis=0, tiled=True)
@@ -262,48 +260,48 @@
 
     here = after(place, down)
     down, up = shift(down, -1), shift(up, 1)
-    sent = list(make(here, 1, (1, Z), [lambda i, s: (1 - s[0], 0)], [ORDER[k : k + 2] for k in (0, 2, 4, 6)]))
+    sent = list(make(here, 1, (1, Z), [lambda i, s: (1 - s[0], 0)], [ORDER[:4], ORDER[4:6], ORDER[6:]]))
     got = [swap(sent[0], "yh")]
     terms = first_terms(after(place, sent[0]), (4, 5, 6, 7))
-    down, up, got[0], *terms = join(down, up, got[0], *terms)
+    down, up, *terms = join(down, up, *terms)
     down, up = add(down, terms[0]), add(up, terms[1])
-    down, up, sent[1] = join(down, up, sent[1])
+    down, up = join(down, up)
 
     here = after(place, down)
     down, up = shift(down, -1), shift(up, 1)
-    got.append(swap(sent[1], "yh"))
     (kept,) = make(here, 1, (1, Z), [lambda i, s: (s[0], 0)], [ORDER])
-    down, up, near, kept, got[1] = join(down, up, near, kept, got[1])
+    down, up, near, kept, got[0] = join(down, up, near, kept, got[0])
     down = add(down, terms[2])
-    down, sent[2], near = join(down, sent[2], near)
+    down, sent[1], near = join(down, sent[1], near)
 
     near = near.reshape(2 * Z, -1, near.shape[-1])
     down = shift(down, -1)
-    got.append(swap(sent[2], "yh"))
+    got.append(swap(sent[1], "yh"))
     context = attend(place, queries, doc_ids, near, swap(near, "c"))
-    down, context, got[2] = join(down, context, got[2])
+    down, context = join(down, context)
     first = add(down, up, terms[3])
 
     def second_term(order):
-        return kept[order], got[order // 2][order % 2]
+        piece = 0 if order < 4 else order // 2 - 1
+        return kept[order], got[piece][order if order < 4 else order % 2]
 
     going = chunk_of(first, 1 - high)
     down, up = add(*second_term(0)), add(*second_term(1))
-    down, up, going, sent[3] = join(down, up, going, sent[3])
-    down, up = shift(down, -1), shift(up, 1)
-    got.append(swap(sent[3], "yh"))
+    down, up, going = join(down, up, going)
+    down, up, moved = shift(down, -1), shift(up, 1), swap(going, "yh")
     residual = lax.all_to_all(context, EXP, split_axis=0, concat_axis=1, tiled=True)
-    down, up = join(down, up)
+    down, up, got[1] = join(down, up, got[1])
     down, up = add(down, *second_term(2)), add(up, *second_term(3))
-    down, up, going = join(down, up, going)
-    down, up, moved = shift(down, -1), shift(up, 1), swap(after(going, got[3]), "yh")
-    down, up, got[3] = join(down, up, got[3])
+    down, up, sent[2] = join(down, up, sent[2])
+    down, up = shift(down, -1), shift(up, 1)
+    got.append(swap(sent[2], "yh"))
+    down, up, moved = join(down, up, moved)
     down, up = add(down, *second_term(4)), add(up, *second_term(5))
     down, up = join(down, up)
     down, up = shift(down, -1), shift(up, 1)
-    down, up, moved = join(down, up, moved)
+    down, up, got[2] = join(down, up, got[2])
     down = add(down, *second_term(6))
-    first = add(chunk_of(first, high), moved)
+    first = add(chunk_of(first, high), after(moved, residual))
     down, residual = join(shift(down, -1), residual)
     second = add(down, up, *second_term(7))
 

time: 177 us -> 172 us (0.972)
  starting transfers between devices: 37.9 us -> 35.2 us
    ppermute x10 -> x9, starting transfers between devices: 5.03 us -> 3.23 us  [swap(): return lax.ppermute(value, axis, [(0, 1), (1, 0)])]
    ppermute x10 -> x9, waiting for transfers between devices: 5.49 us -> 6.6 us  [swap(): return lax.ppermute(value, axis, [(0, 1), (1, 0)])]
  transfers between devices with their start and end apart: 27 -> 26, of which waited for: 16 -> 14; matrix products, arithmetic and copies ran while one was open for 5% -> 5% of each run, Pallas kernels for 20% -> 18%
where the time goes in v6:
time: 172 us
  waiting for transfers between devices  65 us (38%)
  Pallas kernels  38 us (22%)
  starting transfers between devices  35.2 us (20%)
  between operations  14.4 us (8%)
  other arithmetic  14 us (8%)
  local copies, waits for them, and re-layouts  4.7 us (3%)
    ppermute x14, waiting for transfers between devices, shift(): return lax.ppermute(value, 'z', [(i, (i + step) % Z) for i in range(Z)])  37.8 us
    ppermute x14, starting transfers between devices, shift(): return lax.ppermute(value, 'z', [(i, (i + step) % Z) for i in range(Z)])  23.5 us
    pallas_call x5, Pallas kernels, product(): pl.pallas_call(lambda *refs: product_kernel(len(picks), offsets, *refs),...  21.4 us
    all_to_all x1, waiting for transfers between devices, shards(): lax.all_to_all(rows, ('c',) + EXP, split_axis=0, concat_axis=0, tiled=True)  14.4 us
    convert_element_type x11, other arithmetic, add(): return total.astype(jnp.bfloat16)  12.2 us
    pallas_call x1, Pallas kernels, attend(): pl.pallas_call(lambda *refs: attention_kernel(head, *refs), out_shape=jax...  9.66 us
    pallas_call x2, Pallas kernels, other_columns(): pl.pallas_call(slice_kernel, out_shape=jax.ShapeDtypeStruct((depth, colum...  6.91 us
    ppermute x9, waiting for transfers between devices, swap(): return lax.ppermute(value, axis, [(0, 1), (1, 0)])  6.6 us
  transfers between devices with their start and end apart: 26, of which 14 were waited for; matrix products, arithmetic and copies ran while one was open for 5% of the time, Pallas kernels for 18%

profile of v6, /device:TPU:16, one launch (start us, length us, event | category | flops | bytes accessed | tf_op | source)
XLA Modules:
  0.0 171.5 jit_solution(8376141907296164713)
XLA Ops:
  7.3 2.8 %columns.2 = bf16[512,1536]{1,0:T(8,128)(2,1)S(1)} custom-call(s32[3]{0:T(128)S(1)} %pad_add_fusion.place.refs_0_, bf16[512,6144]{1,0:T(8,128)(2,1)} %bitcast.107), custom_call_target="tpu_custom_call" | custom-call | tf_op jit(solution)/shard_map/columns/pallas_call | solution.py:142
  10.7 4.8 %collective-permute-done = bf16[1280,512]{1,0:T(8,128)(2,1)S(1)} collective-permute-done((bf16[1280,512]{1,0:T(8,128)(2,1)S(1)}, bf16[1280,512]{1,0:T(8,128)(2,1)S(1)}, u32[]{:S(2)}, u32[]{:S(2)}) %collective-permute-start) | collective-permute-done | bytes 1310752 | tf_op jit(solution)/shard_map/ppermute | solution.py:29
  15.5 3.9 %product.5 = (bf16[2,1,80,1536]{3,2,1,0:T(8,128)(2,1)}, bf16[2,1,80,1536]{3,2,1,0:T(8,128)(2,1)}) custom-call(s32[3]{0:T(128)S(1)} %pad_add_fusion.place.refs_0_, bf16[2,8,80,512]{3,2,1,0:T(8,128)(2,1)S(1)} %bitcast.78, bf16[2,8,80,512]{3,2,1,0:T(8,128)(2,1)S(1)} %bitcast.79, bf16[2,8,80,512]{3,2,1,0:T(8,128)(2,1)S(1)} %bitcast.88, ...), custom_call_target="tpu_custom_call" | custom-call | tf_op jit(solution)/shard_map/product/pallas_call | solution.py:198
  19.4 5.9 %collective-permute-start.2 = (bf16[2,80,1536]{2,1,0:T(8,128)(2,1)}, bf16[2,80,1536]{2,1,0:T(8,128)(2,1)}, u32[]{:S(2)}, u32[]{:S(2)}) collective-permute-start(bf16[2,80,1536]{2,1,0:T(8,128)(2,1)} %bitcast.7), channel_id=1, source_target_pairs={{0,112},{16,0},{32,16},{48,32},{64,48},{80,64},{96,80},{112,96},{1... | collective-permute-start | bytes 1474568 | tf_op jit(solution)/shard_map/ppermute | solution.py:25
  25.2 4.1 %columns.3 = bf16[512,1536]{1,0:T(8,128)(2,1)} custom-call(s32[3]{0:T(128)S(1)} %pad_add_fusion.place.refs_0_, bf16[512,6144]{1,0:T(8,128)(2,1)} %bitcast.109), custom_call_target="tpu_custom_call" | custom-call | tf_op jit(solution)/shard_map/columns/pallas_call | solution.py:142
  29.8 3.2 %product.6 = (bf16[2,1,80,1536]{3,2,1,0:T(8,128)(2,1)S(1)}, bf16[2,1,80,1536]{3,2,1,0:T(8,128)(2,1)S(1)}) custom-call(s32[3]{0:T(128)S(1)} %pad_add_fusion.place.refs_0_, bf16[2,8,80,512]{3,2,1,0:T(8,128)(2,1)S(1)} %bitcast.80, bf16[2,8,80,512]{3,2,1,0:T(8,128)(2,1)S(1)} %bitcast.81, bf16[2,8,80,512]{3,2,1,0:T(8,128)(2,1)S(1)} %bitcast.90, ...), custom_call_target="tpu_custom_call" | custom-call | tf_op jit(solution)/shard_map/product/pallas_call | solution.py:198
  33.9 1.8 %collective-permute-done.4 = bf16[144,1,256]{2,0,1:T(8,128)(2,1)S(1)} collective-permute-done((bf16[144,1,256]{2,0,1:T(8,128)(2,1)S(1)}, bf16[144,1,256]{2,0,1:T(8,128)(2,1)S(1)}, u32[]{:S(2)}, u32[]{:S(2)}) %collective-permute-start.4) | collective-permute-done | bytes 73760 | tf_op jit(solution)/shard_map/ppermute | solution.py:29
  36.4 3.3 %collective-permute-done.3 = bf16[2,80,1536]{2,1,0:T(8,128)(2,1)} collective-permute-done((bf16[2,80,1536]{2,1,0:T(8,128)(2,1)}, bf16[2,80,1536]{2,1,0:T(8,128)(2,1)}, u32[]{:S(2)}, u32[]{:S(2)}) %collective-permute-start.3) | collective-permute-done | bytes 491552 | tf_op jit(solution)/shard_map/ppermute | solution.py:25
  39.7 1.6 add_convert_fusion.4
  41.7 1.7 %collective-permute-start.6 = (bf16[2,80,1536]{2,1,0:T(8,128)(2,1)S(1)}, bf16[2,80,1536]{2,1,0:T(8,128)(2,1)S(1)}, u32[]{:S(2)}, u32[]{:S(2)}) collective-permute-start(bf16[2,80,1536]{2,1,0:T(8,128)(2,1)S(1)} %get-tuple-element.74), channel_id=1, source_target_pairs={{0,16},{16,32},{32,48},{48,64},{64,80},{80,96},{96,112},{112,0},{1... | collective-permute-start | bytes 1474568 | tf_op jit(solution)/shard_map/ppermute | solution.py:25
  43.4 5.3 %product.7 = (bf16[4,80,1536]{2,1,0:T(8,128)(2,1)}, bf16[2,80,1536]{2,1,0:T(8,128)(2,1)S(1)}, bf16[2,80,1536]{2,1,0:T(8,128)(2,1)S(1)}) custom-call(s32[3]{0:T(128)S(1)} %pad_add_fusion.place.refs_0_, bf16[2,8,80,512]{3,2,1,0:T(8,128)(2,1)S(1)} %bitcast.82, bf16[2,8,80,512]{3,2,1,0:T(8,128)(2,1)S(1)} %bitcast.92, bf16[512,6144]{1,0:T(8,128)(2,1)} %bitcast.111, ...), custom_call_target="tpu_custom_call" | custom-call | tf_op jit(solution)/shard_map/product/pallas_call | solution.py:198
  49.9 4.4 %product.8 = (bf16[2,1,80,1536]{3,2,1,0:T(8,128)(2,1)S(1)}, bf16[2,1,80,1536]{3,2,1,0:T(8,128)(2,1)S(1)}, bf16[2,1,80,1536]{3,2,1,0:T(8,128)(2,1)S(1)}, bf16[2,1,80,1536]{3,2,1,0:T(8,128)(2,1)S(1)}) custom-call(s32[3]{0:T(128)S(1)} %pad_add_fusion.place.refs_0_, bf16[2,8,80,512]{3,2,1,0:T(8,128)(2,1)S(1)} %bitcast.83, bf16[2,8,80,512]{3,2,1,0:T(8,128)(2,1)S(1)} %bitcast.84, ...), custom_call_target="tpu_custom_call" | custom-call | tf_op jit(solution)/shard_map/product/pallas_call | solution.py:198
  54.3 2.6 %collective-permute-done.5 = bf16[2,80,1536]{2,1,0:T(8,128)(2,1)S(1)} collective-permute-done((bf16[2,80,1536]{2,1,0:T(8,128)(2,1)S(1)}, bf16[2,80,1536]{2,1,0:T(8,128)(2,1)S(1)}, u32[]{:S(2)}, u32[]{:S(2)}) %collective-permute-start.5) | collective-permute-done | bytes 491552 | tf_op jit(solution)/shard_map/ppermute | solution.py:25
  56.9 2.4 %collective-permute-done.6 = bf16[2,80,1536]{2,1,0:T(8,128)(2,1)S(1)} collective-permute-done((bf16[2,80,1536]{2,1,0:T(8,128)(2,1)S(1)}, bf16[2,80,1536]{2,1,0:T(8,128)(2,1)S(1)}, u32[]{:S(2)}, u32[]{:S(2)}) %collective-permute-start.6) | collective-permute-done | bytes 491552 | tf_op jit(solution)/shard_map/ppermute | solution.py:25
  59.6 2.0 %collective-permute-start.9 = (bf16[2,80,1536]{2,1,0:T(8,128)(2,1)S(1)}, bf16[2,80,1536]{2,1,0:T(8,128)(2,1)}, u32[]{:S(2)}, u32[]{:S(2)}) collective-permute-start(bf16[2,80,1536]{2,1,0:T(8,128)(2,1)S(1)} %add_convert_fusion.2), channel_id=1, source_target_pairs={{0,16},{16,32},{32,48},{48,64},{64,80},{80,96},{96,112},{112,0},{1... | collective-permute-start | bytes 1474568 | tf_op jit(solution)/shard_map/ppermute | solution.py:25
  61.6 4.6 %product.9 = bf16[8,80,1536]{2,1,0:T(8,128)(2,1)S(1)} custom-call(s32[3]{0:T(128)S(1)} %pad_add_fusion.place.refs_0_, bf16[2,8,80,512]{3,2,1,0:T(8,128)(2,1)S(1)} %bitcast.87, bf16[2,8,80,512]{3,2,1,0:T(8,128)(2,1)S(1)} %bitcast.97, bf16[512,6144]{1,0:T(8,128)(2,1)} %bitcast.113, bf16[512,1536]{1,0:T(8,128)(2,1)} %collective-permute-done.7.refs_4_), custom_call_target="tpu_custom_call" | custom-call | tf_op jit(solution)/shard_map/product/pallas_call | solution.py:198
  67.5 8.8 %collective-permute-done.8 = bf16[2,80,1536]{2,1,0:T(8,128)(2,1)} collective-permute-done((bf16[2,80,1536]{2,1,0:T(8,128)(2,1)S(1)}, bf16[2,80,1536]{2,1,0:T(8,128)(2,1)}, u32[]{:S(2)}, u32[]{:S(2)}) %collective-permute-start.8) | collective-permute-done | bytes 491552 | tf_op jit(solution)/shard_map/ppermute | solution.py:25
  77.1 2.0 %add_convert_fusion.1 = bf16[2,80,1536]{2,1,0:T(8,128)(2,1)} fusion(bf16[2,80,1536]{2,1,0:T(8,128)(2,1)S(1)} %bitcast.100, bf16[2,80,1536]{2,1,0:T(8,128)(2,1)} %collective-permute-done.8), kind=kLoop, calls=%fused_computation.1 | loop fusion | flops 983040 | bytes 1474560 | tf_op jit(solution)/shard_map/convert_element_type | solution.py:222
  79.2 2.0 %collective-permute-start.11 = (bf16[2,80,1536]{2,1,0:T(8,128)(2,1)}, bf16[2,80,1536]{2,1,0:T(8,128)(2,1)S(1)}, u32[]{:S(2)}, u32[]{:S(2)}) collective-permute-start(bf16[2,80,1536]{2,1,0:T(8,128)(2,1)} %add_convert_fusion.1), channel_id=1, source_target_pairs={{0,112},{16,0},{32,16},{48,32},{64,48},{80,64},{96,80},{112,96},{1... | collective-permute-start | bytes 1474568 | tf_op jit(solution)/shard_map/ppermute | solution.py:25
  81.2 1.9 %collective-permute-start.15 = (bf16[2,80,1536]{2,1,0:T(8,128)(2,1)}, bf16[2,80,1536]{2,1,0:T(8,128)(2,1)S(1)}, u32[]{:S(2)}, u32[]{:S(2)}) collective-permute-start(bf16[2,80,1536]{2,1,0:T(8,128)(2,1)} %copy-done.13), channel_id=1, source_target_pairs={{0,128},{128,0},{1,129},{129,1},{2,130},{130,2},{3,131},{131,3},{4... | collective-permute-start | bytes 1474568 | tf_op jit(solution)/shard_map/ppermute | solution.py:29
  84.5 9.7 %attention.1 = bf16[128,768]{1,0:T(8,128)(2,1)} custom-call(s32[3]{0:T(128)S(1)} %pad_add_fusion.place.refs_0_, bf16[128,768]{1,0:T(8,128)(2,1)S(1)} %copy-done.9, s32[1,128]{1,0:T(1,128)S(1)} %bitcast.106, bf16[16,144,256]{2,1,0:T(8,128)(2,1)S(1)} %bitcast.99, bf16[16,144,256]{2,1,0:T(8,128)(2,1)S(1)} %collective-permute-done.12.refs_4_), custom_call_target="tpu_custom_call" | custom-call | tf_op jit(solution)/shard_map/attention/pallas_call | solution.py:118
  95.6 5.8 %collective-permute-start.13 = (bf16[80,1536]{1,0:T(8,128)(2,1)S(1)}, bf16[80,1536]{1,0:T(8,128)(2,1)S(1)}, u32[]{:S(2)}, u32[]{:S(2)}) collective-permute-start(bf16[80,1536]{1,0:T(8,128)(2,1)S(1)} %get-tuple-element.102), channel_id=1, source_target_pairs={{0,112},{16,0},{32,16},{48,32},{64,48},{80,64},{96,80},{112,96},{1... | collective-permute-start | bytes 737288 | tf_op jit(solution)/shard_map/ppermute | solution.py:25
  101.3 6.0 %collective-permute-done.13 = bf16[80,1536]{1,0:T(8,128)(2,1)S(1)} collective-permute-done((bf16[80,1536]{1,0:T(8,128)(2,1)S(1)}, bf16[80,1536]{1,0:T(8,128)(2,1)S(1)}, u32[]{:S(2)}, u32[]{:S(2)}) %collective-permute-start.13) | collective-permute-done | bytes 245792 | tf_op jit(solution)/shard_map/ppermute | solution.py:25
  107.4 3.4 %collective-permute-done.14 = bf16[80,1536]{1,0:T(8,128)(2,1)S(1)} collective-permute-done((bf16[80,1536]{1,0:T(8,128)(2,1)S(1)}, bf16[80,1536]{1,0:T(8,128)(2,1)S(1)}, u32[]{:S(2)}, u32[]{:S(2)}) %collective-permute-start.14) | collective-permute-done | bytes 245792 | tf_op jit(solution)/shard_map/ppermute | solution.py:25
  112.4 1.7 %collective-permute-start.17 = (bf16[80,1536]{1,0:T(8,128)(2,1)S(1)}, bf16[80,1536]{1,0:T(8,128)(2,1)S(1)}, u32[]{:S(2)}, u32[]{:S(2)}) collective-permute-start(bf16[80,1536]{1,0:T(8,128)(2,1)S(1)} %get-tuple-element.109), channel_id=1, source_target_pairs={{0,16},{16,32},{32,48},{48,64},{64,80},{80,96},{96,112},{112,0},{1... | collective-permute-start | bytes 737288 | tf_op jit(solution)/shard_map/ppermute | solution.py:25
  114.1 5.4 %collective-permute-done.16 = bf16[80,1536]{1,0:T(8,128)(2,1)S(1)} collective-permute-done((bf16[80,1536]{1,0:T(8,128)(2,1)S(1)}, bf16[80,1536]{1,0:T(8,128)(2,1)S(1)}, u32[]{:S(2)}, u32[]{:S(2)}) %collective-permute-start.16) | collective-permute-done | bytes 245792 | tf_op jit(solution)/shard_map/ppermute | solution.py:25
  122.2 1.7 %collective-permute-start.20 = (bf16[80,1536]{1,0:T(8,128)(2,1)}, bf16[80,1536]{1,0:T(8,128)(2,1)}, u32[]{:S(2)}, u32[]{:S(2)}) collective-permute-start(bf16[80,1536]{1,0:T(8,128)(2,1)} %get-tuple-element.115), channel_id=1, source_target_pairs={{0,16},{16,32},{32,48},{48,64},{64,80},{80,96},{96,112},{112,0},{1... | collective-permute-start | bytes 737288 | tf_op jit(solution)/shard_map/ppermute | solution.py:25
  124.0 4.8 %all-to-all-start = ((bf16[8,16,768]{2,1,0:T(8,128)(2,1)}), bf16[8,16,768]{2,1,0:T(8,128)(2,1)S(1)}, u32[]{:S(2)}, u32[]{:S(2)}) async-start(bf16[8,16,768]{2,1,0:T(8,128)(2,1)} %bitcast.32), calls=%async_computation | async-start | bytes 393216 | tf_op jit(solution)/shard_map/all_to_all | solution.py:292
  129.3 6.1 %all-to-all-done = bf16[8,16,768]{2,1,0:T(8,128)(2,1)S(1)} async-done(((bf16[8,16,768]{2,1,0:T(8,128)(2,1)}), bf16[8,16,768]{2,1,0:T(8,128)(2,1)S(1)}, u32[]{:S(2)}, u32[]{:S(2)}) %all-to-all-start) | async-done | bytes 196640 | tf_op jit(solution)/shard_map/all_to_all | solution.py:292
  139.2 3.7 %collective-permute-done.22 = bf16[80,1536]{1,0:T(8,128)(2,1)S(1)} collective-permute-done((bf16[80,1536]{1,0:T(8,128)(2,1)S(1)}, bf16[80,1536]{1,0:T(8,128)(2,1)S(1)}, u32[]{:S(2)}, u32[]{:S(2)}) %collective-permute-start.22) | collective-permute-done | bytes 245792 | tf_op jit(solution)/shard_map/ppermute | solution.py:25
  145.3 3.6 %all-to-all-start.1 = ((bf16[16,5,3072]{2,1,0:T(8,128)(2,1)}), bf16[16,5,3072]{2,1,0:T(8,128)(2,1)S(1)}, u32[]{:S(2)}, u32[]{:S(2)}) async-start(bf16[16,5,3072]{2,1,0:T(8,128)(2,1)} %reshape.66), calls=%async_computation.1 | async-start | bytes 1572864 | tf_op jit(solution)/shard_map/all_to_all | solution.py:312
  149.0 14.4 %all-to-all-done.1 = bf16[16,5,3072]{2,1,0:T(8,128)(2,1)S(1)} async-done(((bf16[16,5,3072]{2,1,0:T(8,128)(2,1)}), bf16[16,5,3072]{2,1,0:T(8,128)(2,1)S(1)}, u32[]{:S(2)}, u32[]{:S(2)}) %all-to-all-start.1) | async-done | bytes 491552 | tf_op jit(solution)/shard_map/all_to_all | solution.py:312
  (98 shorter events, 21.7 us)
Async XLA Ops:
  7.2 70.0 %all-gather.2.cloned.1.call-start = ((), (), s32[]{:S(2)}) async-start(), calls=%async_computation.2 | async-start | bytes 1327104 | tf_op jit(solution)/shard_map/all_gather | solution.py:253
  10.1 5.4 %collective-permute-start.1 = (bf16[512,1536]{1,0:T(8,128)(2,1)S(1)}, bf16[512,1536]{1,0:T(8,128)(2,1)S(1)}, u32[]{:S(2)}, u32[]{:S(2)}) collective-permute-start(bf16[512,1536]{1,0:T(8,128)(2,1)S(1)} %columns.2), channel_id=1, source_target_pairs={{0,8},{8,0},{1,9},{9,1},{2,10},{10,2},{3,11},{11,3},{4,12},{12,4},... | collective-permute-start | bytes 4718600 | tf_op jit(solution)/shard_map/ppermute | solution.py:29
  10.2 5.3 %collective-permute-start = (bf16[1280,512]{1,0:T(8,128)(2,1)S(1)}, bf16[1280,512]{1,0:T(8,128)(2,1)S(1)}, u32[]{:S(2)}, u32[]{:S(2)}) collective-permute-start(bf16[1280,512]{1,0:T(8,128)(2,1)S(1)} %bitcast.77), channel_id=1, source_target_pairs={{0,8},{8,0},{1,9},{9,1},{2,10},{10,2},{3,11},{11,3},{4,12},{12,4},... | collective-permute-start | bytes 3932168 | tf_op jit(solution)/shard_map/ppermute | solution.py:29
  15.4 14.4 %copy-start.1 = (bf16[512,1536]{1,0:T(8,128)(2,1)}, bf16[512,1536]{1,0:T(8,128)(2,1)S(1)}, u32[]{:S(2)}) copy-start(bf16[512,1536]{1,0:T(8,128)(2,1)S(1)} %collective-permute-done.1.refs_6_.refs_10_) | copy-start | bytes 4718596
  19.4 17.0 %collective-permute-start.2 = (bf16[2,80,1536]{2,1,0:T(8,128)(2,1)}, bf16[2,80,1536]{2,1,0:T(8,128)(2,1)}, u32[]{:S(2)}, u32[]{:S(2)}) collective-permute-start(bf16[2,80,1536]{2,1,0:T(8,128)(2,1)} %bitcast.7), channel_id=1, source_target_pairs={{0,112},{16,0},{32,16},{48,32},{64,48},{80,64},{96,80},{112,96},{1... | collective-permute-start | bytes 1474568 | tf_op jit(solution)/shard_map/ppermute | solution.py:25
  25.2 14.5 %collective-permute-start.3 = (bf16[2,80,1536]{2,1,0:T(8,128)(2,1)}, bf16[2,80,1536]{2,1,0:T(8,128)(2,1)}, u32[]{:S(2)}, u32[]{:S(2)}) collective-permute-start(bf16[2,80,1536]{2,1,0:T(8,128)(2,1)} %bitcast.8), channel_id=1, source_target_pairs={{0,16},{16,32},{32,48},{48,64},{64,80},{80,96},{96,112},{112,0},{1... | collective-permute-start | bytes 1474568 | tf_op jit(solution)/shard_map/ppermute | solution.py:25
  29.4 14.1 %collective-permute-start.7 = (bf16[512,1536]{1,0:T(8,128)(2,1)}, bf16[512,1536]{1,0:T(8,128)(2,1)}, u32[]{:S(2)}, u32[]{:S(2)}) collective-permute-start(bf16[512,1536]{1,0:T(8,128)(2,1)} %columns.3), channel_id=1, source_target_pairs={{0,8},{8,0},{1,9},{9,1},{2,10},{10,2},{3,11},{11,3},{4,12},{12,4},... | collective-permute-start | bytes 4718600 | tf_op jit(solution)/shard_map/ppermute | solution.py:29
  29.4 6.3 %collective-permute-start.4 = (bf16[144,1,256]{2,0,1:T(8,128)(2,1)S(1)}, bf16[144,1,256]{2,0,1:T(8,128)(2,1)S(1)}, u32[]{:S(2)}, u32[]{:S(2)}) collective-permute-start(bf16[144,1,256]{2,0,1:T(8,128)(2,1)S(1)} %pad_maximum_fusion.2), channel_id=1, source_target_pairs={{0,128},{128,0},{1,129},{129,1},{2,130},{130,2},{3,131},{131,3},{4... | collective-permute-start | bytes 221192 | tf_op jit(solution)/shard_map/ppermute | solution.py:29
  41.3 15.5 %collective-permute-start.5 = (bf16[2,80,1536]{2,1,0:T(8,128)(2,1)S(1)}, bf16[2,80,1536]{2,1,0:T(8,128)(2,1)S(1)}, u32[]{:S(2)}, u32[]{:S(2)}) collective-permute-start(bf16[2,80,1536]{2,1,0:T(8,128)(2,1)S(1)} %get-tuple-element.73), channel_id=1, source_target_pairs={{0,112},{16,0},{32,16},{48,32},{64,48},{80,64},{96,80},{112,96},{1... | collective-permute-start | bytes 1474568 | tf_op jit(solution)/shard_map/ppermute | solution.py:25
  41.7 17.6 %collective-permute-start.6 = (bf16[2,80,1536]{2,1,0:T(8,128)(2,1)S(1)}, bf16[2,80,1536]{2,1,0:T(8,128)(2,1)S(1)}, u32[]{:S(2)}, u32[]{:S(2)}) collective-permute-start(bf16[2,80,1536]{2,1,0:T(8,128)(2,1)S(1)} %get-tuple-element.74), channel_id=1, source_target_pairs={{0,16},{16,32},{32,48},{48,64},{64,80},{80,96},{96,112},{112,0},{1... | collective-permute-start | bytes 1474568 | tf_op jit(solution)/shard_map/ppermute | solution.py:25
  49.5 27.6 %collective-permute-start.10 = (bf16[4,80,1536]{2,1,0:T(8,128)(2,1)}, bf16[4,80,1536]{2,1,0:T(8,128)(2,1)}, u32[]{:S(2)}, u32[]{:S(2)}) collective-permute-start(bf16[4,80,1536]{2,1,0:T(8,128)(2,1)} %get-tuple-element.77), channel_id=1, source_target_pairs={{0,128},{128,0},{1,129},{129,1},{2,130},{130,2},{3,131},{131,3},{4... | collective-permute-start | bytes 2949128 | tf_op jit(solution)/shard_map/ppermute | solution.py:29
  59.5 16.9 %collective-permute-start.8 = (bf16[2,80,1536]{2,1,0:T(8,128)(2,1)S(1)}, bf16[2,80,1536]{2,1,0:T(8,128)(2,1)}, u32[]{:S(2)}, u32[]{:S(2)}) collective-permute-start(bf16[2,80,1536]{2,1,0:T(8,128)(2,1)S(1)} %add_convert_fusion.3), channel_id=1, source_target_pairs={{0,112},{16,0},{32,16},{48,32},{64,48},{80,64},{96,80},{112,96},{1... | collective-permute-start | bytes 1474568 | tf_op jit(solution)/shard_map/ppermute | solution.py:25
  59.6 17.5 %collective-permute-start.9 = (bf16[2,80,1536]{2,1,0:T(8,128)(2,1)S(1)}, bf16[2,80,1536]{2,1,0:T(8,128)(2,1)}, u32[]{:S(2)}, u32[]{:S(2)}) collective-permute-start(bf16[2,80,1536]{2,1,0:T(8,128)(2,1)S(1)} %add_convert_fusion.2), channel_id=1, source_target_pairs={{0,16},{16,32},{32,48},{48,64},{64,80},{80,96},{96,112},{112,0},{1... | collective-permute-start | bytes 1474568 | tf_op jit(solution)/shard_map/ppermute | solution.py:25
  67.5 16.9 %copy-start.9 = (bf16[128,768]{1,0:T(8,128)(2,1)S(1)}, bf16[128,768]{1,0:T(8,128)(2,1)}, u32[]{:S(2)}) copy-start(bf16[128,768]{1,0:T(8,128)(2,1)} %refs_1_.1) | copy-start | bytes 589828
  79.2 5.3 %collective-permute-start.12 = (bf16[16,144,256]{2,1,0:T(8,128)(2,1)}, bf16[16,144,256]{2,1,0:T(8,128)(2,1)S(1)}, u32[]{:S(2)}, u32[]{:S(2)}) collective-permute-start(bf16[16,144,256]{2,1,0:T(8,128)(2,1)} %bitcast.98), channel_id=1, source_target_pairs={{0,8},{8,0},{1,9},{9,1},{2,10},{10,2},{3,11},{11,3},{4,12},{12,4},... | collective-permute-start | bytes 3538952 | tf_op jit(solution)/shard_map/ppermute | solution.py:29
  79.2 15.0 %collective-permute-start.11 = (bf16[2,80,1536]{2,1,0:T(8,128)(2,1)}, bf16[2,80,1536]{2,1,0:T(8,128)(2,1)S(1)}, u32[]{:S(2)}, u32[]{:S(2)}) collective-permute-start(bf16[2,80,1536]{2,1,0:T(8,128)(2,1)} %add_convert_fusion.1), channel_id=1, source_target_pairs={{0,112},{16,0},{32,16},{48,32},{64,48},{80,64},{96,80},{112,96},{1... | collective-permute-start | bytes 1474568 | tf_op jit(solution)/shard_map/ppermute | solution.py:25
  81.2 20.2 %collective-permute-start.15 = (bf16[2,80,1536]{2,1,0:T(8,128)(2,1)}, bf16[2,80,1536]{2,1,0:T(8,128)(2,1)S(1)}, u32[]{:S(2)}, u32[]{:S(2)}) collective-permute-start(bf16[2,80,1536]{2,1,0:T(8,128)(2,1)} %copy-done.13), channel_id=1, source_target_pairs={{0,128},{128,0},{1,129},{129,1},{2,130},{130,2},{3,131},{131,3},{4... | collective-permute-start | bytes 1474568 | tf_op jit(solution)/shard_map/ppermute | solution.py:29
  84.5 9.7 %copy-start.8 = (bf16[2,1,80,1536]{3,2,1,0:T(8,128)(2,1)S(1)}, bf16[2,1,80,1536]{3,2,1,0:T(8,128)(2,1)}, u32[]{:S(2)}) copy-start(bf16[2,1,80,1536]{3,2,1,0:T(8,128)(2,1)} %copy-done.7) | copy-start | bytes 1474564
  94.2 16.6 %copy-start.4 = (bf16[8,80,1536]{2,1,0:T(8,128)(2,1)S(1)}, bf16[8,80,1536]{2,1,0:T(8,128)(2,1)}, u32[]{:S(2)}) copy-start(bf16[8,80,1536]{2,1,0:T(8,128)(2,1)} %copy-done.3) | copy-start | bytes 5898244
  95.5 18.6 %copy-start.12 = (bf16[2,80,1536]{2,1,0:T(8,128)(2,1)S(1)}, bf16[2,80,1536]{2,1,0:T(8,128)(2,1)}, u32[]{:S(2)}) copy-start(bf16[2,80,1536]{2,1,0:T(8,128)(2,1)} %copy-done.11) | copy-start | bytes 1474564
  95.6 11.8 %collective-permute-start.13 = (bf16[80,1536]{1,0:T(8,128)(2,1)S(1)}, bf16[80,1536]{1,0:T(8,128)(2,1)S(1)}, u32[]{:S(2)}, u32[]{:S(2)}) collective-permute-start(bf16[80,1536]{1,0:T(8,128)(2,1)S(1)} %get-tuple-element.102), channel_id=1, source_target_pairs={{0,112},{16,0},{32,16},{48,32},{64,48},{80,64},{96,80},{112,96},{1... | collective-permute-start | bytes 737288 | tf_op jit(solution)/shard_map/ppermute | solution.py:25
  101.3 9.4 %collective-permute-start.14 = (bf16[80,1536]{1,0:T(8,128)(2,1)S(1)}, bf16[80,1536]{1,0:T(8,128)(2,1)S(1)}, u32[]{:S(2)}, u32[]{:S(2)}) collective-permute-start(bf16[80,1536]{1,0:T(8,128)(2,1)S(1)} %get-tuple-element.103), channel_id=1, source_target_pairs={{0,16},{16,32},{32,48},{48,64},{64,80},{80,96},{96,112},{112,0},{1... | collective-permute-start | bytes 737288 | tf_op jit(solution)/shard_map/ppermute | solution.py:25
  101.3 12.8 %collective-permute-start.18 = (bf16[80,1536]{1,0:T(8,128)(2,1)S(1)}, bf16[80,1536]{1,0:T(8,128)(2,1)S(1)}, u32[]{:S(2)}, u32[]{:S(2)}) collective-permute-start(bf16[80,1536]{1,0:T(8,128)(2,1)S(1)} %dynamic-slice_bitcast_fusion), channel_id=1, source_target_pairs={{0,128},{128,0},{1,129},{129,1},{2,130},{130,2},{3,131},{131,3},{4... | collective-permute-start | bytes 737288 | tf_op jit(solution)/shard_map/ppermute | solution.py:29
  112.0 16.8 %copy-start.16 = (s32[16,2]{0,1:T(2,128)S(1)}, s32[16,2]{0,1:T(2,128)}, u32[]{:S(2)}) copy-start(s32[16,2]{0,1:T(2,128)} %param.12) | copy-start | bytes 388
  112.0 7.5 %collective-permute-start.16 = (bf16[80,1536]{1,0:T(8,128)(2,1)S(1)}, bf16[80,1536]{1,0:T(8,128)(2,1)S(1)}, u32[]{:S(2)}, u32[]{:S(2)}) collective-permute-start(bf16[80,1536]{1,0:T(8,128)(2,1)S(1)} %get-tuple-element.108), channel_id=1, source_target_pairs={{0,112},{16,0},{32,16},{48,32},{64,48},{80,64},{96,80},{112,96},{1... | collective-permute-start | bytes 737288 | tf_op jit(solution)/shard_map/ppermute | solution.py:25
  112.4 8.6 %collective-permute-start.17 = (bf16[80,1536]{1,0:T(8,128)(2,1)S(1)}, bf16[80,1536]{1,0:T(8,128)(2,1)S(1)}, u32[]{:S(2)}, u32[]{:S(2)}) collective-permute-start(bf16[80,1536]{1,0:T(8,128)(2,1)S(1)} %get-tuple-element.109), channel_id=1, source_target_pairs={{0,16},{16,32},{32,48},{48,64},{64,80},{80,96},{96,112},{112,0},{1... | collective-permute-start | bytes 737288 | tf_op jit(solution)/shard_map/ppermute | solution.py:25
  114.1 21.4 %collective-permute-start.21 = (bf16[2,80,1536]{2,1,0:T(8,128)(2,1)S(1)}, bf16[2,80,1536]{2,1,0:T(8,128)(2,1)}, u32[]{:S(2)}, u32[]{:S(2)}) collective-permute-start(bf16[2,80,1536]{2,1,0:T(8,128)(2,1)S(1)} %copy-done.12), channel_id=1, source_target_pairs={{0,128},{128,0},{1,129},{129,1},{2,130},{130,2},{3,131},{131,3},{4... | collective-permute-start | bytes 1474568 | tf_op jit(solution)/shard_map/ppermute | solution.py:29
  121.9 13.5 %collective-permute-start.19 = (bf16[80,1536]{1,0:T(8,128)(2,1)}, bf16[80,1536]{1,0:T(8,128)(2,1)}, u32[]{:S(2)}, u32[]{:S(2)}) collective-permute-start(bf16[80,1536]{1,0:T(8,128)(2,1)} %get-tuple-element.114), channel_id=1, source_target_pairs={{0,112},{16,0},{32,16},{48,32},{64,48},{80,64},{96,80},{112,96},{1... | collective-permute-start | bytes 737288 | tf_op jit(solution)/shard_map/ppermute | solution.py:25
  122.2 13.3 %collective-permute-start.20 = (bf16[80,1536]{1,0:T(8,128)(2,1)}, bf16[80,1536]{1,0:T(8,128)(2,1)}, u32[]{:S(2)}, u32[]{:S(2)}) collective-permute-start(bf16[80,1536]{1,0:T(8,128)(2,1)} %get-tuple-element.115), channel_id=1, source_target_pairs={{0,16},{16,32},{32,48},{48,64},{64,80},{80,96},{96,112},{112,0},{1... | collective-permute-start | bytes 737288 | tf_op jit(solution)/shard_map/ppermute | solution.py:25
  124.0 11.5 %all-to-all-start = ((bf16[8,16,768]{2,1,0:T(8,128)(2,1)}), bf16[8,16,768]{2,1,0:T(8,128)(2,1)S(1)}, u32[]{:S(2)}, u32[]{:S(2)}) async-start(bf16[8,16,768]{2,1,0:T(8,128)(2,1)} %bitcast.32), calls=%async_computation | async-start | bytes 393216 | tf_op jit(solution)/shard_map/all_to_all | solution.py:292
  136.7 6.3 %collective-permute-start.22 = (bf16[80,1536]{1,0:T(8,128)(2,1)S(1)}, bf16[80,1536]{1,0:T(8,128)(2,1)S(1)}, u32[]{:S(2)}, u32[]{:S(2)}) collective-permute-start(bf16[80,1536]{1,0:T(8,128)(2,1)S(1)} %fusion.2), channel_id=1, source_target_pairs={{0,112},{16,0},{32,16},{48,32},{64,48},{80,64},{96,80},{112,96},{1... | collective-permute-start | bytes 737288 | tf_op jit(solution)/shard_map/ppermute | solution.py:25
  145.3 18.1 %all-to-all-start.1 = ((bf16[16,5,3072]{2,1,0:T(8,128)(2,1)}), bf16[16,5,3072]{2,1,0:T(8,128)(2,1)S(1)}, u32[]{:S(2)}, u32[]{:S(2)}) async-start(bf16[16,5,3072]{2,1,0:T(8,128)(2,1)} %reshape.66), calls=%async_computation.1 | async-start | bytes 1572864 | tf_op jit(solution)/shard_map/all_to_all | solution.py:312
  (12 other events, 52.6 us)
Sparse Core Ops, SparseCore 0:
  36.5 40.2 all-gather.1

commit v7 on v6

--- a/solution.py
+++ b/solution.py
@@ -288,18 +288,21 @@
     going = chunk_of(first, 1 - high)
     down, up = add(*second_term(0)), add(*second_term(1))
     down, up, going = join(down, up, going)
-    down, up, moved = shift(down, -1), shift(up, 1), swap(going, "yh")
+    down, up = shift(down, -1), shift(up, 1)
+    last = jnp.concatenate([sent[2], going[None]], axis=0)
     residual = lax.all_to_all(context, EXP, split_axis=0, concat_axis=1, tiled=True)
     down, up, got[1] = join(down, up, got[1])
     down, up = add(down, *second_term(2)), add(up, *second_term(3))
-    down, up, sent[2] = join(down, up, sent[2])
-    down, up = shift(down, -1), shift(up, 1)
-    got.append(swap(sent[2], "yh"))
-    down, up, moved = join(down, up, moved)
+    down, up, last = join(down, up, last)
+    down, up = shift(down, -1), shift(up, 1)
+    last = swap(last, "yh")
+    down, up = join(down, up)
     down, up = add(down, *second_term(4)), add(up, *second_term(5))
     down, up = join(down, up)
     down, up = shift(down, -1), shift(up, 1)
-    down, up, got[2] = join(down, up, got[2])
+    down, up, last = join(down, up, last)
+    got.append(last[:2])
+    moved = last[2]
     down = add(down, *second_term(6))
     first = add(chunk_of(first, high), after(moved, residual))
     down, residual = join(shift(down, -1), residual)

time: 172 us -> 176 us (1.023)
    ppermute x9 -> x8, starting transfers between devices: 3.23 us -> 3.86 us  [swap(): return lax.ppermute(value, axis, [(0, 1), (1, 0)])]
    ppermute x9 -> x8, waiting for transfers between devices: 6.6 us -> 6.61 us  [swap(): return lax.ppermute(value, axis, [(0, 1), (1, 0)])]
  transfers between devices with their start and end apart: 26 -> 25, of which waited for: 14 -> 14; matrix products, arithmetic and copies ran while one was open for 5% -> 5% of each run, Pallas kernels for 18% -> 18%
where the time goes in v7:
time: 176 us; the launch traced here: 174 us
  waiting for transfers between devices  65.1 us (37%)
  Pallas kernels  37.9 us (22%)
  starting transfers between devices  36.9 us (21%)
  between operations  14.4 us (8%)
  other arithmetic  14.1 us (8%)
  local copies, waits for them, and re-layouts  5.66 us (3%)
    ppermute x14, waiting for transfers between devices, shift(): return lax.ppermute(value, 'z', [(i, (i + step) % Z) for i in range(Z)])  37.9 us
    ppermute x14, starting transfers between devices, shift(): return lax.ppermute(value, 'z', [(i, (i + step) % Z) for i in range(Z)])  23.6 us
    pallas_call x5, Pallas kernels, product(): pl.pallas_call(lambda *refs: product_kernel(len(picks), offsets, *refs),...  21.4 us
    all_to_all x1, waiting for transfers between devices, shards(): lax.all_to_all(rows, ('c',) + EXP, split_axis=0, concat_axis=0, tiled=True)  14.4 us
    convert_element_type x11, other arithmetic, add(): return total.astype(jnp.bfloat16)  11.3 us
    pallas_call x1, Pallas kernels, attend(): pl.pallas_call(lambda *refs: attention_kernel(head, *refs), out_shape=jax...  9.64 us
    pallas_call x2, Pallas kernels, other_columns(): pl.pallas_call(slice_kernel, out_shape=jax.ShapeDtypeStruct((depth, colum...  6.91 us
    ppermute x8, waiting for transfers between devices, swap(): return lax.ppermute(value, axis, [(0, 1), (1, 0)])  6.61 us
  transfers between devices with their start and end apart: 25, of which 14 were waited for; matrix products, arithmetic and copies ran while one was open for 5% of the time, Pallas kernels for 18%

profile of v7, /device:TPU:16, one launch (start us, length us, event | category | flops | bytes accessed | tf_op | source)
XLA Modules:
  0.0 174.3 jit_solution(5221920617864125751)
XLA Ops:
  7.3 2.8 %columns.2 = bf16[512,1536]{1,0:T(8,128)(2,1)S(1)} custom-call(s32[3]{0:T(128)S(1)} %pad_add_fusion.place.refs_0_, bf16[512,6144]{1,0:T(8,128)(2,1)} %bitcast.110), custom_call_target="tpu_custom_call" | custom-call | tf_op jit(solution)/shard_map/columns/pallas_call | solution.py:142
  10.7 4.8 %collective-permute-done = bf16[1280,512]{1,0:T(8,128)(2,1)S(1)} collective-permute-done((bf16[1280,512]{1,0:T(8,128)(2,1)S(1)}, bf16[1280,512]{1,0:T(8,128)(2,1)S(1)}, u32[]{:S(2)}, u32[]{:S(2)}) %collective-permute-start) | collective-permute-done | bytes 1310752 | tf_op jit(solution)/shard_map/ppermute | solution.py:29
  15.5 3.9 %product.5 = (bf16[2,1,80,1536]{3,2,1,0:T(8,128)(2,1)}, bf16[2,1,80,1536]{3,2,1,0:T(8,128)(2,1)}) custom-call(s32[3]{0:T(128)S(1)} %pad_add_fusion.place.refs_0_, bf16[2,8,80,512]{3,2,1,0:T(8,128)(2,1)S(1)} %bitcast.81, bf16[2,8,80,512]{3,2,1,0:T(8,128)(2,1)S(1)} %bitcast.82, bf16[2,8,80,512]{3,2,1,0:T(8,128)(2,1)S(1)} %bitcast.91, ...), custom_call_target="tpu_custom_call" | custom-call | tf_op jit(solution)/shard_map/product/pallas_call | solution.py:198
  19.4 5.9 %collective-permute-start.2 = (bf16[2,80,1536]{2,1,0:T(8,128)(2,1)}, bf16[2,80,1536]{2,1,0:T(8,128)(2,1)}, u32[]{:S(2)}, u32[]{:S(2)}) collective-permute-start(bf16[2,80,1536]{2,1,0:T(8,128)(2,1)} %bitcast.7), channel_id=1, source_target_pairs={{0,112},{16,0},{32,16},{48,32},{64,48},{80,64},{96,80},{112,96},{1... | collective-permute-start | bytes 1474568 | tf_op jit(solution)/shard_map/ppermute | solution.py:25
  25.2 4.1 %columns.3 = bf16[512,1536]{1,0:T(8,128)(2,1)} custom-call(s32[3]{0:T(128)S(1)} %pad_add_fusion.place.refs_0_, bf16[512,6144]{1,0:T(8,128)(2,1)} %bitcast.112), custom_call_target="tpu_custom_call" | custom-call | tf_op jit(solution)/shard_map/columns/pallas_call | solution.py:142
  29.8 3.2 %product.6 = (bf16[2,1,80,1536]{3,2,1,0:T(8,128)(2,1)S(1)}, bf16[2,1,80,1536]{3,2,1,0:T(8,128)(2,1)S(1)}) custom-call(s32[3]{0:T(128)S(1)} %pad_add_fusion.place.refs_0_, bf16[2,8,80,512]{3,2,1,0:T(8,128)(2,1)S(1)} %bitcast.83, bf16[2,8,80,512]{3,2,1,0:T(8,128)(2,1)S(1)} %bitcast.84, bf16[2,8,80,512]{3,2,1,0:T(8,128)(2,1)S(1)} %bitcast.93, ...), custom_call_target="tpu_custom_call" | custom-call | tf_op jit(solution)/shard_map/product/pallas_call | solution.py:198
  33.9 1.8 %collective-permute-done.4 = bf16[144,1,256]{2,0,1:T(8,128)(2,1)S(1)} collective-permute-done((bf16[144,1,256]{2,0,1:T(8,128)(2,1)S(1)}, bf16[144,1,256]{2,0,1:T(8,128)(2,1)S(1)}, u32[]{:S(2)}, u32[]{:S(2)}) %collective-permute-start.4) | collective-permute-done | bytes 73760 | tf_op jit(solution)/shard_map/ppermute | solution.py:29
  36.4 3.3 %collective-permute-done.3 = bf16[2,80,1536]{2,1,0:T(8,128)(2,1)} collective-permute-done((bf16[2,80,1536]{2,1,0:T(8,128)(2,1)}, bf16[2,80,1536]{2,1,0:T(8,128)(2,1)}, u32[]{:S(2)}, u32[]{:S(2)}) %collective-permute-start.3) | collective-permute-done | bytes 491552 | tf_op jit(solution)/shard_map/ppermute | solution.py:25
  39.7 1.6 add_convert_fusion.4
  41.7 1.7 %collective-permute-start.6 = (bf16[2,80,1536]{2,1,0:T(8,128)(2,1)S(1)}, bf16[2,80,1536]{2,1,0:T(8,128)(2,1)S(1)}, u32[]{:S(2)}, u32[]{:S(2)}) collective-permute-start(bf16[2,80,1536]{2,1,0:T(8,128)(2,1)S(1)} %get-tuple-element.73), channel_id=1, source_target_pairs={{0,16},{16,32},{32,48},{48,64},{64,80},{80,96},{96,112},{112,0},{1... | collective-permute-start | bytes 1474568 | tf_op jit(solution)/shard_map/ppermute | solution.py:25
  43.4 5.3 %product.7 = (bf16[4,80,1536]{2,1,0:T(8,128)(2,1)}, bf16[2,80,1536]{2,1,0:T(8,128)(2,1)S(1)}, bf16[2,80,1536]{2,1,0:T(8,128)(2,1)S(1)}) custom-call(s32[3]{0:T(128)S(1)} %pad_add_fusion.place.refs_0_, bf16[2,8,80,512]{3,2,1,0:T(8,128)(2,1)S(1)} %bitcast.85, bf16[2,8,80,512]{3,2,1,0:T(8,128)(2,1)S(1)} %bitcast.95, bf16[512,6144]{1,0:T(8,128)(2,1)} %bitcast.114, ...), custom_call_target="tpu_custom_call" | custom-call | tf_op jit(solution)/shard_map/product/pallas_call | solution.py:198
  49.1 4.4 %product.8 = (bf16[2,1,80,1536]{3,2,1,0:T(8,128)(2,1)S(1)}, bf16[2,1,80,1536]{3,2,1,0:T(8,128)(2,1)S(1)}, bf16[2,1,80,1536]{3,2,1,0:T(8,128)(2,1)S(1)}, bf16[2,1,80,1536]{3,2,1,0:T(8,128)(2,1)S(1)}) custom-call(s32[3]{0:T(128)S(1)} %pad_add_fusion.place.refs_0_, bf16[2,8,80,512]{3,2,1,0:T(8,128)(2,1)S(1)} %bitcast.86, bf16[2,8,80,512]{3,2,1,0:T(8,128)(2,1)S(1)} %bitcast.87, ...), custom_call_target="tpu_custom_call" | custom-call | tf_op jit(solution)/shard_map/product/pallas_call | solution.py:198
  53.5 3.4 %collective-permute-done.5 = bf16[2,80,1536]{2,1,0:T(8,128)(2,1)S(1)} collective-permute-done((bf16[2,80,1536]{2,1,0:T(8,128)(2,1)S(1)}, bf16[2,80,1536]{2,1,0:T(8,128)(2,1)S(1)}, u32[]{:S(2)}, u32[]{:S(2)}) %collective-permute-start.5) | collective-permute-done | bytes 491552 | tf_op jit(solution)/shard_map/ppermute | solution.py:25
  56.9 2.4 %collective-permute-done.6 = bf16[2,80,1536]{2,1,0:T(8,128)(2,1)S(1)} collective-permute-done((bf16[2,80,1536]{2,1,0:T(8,128)(2,1)S(1)}, bf16[2,80,1536]{2,1,0:T(8,128)(2,1)S(1)}, u32[]{:S(2)}, u32[]{:S(2)}) %collective-permute-start.6) | collective-permute-done | bytes 491552 | tf_op jit(solution)/shard_map/ppermute | solution.py:25
  59.6 2.0 %collective-permute-start.9 = (bf16[2,80,1536]{2,1,0:T(8,128)(2,1)S(1)}, bf16[2,80,1536]{2,1,0:T(8,128)(2,1)}, u32[]{:S(2)}, u32[]{:S(2)}) collective-permute-start(bf16[2,80,1536]{2,1,0:T(8,128)(2,1)S(1)} %add_convert_fusion.2), channel_id=1, source_target_pairs={{0,16},{16,32},{32,48},{48,64},{64,80},{80,96},{96,112},{112,0},{1... | collective-permute-start | bytes 1474568 | tf_op jit(solution)/shard_map/ppermute | solution.py:25
  61.6 4.6 %product.9 = bf16[8,80,1536]{2,1,0:T(8,128)(2,1)S(1)} custom-call(s32[3]{0:T(128)S(1)} %pad_add_fusion.place.refs_0_, bf16[2,8,80,512]{3,2,1,0:T(8,128)(2,1)S(1)} %bitcast.90, bf16[2,8,80,512]{3,2,1,0:T(8,128)(2,1)S(1)} %bitcast.100, bf16[512,6144]{1,0:T(8,128)(2,1)} %bitcast.116, bf16[512,1536]{1,0:T(8,128)(2,1)} %collective-permute-done.7.refs_4_), custom_call_target="tpu_custom_call" | custom-call | tf_op jit(solution)/shard_map/product/pallas_call | solution.py:198
  67.5 8.7 %collective-permute-done.8 = bf16[2,80,1536]{2,1,0:T(8,128)(2,1)S(1)} collective-permute-done((bf16[2,80,1536]{2,1,0:T(8,128)(2,1)S(1)}, bf16[2,80,1536]{2,1,0:T(8,128)(2,1)S(1)}, u32[]{:S(2)}, u32[]{:S(2)}) %collective-permute-start.8) | collective-permute-done | bytes 491552 | tf_op jit(solution)/shard_map/ppermute | solution.py:25
  77.1 2.2 %add_convert_fusion.1 = bf16[2,80,1536]{2,1,0:T(8,128)(2,1)} fusion(bf16[2,80,1536]{2,1,0:T(8,128)(2,1)} %bitcast.103, bf16[2,80,1536]{2,1,0:T(8,128)(2,1)} %copy-done.13), kind=kLoop, calls=%fused_computation.1 | loop fusion | flops 983040 | bytes 1474560 | tf_op jit(solution)/shard_map/convert_element_type | solution.py:222
  79.3 2.0 %collective-permute-start.11 = (bf16[2,80,1536]{2,1,0:T(8,128)(2,1)}, bf16[2,80,1536]{2,1,0:T(8,128)(2,1)}, u32[]{:S(2)}, u32[]{:S(2)}) collective-permute-start(bf16[2,80,1536]{2,1,0:T(8,128)(2,1)} %add_convert_fusion.1), channel_id=1, source_target_pairs={{0,112},{16,0},{32,16},{48,32},{64,48},{80,64},{96,80},{112,96},{1... | collective-permute-start | bytes 1474568 | tf_op jit(solution)/shard_map/ppermute | solution.py:25
  81.3 2.5 %collective-permute-start.15 = (bf16[2,80,1536]{2,1,0:T(8,128)(2,1)}, bf16[2,80,1536]{2,1,0:T(8,128)(2,1)S(1)}, u32[]{:S(2)}, u32[]{:S(2)}) collective-permute-start(bf16[2,80,1536]{2,1,0:T(8,128)(2,1)} %copy-done.12), channel_id=1, source_target_pairs={{0,128},{128,0},{1,129},{129,1},{2,130},{130,2},{3,131},{131,3},{4... | collective-permute-start | bytes 1474568 | tf_op jit(solution)/shard_map/ppermute | solution.py:29
  85.3 9.6 %attention.1 = bf16[128,768]{1,0:T(8,128)(2,1)} custom-call(s32[3]{0:T(128)S(1)} %pad_add_fusion.place.refs_0_, bf16[128,768]{1,0:T(8,128)(2,1)S(1)} %copy-done.10, s32[1,128]{1,0:T(1,128)S(1)} %bitcast.109, bf16[16,144,256]{2,1,0:T(8,128)(2,1)S(1)} %bitcast.102, bf16[16,144,256]{2,1,0:T(8,128)(2,1)S(1)} %collective-permute-done.12.refs_4_), custom_call_target="tpu_custom_call" | custom-call | tf_op jit(solution)/shard_map/attention/pallas_call | solution.py:118
  96.5 5.8 %collective-permute-start.13 = (bf16[80,1536]{1,0:T(8,128)(2,1)S(1)}, bf16[80,1536]{1,0:T(8,128)(2,1)S(1)}, u32[]{:S(2)}, u32[]{:S(2)}) collective-permute-start(bf16[80,1536]{1,0:T(8,128)(2,1)S(1)} %get-tuple-element.101), channel_id=1, source_target_pairs={{0,112},{16,0},{32,16},{48,32},{64,48},{80,64},{96,80},{112,96},{1... | collective-permute-start | bytes 737288 | tf_op jit(solution)/shard_map/ppermute | solution.py:25
  103.3 5.0 %collective-permute-done.13 = bf16[80,1536]{1,0:T(8,128)(2,1)S(1)} collective-permute-done((bf16[80,1536]{1,0:T(8,128)(2,1)S(1)}, bf16[80,1536]{1,0:T(8,128)(2,1)S(1)}, u32[]{:S(2)}, u32[]{:S(2)}) %collective-permute-start.13) | collective-permute-done | bytes 245792 | tf_op jit(solution)/shard_map/ppermute | solution.py:25
  108.3 3.4 %collective-permute-done.14 = bf16[80,1536]{1,0:T(8,128)(2,1)S(1)} collective-permute-done((bf16[80,1536]{1,0:T(8,128)(2,1)S(1)}, bf16[80,1536]{1,0:T(8,128)(2,1)S(1)}, u32[]{:S(2)}, u32[]{:S(2)}) %collective-permute-start.14) | collective-permute-done | bytes 245792 | tf_op jit(solution)/shard_map/ppermute | solution.py:25
  113.3 1.7 collective-permute-start.17
  115.1 5.3 %collective-permute-done.16 = bf16[80,1536]{1,0:T(8,128)(2,1)S(1)} collective-permute-done((bf16[80,1536]{1,0:T(8,128)(2,1)S(1)}, bf16[80,1536]{1,0:T(8,128)(2,1)S(1)}, u32[]{:S(2)}, u32[]{:S(2)}) %collective-permute-start.16) | collective-permute-done | bytes 245792 | tf_op jit(solution)/shard_map/ppermute | solution.py:25
  123.1 1.7 collective-permute-start.19
  124.9 4.9 %all-to-all-start = ((bf16[8,16,768]{2,1,0:T(8,128)(2,1)}), bf16[8,16,768]{2,1,0:T(8,128)(2,1)S(1)}, u32[]{:S(2)}, u32[]{:S(2)}) async-start(bf16[8,16,768]{2,1,0:T(8,128)(2,1)} %bitcast.33), calls=%async_computation | async-start | bytes 393216 | tf_op jit(solution)/shard_map/all_to_all | solution.py:293
  130.2 6.1 %all-to-all-done = bf16[8,16,768]{2,1,0:T(8,128)(2,1)S(1)} async-done(((bf16[8,16,768]{2,1,0:T(8,128)(2,1)}), bf16[8,16,768]{2,1,0:T(8,128)(2,1)S(1)}, u32[]{:S(2)}, u32[]{:S(2)}) %all-to-all-start) | async-done | bytes 196640 | tf_op jit(solution)/shard_map/all_to_all | solution.py:293
  140.2 4.6 %collective-permute-done.21 = bf16[80,1536]{1,0:T(8,128)(2,1)S(1)} collective-permute-done((bf16[80,1536]{1,0:T(8,128)(2,1)S(1)}, bf16[80,1536]{1,0:T(8,128)(2,1)S(1)}, u32[]{:S(2)}, u32[]{:S(2)}) %collective-permute-start.21) | collective-permute-done | bytes 245792 | tf_op jit(solution)/shard_map/ppermute | solution.py:25
  147.0 4.6 %all-to-all-start.1 = ((bf16[16,5,3072]{2,1,0:T(8,128)(2,1)}), bf16[16,5,3072]{2,1,0:T(8,128)(2,1)S(1)}, u32[]{:S(2)}, u32[]{:S(2)}) async-start(bf16[16,5,3072]{2,1,0:T(8,128)(2,1)} %reshape.66), calls=%async_computation.1 | async-start | bytes 1572864 | tf_op jit(solution)/shard_map/all_to_all | solution.py:315
  151.8 14.4 %all-to-all-done.1 = bf16[16,5,3072]{2,1,0:T(8,128)(2,1)S(1)} async-done(((bf16[16,5,3072]{2,1,0:T(8,128)(2,1)}), bf16[16,5,3072]{2,1,0:T(8,128)(2,1)S(1)}, u32[]{:S(2)}, u32[]{:S(2)}) %all-to-all-start.1) | async-done | bytes 491552 | tf_op jit(solution)/shard_map/all_to_all | solution.py:315
  (96 shorter events, 22.0 us)
Async XLA Ops:
  7.2 70.0 %all-gather.2.cloned.1.call-start = ((), (), s32[]{:S(2)}) async-start(), calls=%async_computation.2 | async-start | bytes 1327104 | tf_op jit(solution)/shard_map/all_gather | solution.py:253
  10.1 5.4 %collective-permute-start.1 = (bf16[512,1536]{1,0:T(8,128)(2,1)S(1)}, bf16[512,1536]{1,0:T(8,128)(2,1)S(1)}, u32[]{:S(2)}, u32[]{:S(2)}) collective-permute-start(bf16[512,1536]{1,0:T(8,128)(2,1)S(1)} %columns.2), channel_id=1, source_target_pairs={{0,8},{8,0},{1,9},{9,1},{2,10},{10,2},{3,11},{11,3},{4,12},{12,4},... | collective-permute-start | bytes 4718600 | tf_op jit(solution)/shard_map/ppermute | solution.py:29
  10.2 5.3 %collective-permute-start = (bf16[1280,512]{1,0:T(8,128)(2,1)S(1)}, bf16[1280,512]{1,0:T(8,128)(2,1)S(1)}, u32[]{:S(2)}, u32[]{:S(2)}) collective-permute-start(bf16[1280,512]{1,0:T(8,128)(2,1)S(1)} %bitcast.80), channel_id=1, source_target_pairs={{0,8},{8,0},{1,9},{9,1},{2,10},{10,2},{3,11},{11,3},{4,12},{12,4},... | collective-permute-start | bytes 3932168 | tf_op jit(solution)/shard_map/ppermute | solution.py:29
  15.4 14.4 %copy-start.1 = (bf16[512,1536]{1,0:T(8,128)(2,1)}, bf16[512,1536]{1,0:T(8,128)(2,1)S(1)}, u32[]{:S(2)}) copy-start(bf16[512,1536]{1,0:T(8,128)(2,1)S(1)} %collective-permute-done.1.refs_6_.refs_10_) | copy-start | bytes 4718596
  19.4 17.0 %collective-permute-start.2 = (bf16[2,80,1536]{2,1,0:T(8,128)(2,1)}, bf16[2,80,1536]{2,1,0:T(8,128)(2,1)}, u32[]{:S(2)}, u32[]{:S(2)}) collective-permute-start(bf16[2,80,1536]{2,1,0:T(8,128)(2,1)} %bitcast.7), channel_id=1, source_target_pairs={{0,112},{16,0},{32,16},{48,32},{64,48},{80,64},{96,80},{112,96},{1... | collective-permute-start | bytes 1474568 | tf_op jit(solution)/shard_map/ppermute | solution.py:25
  25.2 14.5 %collective-permute-start.3 = (bf16[2,80,1536]{2,1,0:T(8,128)(2,1)}, bf16[2,80,1536]{2,1,0:T(8,128)(2,1)}, u32[]{:S(2)}, u32[]{:S(2)}) collective-permute-start(bf16[2,80,1536]{2,1,0:T(8,128)(2,1)} %bitcast.8), channel_id=1, source_target_pairs={{0,16},{16,32},{32,48},{48,64},{64,80},{80,96},{96,112},{112,0},{1... | collective-permute-start | bytes 1474568 | tf_op jit(solution)/shard_map/ppermute | solution.py:25
  29.4 14.1 %collective-permute-start.7 = (bf16[512,1536]{1,0:T(8,128)(2,1)}, bf16[512,1536]{1,0:T(8,128)(2,1)}, u32[]{:S(2)}, u32[]{:S(2)}) collective-permute-start(bf16[512,1536]{1,0:T(8,128)(2,1)} %columns.3), channel_id=1, source_target_pairs={{0,8},{8,0},{1,9},{9,1},{2,10},{10,2},{3,11},{11,3},{4,12},{12,4},... | collective-permute-start | bytes 4718600 | tf_op jit(solution)/shard_map/ppermute | solution.py:29
  29.4 6.3 %collective-permute-start.4 = (bf16[144,1,256]{2,0,1:T(8,128)(2,1)S(1)}, bf16[144,1,256]{2,0,1:T(8,128)(2,1)S(1)}, u32[]{:S(2)}, u32[]{:S(2)}) collective-permute-start(bf16[144,1,256]{2,0,1:T(8,128)(2,1)S(1)} %pad_maximum_fusion.3), channel_id=1, source_target_pairs={{0,128},{128,0},{1,129},{129,1},{2,130},{130,2},{3,131},{131,3},{4... | collective-permute-start | bytes 221192 | tf_op jit(solution)/shard_map/ppermute | solution.py:29
  41.3 15.5 %collective-permute-start.5 = (bf16[2,80,1536]{2,1,0:T(8,128)(2,1)S(1)}, bf16[2,80,1536]{2,1,0:T(8,128)(2,1)S(1)}, u32[]{:S(2)}, u32[]{:S(2)}) collective-permute-start(bf16[2,80,1536]{2,1,0:T(8,128)(2,1)S(1)} %get-tuple-element.72), channel_id=1, source_target_pairs={{0,112},{16,0},{32,16},{48,32},{64,48},{80,64},{96,80},{112,96},{1... | collective-permute-start | bytes 1474568 | tf_op jit(solution)/shard_map/ppermute | solution.py:25
  41.7 17.6 %collective-permute-start.6 = (bf16[2,80,1536]{2,1,0:T(8,128)(2,1)S(1)}, bf16[2,80,1536]{2,1,0:T(8,128)(2,1)S(1)}, u32[]{:S(2)}, u32[]{:S(2)}) collective-permute-start(bf16[2,80,1536]{2,1,0:T(8,128)(2,1)S(1)} %get-tuple-element.73), channel_id=1, source_target_pairs={{0,16},{16,32},{32,48},{48,64},{64,80},{80,96},{96,112},{112,0},{1... | collective-permute-start | bytes 1474568 | tf_op jit(solution)/shard_map/ppermute | solution.py:25
  48.8 28.4 %collective-permute-start.10 = (bf16[4,80,1536]{2,1,0:T(8,128)(2,1)}, bf16[4,80,1536]{2,1,0:T(8,128)(2,1)}, u32[]{:S(2)}, u32[]{:S(2)}) collective-permute-start(bf16[4,80,1536]{2,1,0:T(8,128)(2,1)} %get-tuple-element.76), channel_id=1, source_target_pairs={{0,128},{128,0},{1,129},{129,1},{2,130},{130,2},{3,131},{131,3},{4... | collective-permute-start | bytes 2949128 | tf_op jit(solution)/shard_map/ppermute | solution.py:29
  53.5 12.7 %copy-start.6 = (bf16[2,1,80,1536]{3,2,1,0:T(8,128)(2,1)}, bf16[2,1,80,1536]{3,2,1,0:T(8,128)(2,1)S(1)}, u32[]{:S(2)}) copy-start(bf16[2,1,80,1536]{3,2,1,0:T(8,128)(2,1)S(1)} %get-tuple-element.80) | copy-start | bytes 1474564
  59.5 16.8 %collective-permute-start.8 = (bf16[2,80,1536]{2,1,0:T(8,128)(2,1)S(1)}, bf16[2,80,1536]{2,1,0:T(8,128)(2,1)S(1)}, u32[]{:S(2)}, u32[]{:S(2)}) collective-permute-start(bf16[2,80,1536]{2,1,0:T(8,128)(2,1)S(1)} %add_convert_fusion.3), channel_id=1, source_target_pairs={{0,112},{16,0},{32,16},{48,32},{64,48},{80,64},{96,80},{112,96},{1... | collective-permute-start | bytes 1474568 | tf_op jit(solution)/shard_map/ppermute | solution.py:25
  59.6 17.5 %collective-permute-start.9 = (bf16[2,80,1536]{2,1,0:T(8,128)(2,1)S(1)}, bf16[2,80,1536]{2,1,0:T(8,128)(2,1)}, u32[]{:S(2)}, u32[]{:S(2)}) collective-permute-start(bf16[2,80,1536]{2,1,0:T(8,128)(2,1)S(1)} %add_convert_fusion.2), channel_id=1, source_target_pairs={{0,16},{16,32},{32,48},{48,64},{64,80},{80,96},{96,112},{112,0},{1... | collective-permute-start | bytes 1474568 | tf_op jit(solution)/shard_map/ppermute | solution.py:25
  67.5 17.8 %copy-start.10 = (bf16[128,768]{1,0:T(8,128)(2,1)S(1)}, bf16[128,768]{1,0:T(8,128)(2,1)}, u32[]{:S(2)}) copy-start(bf16[128,768]{1,0:T(8,128)(2,1)} %refs_1_.1) | copy-start | bytes 589828
  77.1 8.2 %copy-start.5 = (bf16[2304,1,256]{2,0,1:T(8,128)(2,1)S(1)}, bf16[2304,1,256]{2,0,1:T(8,128)(2,1)}, u32[]{:S(2)}) copy-start(bf16[2304,1,256]{2,0,1:T(8,128)(2,1)} %all-gather.2.cloned.1.call-done) | copy-start | bytes 3538948
  79.3 6.0 %collective-permute-start.12 = (bf16[16,144,256]{2,1,0:T(8,128)(2,1)}, bf16[16,144,256]{2,1,0:T(8,128)(2,1)S(1)}, u32[]{:S(2)}, u32[]{:S(2)}) collective-permute-start(bf16[16,144,256]{2,1,0:T(8,128)(2,1)} %bitcast.101), channel_id=1, source_target_pairs={{0,8},{8,0},{1,9},{9,1},{2,10},{10,2},{3,11},{11,3},{4,12},{12,4},... | collective-permute-start | bytes 3538952 | tf_op jit(solution)/shard_map/ppermute | solution.py:29
  79.3 15.6 %collective-permute-start.11 = (bf16[2,80,1536]{2,1,0:T(8,128)(2,1)}, bf16[2,80,1536]{2,1,0:T(8,128)(2,1)}, u32[]{:S(2)}, u32[]{:S(2)}) collective-permute-start(bf16[2,80,1536]{2,1,0:T(8,128)(2,1)} %add_convert_fusion.1), channel_id=1, source_target_pairs={{0,112},{16,0},{32,16},{48,32},{64,48},{80,64},{96,80},{112,96},{1... | collective-permute-start | bytes 1474568 | tf_op jit(solution)/shard_map/ppermute | solution.py:25
  81.3 21.9 %collective-permute-start.15 = (bf16[2,80,1536]{2,1,0:T(8,128)(2,1)}, bf16[2,80,1536]{2,1,0:T(8,128)(2,1)S(1)}, u32[]{:S(2)}, u32[]{:S(2)}) collective-permute-start(bf16[2,80,1536]{2,1,0:T(8,128)(2,1)} %copy-done.12), channel_id=1, source_target_pairs={{0,128},{128,0},{1,129},{129,1},{2,130},{130,2},{3,131},{131,3},{4... | collective-permute-start | bytes 1474568 | tf_op jit(solution)/shard_map/ppermute | solution.py:29
  85.3 9.7 %copy-start.9 = (bf16[2,1,80,1536]{3,2,1,0:T(8,128)(2,1)S(1)}, bf16[2,1,80,1536]{3,2,1,0:T(8,128)(2,1)}, u32[]{:S(2)}) copy-start(bf16[2,1,80,1536]{3,2,1,0:T(8,128)(2,1)} %copy-done.8) | copy-start | bytes 1474564
  94.9 16.8 %copy-start.4 = (bf16[8,80,1536]{2,1,0:T(8,128)(2,1)S(1)}, bf16[8,80,1536]{2,1,0:T(8,128)(2,1)}, u32[]{:S(2)}) copy-start(bf16[8,80,1536]{2,1,0:T(8,128)(2,1)} %copy-done.3) | copy-start | bytes 5898244
  96.5 11.8 %collective-permute-start.13 = (bf16[80,1536]{1,0:T(8,128)(2,1)S(1)}, bf16[80,1536]{1,0:T(8,128)(2,1)S(1)}, u32[]{:S(2)}, u32[]{:S(2)}) collective-permute-start(bf16[80,1536]{1,0:T(8,128)(2,1)S(1)} %get-tuple-element.101), channel_id=1, source_target_pairs={{0,112},{16,0},{32,16},{48,32},{64,48},{80,64},{96,80},{112,96},{1... | collective-permute-start | bytes 737288 | tf_op jit(solution)/shard_map/ppermute | solution.py:25
  102.3 9.4 %collective-permute-start.14 = (bf16[80,1536]{1,0:T(8,128)(2,1)S(1)}, bf16[80,1536]{1,0:T(8,128)(2,1)S(1)}, u32[]{:S(2)}, u32[]{:S(2)}) collective-permute-start(bf16[80,1536]{1,0:T(8,128)(2,1)S(1)} %get-tuple-element.102), channel_id=1, source_target_pairs={{0,16},{16,32},{32,48},{48,64},{64,80},{80,96},{96,112},{112,0},{1... | collective-permute-start | bytes 737288 | tf_op jit(solution)/shard_map/ppermute | solution.py:25
  112.9 16.8 %copy-start.15 = (s32[16,2]{0,1:T(2,128)S(1)}, s32[16,2]{0,1:T(2,128)}, u32[]{:S(2)}) copy-start(s32[16,2]{0,1:T(2,128)} %param.12) | copy-start | bytes 388
  113.0 7.4 %collective-permute-start.16 = (bf16[80,1536]{1,0:T(8,128)(2,1)S(1)}, bf16[80,1536]{1,0:T(8,128)(2,1)S(1)}, u32[]{:S(2)}, u32[]{:S(2)}) collective-permute-start(bf16[80,1536]{1,0:T(8,128)(2,1)S(1)} %get-tuple-element.108), channel_id=1, source_target_pairs={{0,112},{16,0},{32,16},{48,32},{64,48},{80,64},{96,80},{112,96},{1... | collective-permute-start | bytes 737288 | tf_op jit(solution)/shard_map/ppermute | solution.py:25
  113.3 8.6 %collective-permute-start.17 = (bf16[80,1536]{1,0:T(8,128)(2,1)S(1)}, bf16[80,1536]{1,0:T(8,128)(2,1)S(1)}, u32[]{:S(2)}, u32[]{:S(2)}) collective-permute-start(bf16[80,1536]{1,0:T(8,128)(2,1)S(1)} %get-tuple-element.109), channel_id=1, source_target_pairs={{0,16},{16,32},{32,48},{48,64},{64,80},{80,96},{96,112},{112,0},{1... | collective-permute-start | bytes 737288 | tf_op jit(solution)/shard_map/ppermute | solution.py:25
  115.1 21.4 %collective-permute-start.20 = (bf16[3,80,1536]{2,1,0:T(8,128)(2,1)}, bf16[3,80,1536]{2,1,0:T(8,128)(2,1)}, u32[]{:S(2)}, u32[]{:S(2)}) collective-permute-start(bf16[3,80,1536]{2,1,0:T(8,128)(2,1)} %pad_maximum_fusion), channel_id=1, source_target_pairs={{0,128},{128,0},{1,129},{129,1},{2,130},{130,2},{3,131},{131,3},{4... | collective-permute-start | bytes 2211848 | tf_op jit(solution)/shard_map/ppermute | solution.py:29
  122.8 13.6 %collective-permute-start.18 = (bf16[80,1536]{1,0:T(8,128)(2,1)}, bf16[80,1536]{1,0:T(8,128)(2,1)}, u32[]{:S(2)}, u32[]{:S(2)}) collective-permute-start(bf16[80,1536]{1,0:T(8,128)(2,1)} %get-tuple-element.113), channel_id=1, source_target_pairs={{0,112},{16,0},{32,16},{48,32},{64,48},{80,64},{96,80},{112,96},{1... | collective-permute-start | bytes 737288 | tf_op jit(solution)/shard_map/ppermute | solution.py:25
  123.1 13.3 %collective-permute-start.19 = (bf16[80,1536]{1,0:T(8,128)(2,1)S(1)}, bf16[80,1536]{1,0:T(8,128)(2,1)S(1)}, u32[]{:S(2)}, u32[]{:S(2)}) collective-permute-start(bf16[80,1536]{1,0:T(8,128)(2,1)S(1)} %get-tuple-element.114), channel_id=1, source_target_pairs={{0,16},{16,32},{32,48},{48,64},{64,80},{80,96},{96,112},{112,0},{1... | collective-permute-start | bytes 737288 | tf_op jit(solution)/shard_map/ppermute | solution.py:25
  124.9 11.5 %all-to-all-start = ((bf16[8,16,768]{2,1,0:T(8,128)(2,1)}), bf16[8,16,768]{2,1,0:T(8,128)(2,1)S(1)}, u32[]{:S(2)}, u32[]{:S(2)}) async-start(bf16[8,16,768]{2,1,0:T(8,128)(2,1)} %bitcast.33), calls=%async_computation | async-start | bytes 393216 | tf_op jit(solution)/shard_map/all_to_all | solution.py:293
  138.6 6.3 %collective-permute-start.21 = (bf16[80,1536]{1,0:T(8,128)(2,1)S(1)}, bf16[80,1536]{1,0:T(8,128)(2,1)S(1)}, u32[]{:S(2)}, u32[]{:S(2)}) collective-permute-start(bf16[80,1536]{1,0:T(8,128)(2,1)S(1)} %fusion.2), channel_id=1, source_target_pairs={{0,112},{16,0},{32,16},{48,32},{64,48},{80,64},{96,80},{112,96},{1... | collective-permute-start | bytes 737288 | tf_op jit(solution)/shard_map/ppermute | solution.py:25
  147.0 19.2 %all-to-all-start.1 = ((bf16[16,5,3072]{2,1,0:T(8,128)(2,1)}), bf16[16,5,3072]{2,1,0:T(8,128)(2,1)S(1)}, u32[]{:S(2)}, u32[]{:S(2)}) async-start(bf16[16,5,3072]{2,1,0:T(8,128)(2,1)} %reshape.66), calls=%async_computation.1 | async-start | bytes 1572864 | tf_op jit(solution)/shard_map/all_to_all | solution.py:315
  (10 other events, 38.5 us)
Sparse Core Ops, SparseCore 0:
  36.5 40.2 all-gather.1

commit v8 on v6

--- a/solution.py
+++ b/solution.py
@@ -15,6 +15,7 @@
 Z = 8
 EXPERTS = 8
 PAD = 16
+SPLIT = 8
 GROUPS = 2
 ORDER = (4, 3, 5, 2, 6, 1, 7, 0)
 PRODUCT_VMEM = 16 * 1024 * 1024
@@ -308,11 +309,14 @@
     tokens = routes.shape[0]
     capacity = first.shape[0] // (2 * EXPERTS)
     mix = mixing(routes, route_weights, capacity)
-    rows = jnp.concatenate([first, second], axis=1).reshape(2 * EXPERTS, capacity, -1)
+    unit = (jnp.arange(SPLIT)[:, None] == jnp.arange(SPLIT)[None, :]).astype(mix.dtype)
+    mix = (mix[None, :, :, None] * unit[:, None, None, :]).reshape(SPLIT * 2 * tokens, -1)
+    rows = jnp.concatenate([first, second], axis=1).reshape(2 * EXPERTS, capacity * SPLIT, -1)
     home = lax.all_to_all(rows, ("c",) + EXP, split_axis=0, concat_axis=0, tiled=True)
-    home = home.reshape(2, EXPERTS * capacity, -1)
-    both = jnp.einsum("tr,crn->tcn", mix, home, preferred_element_type=jnp.float32)
-    mixed = (both[:tokens] + both[tokens:]).reshape(tokens, -1)
+    home = home.reshape(2, EXPERTS * capacity * SPLIT, -1)
+    both = jnp.einsum("tr,crn->ctn", mix, home, preferred_element_type=jnp.float32)
+    both = both.reshape(2, SPLIT, 2 * tokens, -1)
+    mixed = (both[:, :, :tokens] + both[:, :, tokens:]).transpose(2, 0, 1, 3).reshape(tokens, -1)
     moe_out = residual.astype(jnp.float32) + mixed
     return (context, moe_out.astype(jnp.bfloat16))
 

time: 172 us -> 173 us (level)
  waiting for transfers between devices: 65 us -> 61.1 us
  other arithmetic: 14 us -> 17.2 us
    all_to_all x1, waiting for transfers between devices: 14.4 us -> 9.99 us  [shards(): lax.all_to_all(rows, ('c',) + EXP, split_axis=0, concat_axis=0, tiled=True)]
    convert_element_type x11, other arithmetic: 12.2 us -> 15.2 us  [add(): return total.astype(jnp.bfloat16)]
  transfers between devices with their start and end apart: 26 -> 26, of which waited for: 14 -> 14; matrix products, arithmetic and copies ran while one was open for 5% -> 8% of each run, Pallas kernels for 18% -> 18%
where the time goes in v8:
time: 173 us; the launch traced here: 172 us
  waiting for transfers between devices  61.1 us (35%)
  Pallas kernels  38 us (22%)
  starting transfers between devices  35.2 us (20%)
  other arithmetic  17.2 us (10%)
  between operations  14.4 us (8%)
  local copies, waits for them, and re-layouts  5.59 us (3%)
    ppermute x14, waiting for transfers between devices, shift(): return lax.ppermute(value, 'z', [(i, (i + step) % Z) for i in range(Z)])  37.8 us
    ppermute x14, starting transfers between devices, shift(): return lax.ppermute(value, 'z', [(i, (i + step) % Z) for i in range(Z)])  23.5 us
    pallas_call x5, Pallas kernels, product(): pl.pallas_call(lambda *refs: product_kernel(len(picks), offsets, *refs),...  21.4 us
    convert_element_type x11, other arithmetic, add(): return total.astype(jnp.bfloat16)  15.2 us
    all_to_all x1, waiting for transfers between devices, shards(): lax.all_to_all(rows, ('c',) + EXP, split_axis=0, concat_axis=0, tiled=True)  9.99 us
    pallas_call x1, Pallas kernels, attend(): pl.pallas_call(lambda *refs: attention_kernel(head, *refs), out_shape=jax...  9.65 us
    pallas_call x2, Pallas kernels, other_columns(): pl.pallas_call(slice_kernel, out_shape=jax.ShapeDtypeStruct((depth, colum...  6.93 us
    all_to_all x1, waiting for transfers between devices, shards(): lax.all_to_all(context, EXP, split_axis=0, concat_axis=1, tiled=True)  6.66 us
  transfers between devices with their start and end apart: 26, of which 14 were waited for; matrix products, arithmetic and copies ran while one was open for 8% of the time, Pallas kernels for 18%

profile of v8, /device:TPU:16, one launch (start us, length us, event | category | flops | bytes accessed | tf_op | source)
XLA Modules:
  0.0 171.8 jit_solution(120344396720050920)
XLA Ops:
  7.3 2.8 %columns.2 = bf16[512,1536]{1,0:T(8,128)(2,1)S(1)} custom-call(s32[3]{0:T(128)S(1)} %pad_add_fusion.place.refs_0_, bf16[512,6144]{1,0:T(8,128)(2,1)} %bitcast.116), custom_call_target="tpu_custom_call" | custom-call | tf_op jit(solution)/shard_map/columns/pallas_call | solution.py:143
  10.7 4.8 %collective-permute-done = bf16[1280,512]{1,0:T(8,128)(2,1)S(1)} collective-permute-done((bf16[1280,512]{1,0:T(8,128)(2,1)S(1)}, bf16[1280,512]{1,0:T(8,128)(2,1)S(1)}, u32[]{:S(2)}, u32[]{:S(2)}) %collective-permute-start) | collective-permute-done | bytes 1310752 | tf_op jit(solution)/shard_map/ppermute | solution.py:30
  15.5 3.9 %product.5 = (bf16[2,1,80,1536]{3,2,1,0:T(8,128)(2,1)}, bf16[2,1,80,1536]{3,2,1,0:T(8,128)(2,1)}) custom-call(s32[3]{0:T(128)S(1)} %pad_add_fusion.place.refs_0_, bf16[2,8,80,512]{3,2,1,0:T(8,128)(2,1)S(1)} %bitcast.87, bf16[2,8,80,512]{3,2,1,0:T(8,128)(2,1)S(1)} %bitcast.88, bf16[2,8,80,512]{3,2,1,0:T(8,128)(2,1)S(1)} %bitcast.97, ...), custom_call_target="tpu_custom_call" | custom-call | tf_op jit(solution)/shard_map/product/pallas_call | solution.py:199
  19.4 5.9 %collective-permute-start.2 = (bf16[2,80,1536]{2,1,0:T(8,128)(2,1)}, bf16[2,80,1536]{2,1,0:T(8,128)(2,1)}, u32[]{:S(2)}, u32[]{:S(2)}) collective-permute-start(bf16[2,80,1536]{2,1,0:T(8,128)(2,1)} %bitcast.7), channel_id=1, source_target_pairs={{0,112},{16,0},{32,16},{48,32},{64,48},{80,64},{96,80},{112,96},{1... | collective-permute-start | bytes 1474568 | tf_op jit(solution)/shard_map/ppermute | solution.py:26
  25.2 4.2 %columns.3 = bf16[512,1536]{1,0:T(8,128)(2,1)} custom-call(s32[3]{0:T(128)S(1)} %pad_add_fusion.place.refs_0_, bf16[512,6144]{1,0:T(8,128)(2,1)} %bitcast.118), custom_call_target="tpu_custom_call" | custom-call | tf_op jit(solution)/shard_map/columns/pallas_call | solution.py:143
  29.9 3.2 %product.6 = (bf16[2,1,80,1536]{3,2,1,0:T(8,128)(2,1)S(1)}, bf16[2,1,80,1536]{3,2,1,0:T(8,128)(2,1)S(1)}) custom-call(s32[3]{0:T(128)S(1)} %pad_add_fusion.place.refs_0_, bf16[2,8,80,512]{3,2,1,0:T(8,128)(2,1)S(1)} %bitcast.89, bf16[2,8,80,512]{3,2,1,0:T(8,128)(2,1)S(1)} %bitcast.90, bf16[2,8,80,512]{3,2,1,0:T(8,128)(2,1)S(1)} %bitcast.99, ...), custom_call_target="tpu_custom_call" | custom-call | tf_op jit(solution)/shard_map/product/pallas_call | solution.py:199
  33.9 1.8 %collective-permute-done.4 = bf16[144,1,256]{2,0,1:T(8,128)(2,1)S(1)} collective-permute-done((bf16[144,1,256]{2,0,1:T(8,128)(2,1)S(1)}, bf16[144,1,256]{2,0,1:T(8,128)(2,1)S(1)}, u32[]{:S(2)}, u32[]{:S(2)}) %collective-permute-start.4) | collective-permute-done | bytes 73760 | tf_op jit(solution)/shard_map/ppermute | solution.py:30
  36.4 3.3 %collective-permute-done.3 = bf16[2,80,1536]{2,1,0:T(8,128)(2,1)} collective-permute-done((bf16[2,80,1536]{2,1,0:T(8,128)(2,1)}, bf16[2,80,1536]{2,1,0:T(8,128)(2,1)}, u32[]{:S(2)}, u32[]{:S(2)}) %collective-permute-start.3) | collective-permute-done | bytes 491552 | tf_op jit(solution)/shard_map/ppermute | solution.py:26
  41.7 1.7 %collective-permute-start.6 = (bf16[2,80,1536]{2,1,0:T(8,128)(2,1)S(1)}, bf16[2,80,1536]{2,1,0:T(8,128)(2,1)S(1)}, u32[]{:S(2)}, u32[]{:S(2)}) collective-permute-start(bf16[2,80,1536]{2,1,0:T(8,128)(2,1)S(1)} %get-tuple-element.74), channel_id=1, source_target_pairs={{0,16},{16,32},{32,48},{48,64},{64,80},{80,96},{96,112},{112,0},{1... | collective-permute-start | bytes 1474568 | tf_op jit(solution)/shard_map/ppermute | solution.py:26
  43.4 5.3 %product.7 = (bf16[4,80,1536]{2,1,0:T(8,128)(2,1)}, bf16[2,80,1536]{2,1,0:T(8,128)(2,1)S(1)}, bf16[2,80,1536]{2,1,0:T(8,128)(2,1)S(1)}) custom-call(s32[3]{0:T(128)S(1)} %pad_add_fusion.place.refs_0_, bf16[2,8,80,512]{3,2,1,0:T(8,128)(2,1)S(1)} %bitcast.91, bf16[2,8,80,512]{3,2,1,0:T(8,128)(2,1)S(1)} %bitcast.101, bf16[512,6144]{1,0:T(8,128)(2,1)} %bitcast.120, ...), custom_call_target="tpu_custom_call" | custom-call | tf_op jit(solution)/shard_map/product/pallas_call | solution.py:199
  49.9 4.4 %product.8 = (bf16[2,1,80,1536]{3,2,1,0:T(8,128)(2,1)S(1)}, bf16[2,1,80,1536]{3,2,1,0:T(8,128)(2,1)S(1)}, bf16[2,1,80,1536]{3,2,1,0:T(8,128)(2,1)S(1)}, bf16[2,1,80,1536]{3,2,1,0:T(8,128)(2,1)S(1)}) custom-call(s32[3]{0:T(128)S(1)} %pad_add_fusion.place.refs_0_, bf16[2,8,80,512]{3,2,1,0:T(8,128)(2,1)S(1)} %bitcast.92, bf16[2,8,80,512]{3,2,1,0:T(8,128)(2,1)S(1)} %bitcast.93, ...), custom_call_target="tpu_custom_call" | custom-call | tf_op jit(solution)/shard_map/product/pallas_call | solution.py:199
  54.3 2.6 %collective-permute-done.5 = bf16[2,80,1536]{2,1,0:T(8,128)(2,1)S(1)} collective-permute-done((bf16[2,80,1536]{2,1,0:T(8,128)(2,1)S(1)}, bf16[2,80,1536]{2,1,0:T(8,128)(2,1)S(1)}, u32[]{:S(2)}, u32[]{:S(2)}) %collective-permute-start.5) | collective-permute-done | bytes 491552 | tf_op jit(solution)/shard_map/ppermute | solution.py:26
  56.9 2.4 %collective-permute-done.6 = bf16[2,80,1536]{2,1,0:T(8,128)(2,1)S(1)} collective-permute-done((bf16[2,80,1536]{2,1,0:T(8,128)(2,1)S(1)}, bf16[2,80,1536]{2,1,0:T(8,128)(2,1)S(1)}, u32[]{:S(2)}, u32[]{:S(2)}) %collective-permute-start.6) | collective-permute-done | bytes 491552 | tf_op jit(solution)/shard_map/ppermute | solution.py:26
  59.6 2.0 %collective-permute-start.9 = (bf16[2,80,1536]{2,1,0:T(8,128)(2,1)S(1)}, bf16[2,80,1536]{2,1,0:T(8,128)(2,1)}, u32[]{:S(2)}, u32[]{:S(2)}) collective-permute-start(bf16[2,80,1536]{2,1,0:T(8,128)(2,1)S(1)} %add_convert_fusion.2), channel_id=1, source_target_pairs={{0,16},{16,32},{32,48},{48,64},{64,80},{80,96},{96,112},{112,0},{1... | collective-permute-start | bytes 1474568 | tf_op jit(solution)/shard_map/ppermute | solution.py:26
  61.6 4.6 %product.9 = bf16[8,80,1536]{2,1,0:T(8,128)(2,1)S(1)} custom-call(s32[3]{0:T(128)S(1)} %pad_add_fusion.place.refs_0_, bf16[2,8,80,512]{3,2,1,0:T(8,128)(2,1)S(1)} %bitcast.96, bf16[2,8,80,512]{3,2,1,0:T(8,128)(2,1)S(1)} %bitcast.106, bf16[512,6144]{1,0:T(8,128)(2,1)} %bitcast.122, bf16[512,1536]{1,0:T(8,128)(2,1)} %collective-permute-done.7.refs_4_), custom_call_target="tpu_custom_call" | custom-call | tf_op jit(solution)/shard_map/product/pallas_call | solution.py:199
  67.5 8.8 %collective-permute-done.8 = bf16[2,80,1536]{2,1,0:T(8,128)(2,1)} collective-permute-done((bf16[2,80,1536]{2,1,0:T(8,128)(2,1)S(1)}, bf16[2,80,1536]{2,1,0:T(8,128)(2,1)}, u32[]{:S(2)}, u32[]{:S(2)}) %collective-permute-start.8) | collective-permute-done | bytes 491552 | tf_op jit(solution)/shard_map/ppermute | solution.py:26
  77.2 2.1 %add_convert_fusion.1 = bf16[2,80,1536]{2,1,0:T(8,128)(2,1)} fusion(bf16[2,80,1536]{2,1,0:T(8,128)(2,1)S(1)} %bitcast.109, bf16[2,80,1536]{2,1,0:T(8,128)(2,1)} %collective-permute-done.8), kind=kLoop, calls=%fused_computation.1 | loop fusion | flops 983040 | bytes 1474560 | tf_op jit(solution)/shard_map/convert_element_type | solution.py:223
  79.2 2.1 %collective-permute-start.11 = (bf16[2,80,1536]{2,1,0:T(8,128)(2,1)}, bf16[2,80,1536]{2,1,0:T(8,128)(2,1)}, u32[]{:S(2)}, u32[]{:S(2)}) collective-permute-start(bf16[2,80,1536]{2,1,0:T(8,128)(2,1)} %add_convert_fusion.1), channel_id=1, source_target_pairs={{0,112},{16,0},{32,16},{48,32},{64,48},{80,64},{96,80},{112,96},{1... | collective-permute-start | bytes 1474568 | tf_op jit(solution)/shard_map/ppermute | solution.py:26
  81.3 1.8 %collective-permute-start.15 = (bf16[2,80,1536]{2,1,0:T(8,128)(2,1)}, bf16[2,80,1536]{2,1,0:T(8,128)(2,1)S(1)}, u32[]{:S(2)}, u32[]{:S(2)}) collective-permute-start(bf16[2,80,1536]{2,1,0:T(8,128)(2,1)} %copy-done.13), channel_id=1, source_target_pairs={{0,128},{128,0},{1,129},{129,1},{2,130},{130,2},{3,131},{131,3},{4... | collective-permute-start | bytes 1474568 | tf_op jit(solution)/shard_map/ppermute | solution.py:30
  83.1 2.2 %fusion.9 = (bf16[80,1536]{1,0:T(8,128)(2,1)}, bf16[80,1536]{1,0:T(8,128)(2,1)}) fusion(bf16[4,80,1536]{2,1,0:T(8,128)(2,1)} %collective-permute-done.10, bf16[8,80,1536]{2,1,0:T(8,128)(2,1)} %copy-done.3), kind=kLoop, calls=%fused_computation.34 | loop fusion | flops 983040 | bytes 1474560 | tf_op jit(solution)/shard_map/convert_element_type | solution.py:223
  85.3 9.6 %attention.1 = bf16[128,768]{1,0:T(8,128)(2,1)} custom-call(s32[3]{0:T(128)S(1)} %pad_add_fusion.place.refs_0_, bf16[128,768]{1,0:T(8,128)(2,1)S(1)} %copy-done.9, s32[1,128]{1,0:T(1,128)S(1)} %bitcast.115, bf16[16,144,256]{2,1,0:T(8,128)(2,1)S(1)} %bitcast.108, bf16[16,144,256]{2,1,0:T(8,128)(2,1)S(1)} %collective-permute-done.12.refs_4_), custom_call_target="tpu_custom_call" | custom-call | tf_op jit(solution)/shard_map/attention/pallas_call | solution.py:119
  97.2 5.7 %collective-permute-start.13 = (bf16[80,1536]{1,0:T(8,128)(2,1)}, bf16[80,1536]{1,0:T(8,128)(2,1)}, u32[]{:S(2)}, u32[]{:S(2)}) collective-permute-start(bf16[80,1536]{1,0:T(8,128)(2,1)} %get-tuple-element.102), channel_id=1, source_target_pairs={{0,112},{16,0},{32,16},{48,32},{64,48},{80,64},{96,80},{112,96},{1... | collective-permute-start | bytes 737288 | tf_op jit(solution)/shard_map/ppermute | solution.py:26
  103.2 6.0 %collective-permute-done.13 = bf16[80,1536]{1,0:T(8,128)(2,1)} collective-permute-done((bf16[80,1536]{1,0:T(8,128)(2,1)}, bf16[80,1536]{1,0:T(8,128)(2,1)}, u32[]{:S(2)}, u32[]{:S(2)}) %collective-permute-start.13) | collective-permute-done | bytes 245792 | tf_op jit(solution)/shard_map/ppermute | solution.py:26
  109.3 3.4 %collective-permute-done.14 = bf16[80,1536]{1,0:T(8,128)(2,1)} collective-permute-done((bf16[80,1536]{1,0:T(8,128)(2,1)}, bf16[80,1536]{1,0:T(8,128)(2,1)}, u32[]{:S(2)}, u32[]{:S(2)}) %collective-permute-start.14) | collective-permute-done | bytes 245792 | tf_op jit(solution)/shard_map/ppermute | solution.py:26
  112.7 2.3 %fusion.5 = (bf16[80,1536]{1,0:T(8,128)(2,1)}, bf16[80,1536]{1,0:T(8,128)(2,1)}) fusion(bf16[80,1536]{1,0:T(8,128)(2,1)} %collective-permute-done.14, bf16[4,80,1536]{2,1,0:T(8,128)(2,1)} %collective-permute-done.10, bf16[8,80,1536]{2,1,0:T(8,128)(2,1)S(1)} %copy-done.4, bf16[80,1536]{1,0:T(8,128)(2,1)} %collective-permute-done.13), kind=kLoop, calls=%fused_computation.22 | loop fusion | flops 1474560 | bytes 1966080 | tf_op jit(solution)/shard_map/convert_element_type | solution.py:223
  117.4 5.2 %collective-permute-done.16 = bf16[80,1536]{1,0:T(8,128)(2,1)} collective-permute-done((bf16[80,1536]{1,0:T(8,128)(2,1)}, bf16[80,1536]{1,0:T(8,128)(2,1)}, u32[]{:S(2)}, u32[]{:S(2)}) %collective-permute-start.16) | collective-permute-done | bytes 245792 | tf_op jit(solution)/shard_map/ppermute | solution.py:26
  124.1 2.1 %fusion.3 = (bf16[80,1536]{1,0:T(8,128)(2,1)}, bf16[80,1536]{1,0:T(8,128)(2,1)}) fusion(bf16[80,1536]{1,0:T(8,128)(2,1)} %collective-permute-done.17, bf16[2,80,1536]{2,1,0:T(8,128)(2,1)S(1)} %collective-permute-done.15, bf16[8,80,1536]{2,1,0:T(8,128)(2,1)S(1)} %copy-done.4, bf16[80,1536]{1,0:T(8,128)(2,1)} %collective-permute-done.16), kind=kLoop, calls=%fused_computation.16 | loop fusion | flops 1474560 | bytes 1966080 | tf_op jit(solution)/shard_map/convert_element_type | solution.py:223
  128.3 4.8 %all-to-all-start = ((bf16[8,16,768]{2,1,0:T(8,128)(2,1)}), bf16[8,16,768]{2,1,0:T(8,128)(2,1)S(1)}, u32[]{:S(2)}, u32[]{:S(2)}) async-start(bf16[8,16,768]{2,1,0:T(8,128)(2,1)} %bitcast.32), calls=%async_computation | async-start | bytes 393216 | tf_op jit(solution)/shard_map/all_to_all | solution.py:293
  133.1 6.7 %all-to-all-done = bf16[8,16,768]{2,1,0:T(8,128)(2,1)S(1)} async-done(((bf16[8,16,768]{2,1,0:T(8,128)(2,1)}), bf16[8,16,768]{2,1,0:T(8,128)(2,1)S(1)}, u32[]{:S(2)}, u32[]{:S(2)}) %all-to-all-start) | async-done | bytes 196640 | tf_op jit(solution)/shard_map/all_to_all | solution.py:293
  143.6 3.7 %collective-permute-done.22 = bf16[80,1536]{1,0:T(8,128)(2,1)S(1)} collective-permute-done((bf16[80,1536]{1,0:T(8,128)(2,1)S(1)}, bf16[80,1536]{1,0:T(8,128)(2,1)S(1)}, u32[]{:S(2)}, u32[]{:S(2)}) %collective-permute-start.22) | collective-permute-done | bytes 245792 | tf_op jit(solution)/shard_map/ppermute | solution.py:26
  149.5 3.6 %all-to-all-start.1 = ((bf16[16,40,384]{2,1,0:T(8,128)(2,1)}), bf16[16,40,384]{2,1,0:T(8,128)(2,1)S(1)}, u32[]{:S(2)}, u32[]{:S(2)}) async-start(bf16[16,40,384]{2,1,0:T(8,128)(2,1)} %reshape.94), calls=%async_computation.1 | async-start | bytes 983040 | tf_op jit(solution)/shard_map/all_to_all | solution.py:315
  153.8 10.0 %all-to-all-done.1 = bf16[16,40,384]{2,1,0:T(8,128)(2,1)S(1)} async-done(((bf16[16,40,384]{2,1,0:T(8,128)(2,1)}), bf16[16,40,384]{2,1,0:T(8,128)(2,1)S(1)}, u32[]{:S(2)}, u32[]{:S(2)}) %all-to-all-start.1) | async-done | bytes 491552 | tf_op jit(solution)/shard_map/all_to_all | solution.py:315
  (100 shorter events, 24.5 us)
Async XLA Ops:
  7.2 70.0 %all-gather.2.cloned.1.call-start = ((), (), s32[]{:S(2)}) async-start(), calls=%async_computation.2 | async-start | bytes 1327104 | tf_op jit(solution)/shard_map/all_gather | solution.py:254
  10.1 5.4 %collective-permute-start.1 = (bf16[512,1536]{1,0:T(8,128)(2,1)S(1)}, bf16[512,1536]{1,0:T(8,128)(2,1)S(1)}, u32[]{:S(2)}, u32[]{:S(2)}) collective-permute-start(bf16[512,1536]{1,0:T(8,128)(2,1)S(1)} %columns.2), channel_id=1, source_target_pairs={{0,8},{8,0},{1,9},{9,1},{2,10},{10,2},{3,11},{11,3},{4,12},{12,4},... | collective-permute-start | bytes 4718600 | tf_op jit(solution)/shard_map/ppermute | solution.py:30
  10.2 5.3 %collective-permute-start = (bf16[1280,512]{1,0:T(8,128)(2,1)S(1)}, bf16[1280,512]{1,0:T(8,128)(2,1)S(1)}, u32[]{:S(2)}, u32[]{:S(2)}) collective-permute-start(bf16[1280,512]{1,0:T(8,128)(2,1)S(1)} %bitcast.86), channel_id=1, source_target_pairs={{0,8},{8,0},{1,9},{9,1},{2,10},{10,2},{3,11},{11,3},{4,12},{12,4},... | collective-permute-start | bytes 3932168 | tf_op jit(solution)/shard_map/ppermute | solution.py:30
  15.4 14.4 %copy-start.1 = (bf16[512,1536]{1,0:T(8,128)(2,1)}, bf16[512,1536]{1,0:T(8,128)(2,1)S(1)}, u32[]{:S(2)}) copy-start(bf16[512,1536]{1,0:T(8,128)(2,1)S(1)} %collective-permute-done.1.refs_6_.refs_10_) | copy-start | bytes 4718596
  19.4 17.0 %collective-permute-start.2 = (bf16[2,80,1536]{2,1,0:T(8,128)(2,1)}, bf16[2,80,1536]{2,1,0:T(8,128)(2,1)}, u32[]{:S(2)}, u32[]{:S(2)}) collective-permute-start(bf16[2,80,1536]{2,1,0:T(8,128)(2,1)} %bitcast.7), channel_id=1, source_target_pairs={{0,112},{16,0},{32,16},{48,32},{64,48},{80,64},{96,80},{112,96},{1... | collective-permute-start | bytes 1474568 | tf_op jit(solution)/shard_map/ppermute | solution.py:26
  25.2 14.5 %collective-permute-start.3 = (bf16[2,80,1536]{2,1,0:T(8,128)(2,1)}, bf16[2,80,1536]{2,1,0:T(8,128)(2,1)}, u32[]{:S(2)}, u32[]{:S(2)}) collective-permute-start(bf16[2,80,1536]{2,1,0:T(8,128)(2,1)} %bitcast.8), channel_id=1, source_target_pairs={{0,16},{16,32},{32,48},{48,64},{64,80},{80,96},{96,112},{112,0},{1... | collective-permute-start | bytes 1474568 | tf_op jit(solution)/shard_map/ppermute | solution.py:26
  29.4 14.1 %collective-permute-start.7 = (bf16[512,1536]{1,0:T(8,128)(2,1)}, bf16[512,1536]{1,0:T(8,128)(2,1)}, u32[]{:S(2)}, u32[]{:S(2)}) collective-permute-start(bf16[512,1536]{1,0:T(8,128)(2,1)} %columns.3), channel_id=1, source_target_pairs={{0,8},{8,0},{1,9},{9,1},{2,10},{10,2},{3,11},{11,3},{4,12},{12,4},... | collective-permute-start | bytes 4718600 | tf_op jit(solution)/shard_map/ppermute | solution.py:30
  29.4 6.3 %collective-permute-start.4 = (bf16[144,1,256]{2,0,1:T(8,128)(2,1)S(1)}, bf16[144,1,256]{2,0,1:T(8,128)(2,1)S(1)}, u32[]{:S(2)}, u32[]{:S(2)}) collective-permute-start(bf16[144,1,256]{2,0,1:T(8,128)(2,1)S(1)} %pad_maximum_fusion.2), channel_id=1, source_target_pairs={{0,128},{128,0},{1,129},{129,1},{2,130},{130,2},{3,131},{131,3},{4... | collective-permute-start | bytes 221192 | tf_op jit(solution)/shard_map/ppermute | solution.py:30
  41.3 15.5 %collective-permute-start.5 = (bf16[2,80,1536]{2,1,0:T(8,128)(2,1)S(1)}, bf16[2,80,1536]{2,1,0:T(8,128)(2,1)S(1)}, u32[]{:S(2)}, u32[]{:S(2)}) collective-permute-start(bf16[2,80,1536]{2,1,0:T(8,128)(2,1)S(1)} %get-tuple-element.73), channel_id=1, source_target_pairs={{0,112},{16,0},{32,16},{48,32},{64,48},{80,64},{96,80},{112,96},{1... | collective-permute-start | bytes 1474568 | tf_op jit(solution)/shard_map/ppermute | solution.py:26
  41.7 17.6 %collective-permute-start.6 = (bf16[2,80,1536]{2,1,0:T(8,128)(2,1)S(1)}, bf16[2,80,1536]{2,1,0:T(8,128)(2,1)S(1)}, u32[]{:S(2)}, u32[]{:S(2)}) collective-permute-start(bf16[2,80,1536]{2,1,0:T(8,128)(2,1)S(1)} %get-tuple-element.74), channel_id=1, source_target_pairs={{0,16},{16,32},{32,48},{48,64},{64,80},{80,96},{96,112},{112,0},{1... | collective-permute-start | bytes 1474568 | tf_op jit(solution)/shard_map/ppermute | solution.py:26
  49.6 27.6 %collective-permute-start.10 = (bf16[4,80,1536]{2,1,0:T(8,128)(2,1)}, bf16[4,80,1536]{2,1,0:T(8,128)(2,1)}, u32[]{:S(2)}, u32[]{:S(2)}) collective-permute-start(bf16[4,80,1536]{2,1,0:T(8,128)(2,1)} %get-tuple-element.77), channel_id=1, source_target_pairs={{0,128},{128,0},{1,129},{129,1},{2,130},{130,2},{3,131},{131,3},{4... | collective-permute-start | bytes 2949128 | tf_op jit(solution)/shard_map/ppermute | solution.py:30
  59.5 16.9 %collective-permute-start.8 = (bf16[2,80,1536]{2,1,0:T(8,128)(2,1)S(1)}, bf16[2,80,1536]{2,1,0:T(8,128)(2,1)}, u32[]{:S(2)}, u32[]{:S(2)}) collective-permute-start(bf16[2,80,1536]{2,1,0:T(8,128)(2,1)S(1)} %add_convert_fusion.3), channel_id=1, source_target_pairs={{0,112},{16,0},{32,16},{48,32},{64,48},{80,64},{96,80},{112,96},{1... | collective-permute-start | bytes 1474568 | tf_op jit(solution)/shard_map/ppermute | solution.py:26
  59.6 17.5 %collective-permute-start.9 = (bf16[2,80,1536]{2,1,0:T(8,128)(2,1)S(1)}, bf16[2,80,1536]{2,1,0:T(8,128)(2,1)}, u32[]{:S(2)}, u32[]{:S(2)}) collective-permute-start(bf16[2,80,1536]{2,1,0:T(8,128)(2,1)S(1)} %add_convert_fusion.2), channel_id=1, source_target_pairs={{0,16},{16,32},{32,48},{48,64},{64,80},{80,96},{96,112},{112,0},{1... | collective-permute-start | bytes 1474568 | tf_op jit(solution)/shard_map/ppermute | solution.py:26
  67.5 17.8 %copy-start.9 = (bf16[128,768]{1,0:T(8,128)(2,1)S(1)}, bf16[128,768]{1,0:T(8,128)(2,1)}, u32[]{:S(2)}) copy-start(bf16[128,768]{1,0:T(8,128)(2,1)} %refs_1_.1) | copy-start | bytes 589828
  79.2 6.0 %collective-permute-start.12 = (bf16[16,144,256]{2,1,0:T(8,128)(2,1)}, bf16[16,144,256]{2,1,0:T(8,128)(2,1)S(1)}, u32[]{:S(2)}, u32[]{:S(2)}) collective-permute-start(bf16[16,144,256]{2,1,0:T(8,128)(2,1)} %bitcast.107), channel_id=1, source_target_pairs={{0,8},{8,0},{1,9},{9,1},{2,10},{10,2},{3,11},{11,3},{4,12},{12,4},... | collective-permute-start | bytes 3538952 | tf_op jit(solution)/shard_map/ppermute | solution.py:30
  79.2 15.7 %collective-permute-start.11 = (bf16[2,80,1536]{2,1,0:T(8,128)(2,1)}, bf16[2,80,1536]{2,1,0:T(8,128)(2,1)}, u32[]{:S(2)}, u32[]{:S(2)}) collective-permute-start(bf16[2,80,1536]{2,1,0:T(8,128)(2,1)} %add_convert_fusion.1), channel_id=1, source_target_pairs={{0,112},{16,0},{32,16},{48,32},{64,48},{80,64},{96,80},{112,96},{1... | collective-permute-start | bytes 1474568 | tf_op jit(solution)/shard_map/ppermute | solution.py:26
  81.3 21.9 %collective-permute-start.15 = (bf16[2,80,1536]{2,1,0:T(8,128)(2,1)}, bf16[2,80,1536]{2,1,0:T(8,128)(2,1)S(1)}, u32[]{:S(2)}, u32[]{:S(2)}) collective-permute-start(bf16[2,80,1536]{2,1,0:T(8,128)(2,1)} %copy-done.13), channel_id=1, source_target_pairs={{0,128},{128,0},{1,129},{129,1},{2,130},{130,2},{3,131},{131,3},{4... | collective-permute-start | bytes 1474568 | tf_op jit(solution)/shard_map/ppermute | solution.py:30
  85.3 9.7 %copy-start.8 = (bf16[2,1,80,1536]{3,2,1,0:T(8,128)(2,1)S(1)}, bf16[2,1,80,1536]{3,2,1,0:T(8,128)(2,1)}, u32[]{:S(2)}) copy-start(bf16[2,1,80,1536]{3,2,1,0:T(8,128)(2,1)} %copy-done.7) | copy-start | bytes 1474564
  95.0 17.7 %copy-start.4 = (bf16[8,80,1536]{2,1,0:T(8,128)(2,1)S(1)}, bf16[8,80,1536]{2,1,0:T(8,128)(2,1)}, u32[]{:S(2)}) copy-start(bf16[8,80,1536]{2,1,0:T(8,128)(2,1)} %copy-done.3) | copy-start | bytes 5898244
  96.5 20.9 %copy-start.12 = (bf16[2,80,1536]{2,1,0:T(8,128)(2,1)S(1)}, bf16[2,80,1536]{2,1,0:T(8,128)(2,1)}, u32[]{:S(2)}) copy-start(bf16[2,80,1536]{2,1,0:T(8,128)(2,1)} %copy-done.11) | copy-start | bytes 1474564
  97.2 12.1 %collective-permute-start.13 = (bf16[80,1536]{1,0:T(8,128)(2,1)}, bf16[80,1536]{1,0:T(8,128)(2,1)}, u32[]{:S(2)}, u32[]{:S(2)}) collective-permute-start(bf16[80,1536]{1,0:T(8,128)(2,1)} %get-tuple-element.102), channel_id=1, source_target_pairs={{0,112},{16,0},{32,16},{48,32},{64,48},{80,64},{96,80},{112,96},{1... | collective-permute-start | bytes 737288 | tf_op jit(solution)/shard_map/ppermute | solution.py:26
  102.9 9.7 %collective-permute-start.14 = (bf16[80,1536]{1,0:T(8,128)(2,1)}, bf16[80,1536]{1,0:T(8,128)(2,1)}, u32[]{:S(2)}, u32[]{:S(2)}) collective-permute-start(bf16[80,1536]{1,0:T(8,128)(2,1)} %get-tuple-element.103), channel_id=1, source_target_pairs={{0,16},{16,32},{32,48},{48,64},{64,80},{80,96},{96,112},{112,0},{1... | collective-permute-start | bytes 737288 | tf_op jit(solution)/shard_map/ppermute | solution.py:26
  103.1 25.1 %copy-start.16 = (f32[16,2]{0,1:T(2,128)S(1)}, f32[16,2]{0,1:T(2,128)}, u32[]{:S(2)}) copy-start(f32[16,2]{0,1:T(2,128)} %param.13) | copy-start | bytes 388
  103.1 14.3 %collective-permute-start.18 = (bf16[80,1536]{1,0:T(8,128)(2,1)}, bf16[80,1536]{1,0:T(8,128)(2,1)}, u32[]{:S(2)}, u32[]{:S(2)}) collective-permute-start(bf16[80,1536]{1,0:T(8,128)(2,1)} %dynamic-slice_bitcast_fusion), channel_id=1, source_target_pairs={{0,128},{128,0},{1,129},{129,1},{2,130},{130,2},{3,131},{131,3},{4... | collective-permute-start | bytes 737288 | tf_op jit(solution)/shard_map/ppermute | solution.py:30
  114.9 7.7 %collective-permute-start.16 = (bf16[80,1536]{1,0:T(8,128)(2,1)}, bf16[80,1536]{1,0:T(8,128)(2,1)}, u32[]{:S(2)}, u32[]{:S(2)}) collective-permute-start(bf16[80,1536]{1,0:T(8,128)(2,1)} %get-tuple-element.108), channel_id=1, source_target_pairs={{0,112},{16,0},{32,16},{48,32},{64,48},{80,64},{96,80},{112,96},{1... | collective-permute-start | bytes 737288 | tf_op jit(solution)/shard_map/ppermute | solution.py:26
  115.2 8.9 %collective-permute-start.17 = (bf16[80,1536]{1,0:T(8,128)(2,1)}, bf16[80,1536]{1,0:T(8,128)(2,1)}, u32[]{:S(2)}, u32[]{:S(2)}) collective-permute-start(bf16[80,1536]{1,0:T(8,128)(2,1)} %get-tuple-element.109), channel_id=1, source_target_pairs={{0,16},{16,32},{32,48},{48,64},{64,80},{80,96},{96,112},{112,0},{1... | collective-permute-start | bytes 737288 | tf_op jit(solution)/shard_map/ppermute | solution.py:26
  117.3 22.5 %collective-permute-start.21 = (bf16[2,80,1536]{2,1,0:T(8,128)(2,1)S(1)}, bf16[2,80,1536]{2,1,0:T(8,128)(2,1)}, u32[]{:S(2)}, u32[]{:S(2)}) collective-permute-start(bf16[2,80,1536]{2,1,0:T(8,128)(2,1)S(1)} %copy-done.12), channel_id=1, source_target_pairs={{0,128},{128,0},{1,129},{129,1},{2,130},{130,2},{3,131},{131,3},{4... | collective-permute-start | bytes 1474568 | tf_op jit(solution)/shard_map/ppermute | solution.py:30
  126.2 13.6 %collective-permute-start.19 = (bf16[80,1536]{1,0:T(8,128)(2,1)}, bf16[80,1536]{1,0:T(8,128)(2,1)}, u32[]{:S(2)}, u32[]{:S(2)}) collective-permute-start(bf16[80,1536]{1,0:T(8,128)(2,1)} %get-tuple-element.114), channel_id=1, source_target_pairs={{0,112},{16,0},{32,16},{48,32},{64,48},{80,64},{96,80},{112,96},{1... | collective-permute-start | bytes 737288 | tf_op jit(solution)/shard_map/ppermute | solution.py:26
  126.4 13.4 %collective-permute-start.20 = (bf16[80,1536]{1,0:T(8,128)(2,1)}, bf16[80,1536]{1,0:T(8,128)(2,1)}, u32[]{:S(2)}, u32[]{:S(2)}) collective-permute-start(bf16[80,1536]{1,0:T(8,128)(2,1)} %get-tuple-element.115), channel_id=1, source_target_pairs={{0,16},{16,32},{32,48},{48,64},{64,80},{80,96},{96,112},{112,0},{1... | collective-permute-start | bytes 737288 | tf_op jit(solution)/shard_map/ppermute | solution.py:26
  128.3 11.5 %all-to-all-start = ((bf16[8,16,768]{2,1,0:T(8,128)(2,1)}), bf16[8,16,768]{2,1,0:T(8,128)(2,1)S(1)}, u32[]{:S(2)}, u32[]{:S(2)}) async-start(bf16[8,16,768]{2,1,0:T(8,128)(2,1)} %bitcast.32), calls=%async_computation | async-start | bytes 393216 | tf_op jit(solution)/shard_map/all_to_all | solution.py:293
  141.0 6.3 %collective-permute-start.22 = (bf16[80,1536]{1,0:T(8,128)(2,1)S(1)}, bf16[80,1536]{1,0:T(8,128)(2,1)S(1)}, u32[]{:S(2)}, u32[]{:S(2)}) collective-permute-start(bf16[80,1536]{1,0:T(8,128)(2,1)S(1)} %fusion.2), channel_id=1, source_target_pairs={{0,112},{16,0},{32,16},{48,32},{64,48},{80,64},{96,80},{112,96},{1... | collective-permute-start | bytes 737288 | tf_op jit(solution)/shard_map/ppermute | solution.py:26
  149.5 14.3 %all-to-all-start.1 = ((bf16[16,40,384]{2,1,0:T(8,128)(2,1)}), bf16[16,40,384]{2,1,0:T(8,128)(2,1)S(1)}, u32[]{:S(2)}, u32[]{:S(2)}) async-start(bf16[16,40,384]{2,1,0:T(8,128)(2,1)} %reshape.94), calls=%async_computation.1 | async-start | bytes 983040 | tf_op jit(solution)/shard_map/all_to_all | solution.py:315
  (11 other events, 48.9 us)
Sparse Core Ops, SparseCore 0:
  36.5 40.5 all-gather.1
